TPU v7x, 256 devices: a whole 4x4x8 slice. The times are simulated.
256 devices in a mesh: ctx: 32 (over y, x, core), tp: 8 (over z).
Axes of the slice: x: 4, y: 4, z: 8, core: 2. Of those that a mesh axis runs over, the one named last changes fastest.
Arguments:
- hidden: bfloat16 [16384, 8192], P('ctx', 'tp'), may hold values from -6 to 6
- queries: bfloat16 [16384, 8192], P('ctx', 'tp'), may hold values from -6.5 to 6.5
- rotated_keys: bfloat16 [16384, 1024], P('ctx', 'tp'), may hold values from -6 to 6
- frozen_value_rows: bfloat16 [16384, 1024], P('ctx', 'tp'), may hold values from -6 to 6
- adapter_a_v: bfloat16 [8192, 16], P('tp'), may hold values from -0.0625 to 0.0625
- value_up_matrix: bfloat16 [16, 1024], P(None, 'tp'), may hold values from -1.5 to 1.5
- adapter_a_o: bfloat16 [8192, 16], P('tp'), may hold values from -0.0625 to 0.0625
- output_up_matrix: bfloat16 [16, 8192], P(None, 'tp'), may hold values from -1.5 to 1.5
- doc_lengths: int32 [64], replicated, may hold values from 1 to 1536, 16384 in all
- pair_slots: int32 [64], replicated, may hold values from 0 to 63, each once
- token_logratio: float32 [16384], P('ctx'), may hold values from -0.6 to 0.6
- out_cotangent: bfloat16 [16384, 8192], P('ctx', 'tp'), may hold values from -6 to 6
- attn_cotangent: bfloat16 [16384, 8192], P('ctx', 'tp'), may hold values from -6 to 6
Outputs:
- attention_output_rows: bfloat16 [16384, 8192], P('ctx', 'tp')
- output_adapter_term: bfloat16 [16384, 8192], P('ctx', 'tp')
- input_adapter_gradient: bfloat16 [16384, 8192], P('ctx', 'tp')
- value_down_gradient: float32 [8192, 16], P('tp')
- value_up_gradient: float32 [16, 1024], P(None, 'tp')
- output_down_gradient: float32 [8192, 16], P('tp')
- output_up_gradient: float32 [16, 8192], P(None, 'tp')
Inputs may be any that keep to these rules, and one draw needn't show every extreme that they name: `doc_lengths`: the lengths sum to 16384, and the longest document has exactly 1536 tokens. `pair_slots`: each value once; the documents with slots 2p and 2p + 1 answer the same prompt, the even slot being the chosen answer and the odd one the rejected answer.
All inputs are finite; a program needn't handle non-finite values.
Results may differ from a plain program's by a relative error of at most 0.022.
Values may be sent and summed in bfloat16 or wider, within the bound.
No kernel may reach another device: no remote copies, remote signals or barrier semaphores. Data moves between devices by JAX's collectives and lax.ppermute only.
A program may use at most 128 MiB of HBM per device.

v0:
```python
import math

import jax
import jax.numpy as jnp
from jax import lax
from jax.sharding import PartitionSpec as P

HEADS = 64
KV_HEADS = 8
HD = 128


ADAPTER_SCALE = 2.0
BETA = 0.5
NEG_FILL = -1e30


def from_behind(value, axis, by):
    peers = lax.axis_size(axis)
    pairs = [(i, i + by) for i in range(peers) if 0 <= i + by < peers]
    return lax.ppermute(value, axis, pairs)


def doc_index(positions, doc_ends):
    return jnp.sum((doc_ends[None, :] <= positions[:, None]).astype(jnp.int32), axis=1)


def doc_weights(margins, pair_slots):
    pair_ids = pair_slots // 2
    signs = jnp.where(pair_slots % 2 == 0, 1.0, -1.0).astype(jnp.float32)
    same_pair = (pair_ids[:, None] == pair_ids[None, :]).astype(jnp.float32)
    gaps = jnp.sum(same_pair * (signs * margins)[None, :], axis=1)
    return -BETA * signs * jax.nn.sigmoid(-BETA * gaps)


def lowrank_sum(local_term):
    return lax.psum(local_term, "tp")


def score_block(left, right):
    return lax.dot_general(
        left, right, (((1,), (1,)), ((), ())), preferred_element_type=jnp.float32
    )


def row_contraction(left, right):
    return lax.dot_general(
        left, right, (((0,), (0,)), ((), ())), preferred_element_type=jnp.float32
    )


def shards(
    hidden,
    queries,
    rotated_keys,
    frozen_value_rows,
    adapter_a_v,
    value_up_matrix,
    adapter_a_o,
    output_up_matrix,
    doc_lengths,
    pair_slots,
    token_logratio,
    out_cotangent,
    attn_cotangent,
):
    row_count = hidden.shape[0]
    group_size = HEADS // KV_HEADS
    local_heads = queries.shape[1] // HD
    local_kv = rotated_keys.shape[1] // HD
    doc_count = doc_lengths.shape[0]
    score_scale = 1.0 / math.sqrt(HD)
    first_row = lax.axis_index("ctx") * row_count
    doc_ends = jnp.cumsum(doc_lengths)
    query_pos = first_row + jnp.arange(row_count, dtype=jnp.int32)
    query_doc = doc_index(query_pos, doc_ends)
    key_pos = first_row - 3 * row_count + jnp.arange(4 * row_count, dtype=jnp.int32)
    key_doc = doc_index(key_pos, doc_ends)
    allowed = (
        (query_doc[:, None] == key_doc[None, :])
        & (key_pos[None, :] <= query_pos[:, None])
        & (key_pos[None, :] >= 0)
    )
    live_slots = []
    for slot_index in range(3):
        last_key = (slot_index + 1) * row_count - 1
        live_slots.append((key_doc[last_key] == query_doc[0]) & (key_pos[last_key] >= 0))
    value_down_rows = lowrank_sum(
        jnp.dot(hidden, adapter_a_v, preferred_element_type=jnp.float32)
    ).astype(jnp.bfloat16)
    value_rows = (
        frozen_value_rows.astype(jnp.float32)
        + ADAPTER_SCALE
        * jnp.dot(value_down_rows, value_up_matrix, preferred_element_type=jnp.float32)
    ).astype(jnp.bfloat16)
    own_pair = jnp.stack([rotated_keys, value_rows])
    pieces = [own_pair]
    current = own_pair
    for step_index in range(3):
        current = from_behind(current, "ctx", 1)
        pieces.append(current)
    window = jnp.concatenate(pieces[::-1], axis=1)
    window = window.reshape(2, 4 * row_count, local_kv, HD).transpose(0, 2, 1, 3)
    query_heads = queries.reshape(row_count, local_heads, HD).transpose(1, 0, 2)
    head_ids = jnp.arange(local_heads, dtype=jnp.int32)

    def head_forward(head_index):
        kv_index = head_index // group_size
        query_head = lax.dynamic_index_in_dim(query_heads, head_index, 0, keepdims=False)
        key_head = lax.dynamic_index_in_dim(window[0], kv_index, 0, keepdims=False)
        value_head = lax.dynamic_index_in_dim(window[1], kv_index, 0, keepdims=False)
        scores = score_block(query_head, key_head)
        scores = jnp.where(allowed, scores * score_scale, NEG_FILL)
        row_top = jnp.max(scores, axis=1, keepdims=True)
        exponent = jnp.exp(scores - row_top)
        attention = (exponent / jnp.sum(exponent, axis=1, keepdims=True)).astype(jnp.bfloat16)
        output = jnp.dot(attention, value_head, preferred_element_type=jnp.float32)
        return (attention, output.astype(jnp.bfloat16))

    def head_backward(attention, grad_head):
        return row_contraction(attention, grad_head)

    stored, outputs = lax.map(head_forward, head_ids)
    onehot = (query_doc[:, None] == jnp.arange(doc_count, dtype=jnp.int32)[None, :]).astype(
        jnp.float32
    )
    margins = lax.psum(jnp.sum(onehot * token_logratio[:, None], axis=0), "ctx")
    token_weight = jnp.sum(onehot * doc_weights(margins, pair_slots)[None, :], axis=1)
    output_gradient_rows = (token_weight[:, None] * out_cotangent.astype(jnp.float32)).astype(
        jnp.bfloat16
    )
    output_down_row_gradient = (
        ADAPTER_SCALE
        * lowrank_sum(
            jnp.dot(output_gradient_rows, output_up_matrix.T, preferred_element_type=jnp.float32)
        )
    ).astype(jnp.bfloat16)
    attn_grad = (
        token_weight[:, None] * attn_cotangent.astype(jnp.float32)
        + jnp.dot(output_down_row_gradient, adapter_a_o.T, preferred_element_type=jnp.float32)
    ).astype(jnp.bfloat16)
    grad_heads = attn_grad.reshape(row_count, local_heads, HD).transpose(1, 0, 2)
    output_gradient_rows, output_down_row_gradient, grad_heads = (
        output_gradient_rows,
        output_down_row_gradient,
        grad_heads,
    )

    def head_after(operands):
        return head_backward(operands[0], operands[1])

    value_terms = lax.map(head_after, (stored, grad_heads))
    attention_output_rows = outputs.transpose(1, 0, 2).reshape(row_count, local_heads * HD)
    value_window = jnp.sum(value_terms.reshape(local_kv, group_size, 4 * row_count, HD), axis=1)
    value_window = value_window.transpose(1, 0, 2).reshape(4 * row_count, local_kv * HD)
    slot_terms = [
        value_window[slot_index * row_count : (slot_index + 1) * row_count]
        for slot_index in range(4)
    ]
    carried = slot_terms[0]
    for step_index in range(1, 4):
        carried = from_behind(carried, "ctx", -1) + slot_terms[step_index]
    value_gradient_rows = carried.astype(jnp.bfloat16)
    output_down_rows = lowrank_sum(
        jnp.dot(attention_output_rows, adapter_a_o, preferred_element_type=jnp.float32)
    ).astype(jnp.bfloat16)
    output_adapter_term = (
        ADAPTER_SCALE
        * jnp.dot(output_down_rows, output_up_matrix, preferred_element_type=jnp.float32)
    ).astype(jnp.bfloat16)
    value_down_row_gradient = (
        ADAPTER_SCALE
        * lowrank_sum(
            jnp.dot(value_gradient_rows, value_up_matrix.T, preferred_element_type=jnp.float32)
        )
    ).astype(jnp.bfloat16)
    input_adapter_gradient = jnp.dot(
        value_down_row_gradient, adapter_a_v.T, preferred_element_type=jnp.float32
    ).astype(jnp.bfloat16)
    local_a_v = row_contraction(hidden, value_down_row_gradient)
    local_value_up = ADAPTER_SCALE * row_contraction(value_down_rows, value_gradient_rows)
    local_a_o = row_contraction(attention_output_rows, output_down_row_gradient)
    local_output_up = ADAPTER_SCALE * row_contraction(output_down_rows, output_gradient_rows)
    value_down_gradient, value_up_gradient, output_down_gradient, output_up_gradient = (
        lax.psum(local_a_v.astype(jnp.bfloat16), "ctx").astype(jnp.float32),
        lax.psum(local_value_up.astype(jnp.bfloat16), "ctx").astype(jnp.float32),
        lax.psum(local_a_o.astype(jnp.bfloat16), "ctx").astype(jnp.float32),
        lax.psum(local_output_up.astype(jnp.bfloat16), "ctx").astype(jnp.float32),
    )
    return (
        attention_output_rows,
        output_adapter_term,
        input_adapter_gradient,
        value_down_gradient,
        value_up_gradient,
        output_down_gradient,
        output_up_gradient,
    )


def solution(mesh):
    in_specs = (
        P("ctx", "tp"),
        P("ctx", "tp"),
        P("ctx", "tp"),
        P("ctx", "tp"),
        P("tp", None),
        P(None, "tp"),
        P("tp", None),
        P(None, "tp"),
        P(),
        P(),
        P("ctx"),
        P("ctx", "tp"),
        P("ctx", "tp"),
    )
    out_specs = (
        P("ctx", "tp"),
        P("ctx", "tp"),
        P("ctx", "tp"),
        P("tp", None),
        P(None, "tp"),
        P("tp", None),
        P(None, "tp"),
    )
    return jax.shard_map(shards, mesh=mesh, in_specs=in_specs, out_specs=out_specs, check_vma=False)
```

profile of v0, /device:TPU:2, one launch (start us, length us, event | category | flops | bytes accessed | tf_op | source)
XLA Modules:
  0.0 417.1 jit_solution(17709361445924349157)
XLA Ops:
  9.2 62.3 %psum.65 = f32[64]{0:T(128)S(1)} all-reduce(f32[64]{0:T(128)S(1)} %select_reduce_fusion.1), channel_id=1, replica_groups=mesh['ctx'=32,'tp'=8] {'ctx'}, use_global_device_ids=true, to_apply=%region_10.11 | all-reduce | flops 64 | bytes 512 | tf_op jit(solution)/shard_map/psum | solution.py:127
  74.3 1.7 fusion.25
  76.0 33.2 %all-reduce.1 = (bf16[512,16]{0,1:T(8,128)(2,1)S(1)}, f32[512,16]{0,1:T(8,128)S(1)}) all-reduce(f32[512,16]{0,1:T(8,128)S(1)} %fusion.40, f32[512,16]{0,1:T(8,128)S(1)} %fusion.25), channel_id=1, replica_groups=mesh['ctx'=32,'tp'=8] {'tp'}, use_global_device_ids=true, to_apply=%region_0.0 | all-reduce | flops 16384 | bytes 114688 | tf_op jit(solution)/shard_map/psum | solution.py:37
  109.2 1.1 fusion.21
  111.3 1.9 collective-permute-start
  113.3 5.9 %collective-permute-done = bf16[2,512,128]{2,1,0:T(8,128)(2,1)} collective-permute-done((bf16[2,512,128]{2,1,0:T(8,128)(2,1)S(1)}, bf16[2,512,128]{2,1,0:T(8,128)(2,1)}, u32[]{:S(2)}, u32[]{:S(2)}) %collective-permute-start) | collective-permute-done | bytes 262176 | tf_op jit(solution)/shard_map/ppermute | solution.py:21
  119.1 1.9 collective-permute-start.1
  121.0 1.7 fusion.18
  122.8 4.4 %collective-permute-done.1 = bf16[2,512,128]{2,1,0:T(8,128)(2,1)} collective-permute-done((bf16[2,512,128]{2,1,0:T(8,128)(2,1)}, bf16[2,512,128]{2,1,0:T(8,128)(2,1)}, u32[]{:S(2)}, u32[]{:S(2)}) %collective-permute-start.1) | collective-permute-done | bytes 262176 | tf_op jit(solution)/shard_map/ppermute | solution.py:21
  127.1 1.9 collective-permute-start.2
  129.1 1.3 copy.30
  130.8 4.4 %collective-permute-done.2 = bf16[2,512,128]{2,1,0:T(8,128)(2,1)} collective-permute-done((bf16[2,512,128]{2,1,0:T(8,128)(2,1)}, bf16[2,512,128]{2,1,0:T(8,128)(2,1)}, u32[]{:S(2)}, u32[]{:S(2)}) %collective-permute-start.2) | collective-permute-done | bytes 262176 | tf_op jit(solution)/shard_map/ppermute | solution.py:21
  135.1 1.2 maximum_bitcast_fusion
  136.3 74.5 %while.24 = (s32[]{:T(128)}, bf16[8,512,2048]{2,1,0:T(8,128)(2,1)}, bf16[8,512,128]{2,1,0:T(8,128)(2,1)}, s32[8]{0:T(128)S(1)}, bf16[8,512,128]{1,2,0:T(8,128)(2...) while((s32[]{:T(128)}, bf16[8,512,2048]{2,1,0:T(8,128)(2,1)}, ...), condition=%wide.region_7.8_spmd.clone, body=%wide.region_4.7_spmd.clone.sunk | while | flops 549518336 | bytes 20219064 | solution.py:123
  138.9 2.6 fusion.76
  142.2 2.1 bitcast_dynamic-update-slice_fusion.2
  144.3 1.4 fusion.78
  148.2 2.6 fusion.76
  151.5 2.1 bitcast_dynamic-update-slice_fusion.2
  153.6 1.4 fusion.78
  157.4 2.6 fusion.76
  160.8 2.1 bitcast_dynamic-update-slice_fusion.2
  162.9 1.4 fusion.78
  166.7 2.6 fusion.76
  170.1 2.1 bitcast_dynamic-update-slice_fusion.2
  172.2 1.4 fusion.78
  176.1 2.6 fusion.76
  179.4 2.2 bitcast_dynamic-update-slice_fusion.2
  181.5 1.4 fusion.78
  185.4 2.6 fusion.76
  188.8 2.1 bitcast_dynamic-update-slice_fusion.2
  190.8 1.4 fusion.78
  194.7 2.6 fusion.76
  198.0 2.1 bitcast_dynamic-update-slice_fusion.2
  200.2 1.4 fusion.78
  204.0 2.6 fusion.76
  207.4 2.1 bitcast_dynamic-update-slice_fusion.2
  209.5 1.4 fusion.78
  210.8 26.6 %while.23 = (s32[]{:T(128)}, f32[8,2048,128]{2,1,0:T(8,128)}, bf16[8,512,2048]{2,1,0:T(8,128)(2,1)}, bf16[8,512,128]{2,1,0:T(8,128)(2,1)S(1)}, s32[]{:T(128)}) while((s32[]{:T(128)}, f32[8,2048,128]{2,1,0:T(8,128)}, bf16[8,512,2048]{2,1,0:T(8,128)(2,1)}, bf16[8,512,128]{2,1,0:T(8,128)(2,1)S(1)}, s32[]{:T(128)}) %tuple.57), condition=%wide.region_15.16_spmd, body=%wide.region_14.15_spmd.sunk | while | flops 268435456 | bytes 3278397 | solution.py:152
  210.8 3.3 fusion.73
  214.2 3.4 fusion.73
  217.5 3.3 fusion.73
  220.8 3.3 fusion.73
  224.2 3.3 fusion.73
  227.5 3.3 fusion.73
  230.8 3.3 fusion.73
  234.1 3.3 fusion.73
  237.4 3.9 reduce_sum.70
  241.4 1.9 collective-permute-start.3
  243.3 3.9 collective-permute-done.3
  247.2 3.8 collective-permute-start.4
  251.1 1.4 copy_bitcast_fusion
  252.5 2.5 collective-permute-done.4
  255.0 3.8 collective-permute-start.5
  260.1 2.6 collective-permute-done.5
  263.6 27.5 %all-reduce = (bf16[512,16]{0,1:T(8,128)(2,1)S(1)}, f32[512,16]{0,1:T(8,128)S(1)}) all-reduce(f32[512,16]{0,1:T(8,128)S(1)} %fusion.41, f32[512,16]{0,1:T(8,128)S(1)} %fusion.42), channel_id=1, replica_groups=mesh['ctx'=32,'tp'=8] {'tp'}, use_global_device_ids=true, to_apply=%region_8.9 | all-reduce | flops 16384 | bytes 114688 | tf_op jit(solution)/shard_map/psum | solution.py:37
  291.9 1.4 convolution_convert_fusion.1
  293.3 2.2 fusion.22
  295.6 1.4 multiply_convert_fusion.1
  297.0 107.8 %all-reduce.5.cloned.1.call-done = (bf16[1024,16]{0,1:T(8,128)(2,1)}, bf16[16,128]{1,0:T(8,128)(2,1)}, bf16[1024,16]{0,1:T(8,128)(2,1)}, bf16[16,1024]{1,0:T(8,128)(2,1)}) async-done(((bf16[1024,16]{0,1:T(8,128)(2,1)}, bf16[16,128]{1,0:T(8,128)(2,1)}, bf16[1024,16]{0,1:T(8,128)(2,1)}, bf16[16,1024]{1,0:T(8,128)(2,1)}), (bf16[1024,16]{0,1:T(8,128)(2,1)}, bf16[16,128]{1,0:T(8,128)(2,1)}, ...) | async-done | bytes 102416 | tf_op jit(solution)/shard_map/psum | solution.py:185
  404.8 1.4 convert_element_type.101
  406.2 1.4 convert_element_type.103
  407.6 1.4 convert_element_type.97
  409.0 1.3 convert_element_type.99
  (64 shorter events, 19.6 us)
Async XLA Ops:
  7.2 66.0 %copy-start = (bf16[512,1024]{1,0:T(8,128)(2,1)S(1)}, bf16[512,1024]{1,0:T(8,128)(2,1)}, u32[]{:S(2)}) copy-start(bf16[512,1024]{1,0:T(8,128)(2,1)} %param.17) | copy-start | bytes 3145732
  7.2 121.9 %copy-start.2 = (bf16[512,1024]{1,0:T(8,128)(2,1)S(1)}, bf16[512,1024]{1,0:T(8,128)(2,1)}, u32[]{:S(2)}) copy-start(bf16[512,1024]{1,0:T(8,128)(2,1)} %param.18) | copy-start | bytes 3145732
  7.2 397.6 %all-reduce.5.cloned.1.call-start = ((), (), s32[]{:S(2)}) async-start(), calls=%async_computation | async-start | bytes 204800 | tf_op jit(solution)/shard_map/psum | solution.py:185
  74.3 60.8 %copy-start.3 = (bf16[512,128]{1,0:T(8,128)(2,1)S(1)}, bf16[512,128]{1,0:T(8,128)(2,1)}, u32[]{:S(2)}) copy-start(bf16[512,128]{1,0:T(8,128)(2,1)} %param.19) | copy-start | bytes 393220
  111.3 7.8 %collective-permute-start = (bf16[2,512,128]{2,1,0:T(8,128)(2,1)S(1)}, bf16[2,512,128]{2,1,0:T(8,128)(2,1)}, u32[]{:S(2)}, u32[]{:S(2)}) collective-permute-start(bf16[2,512,128]{2,1,0:T(8,128)(2,1)S(1)} %pad_maximum_fusion), channel_id=1, source_target_pairs={{0,8},{8,16},{16,24},{24,32},{32,40},{40,48},{48,56},{56,64},{64,7... | collective-permute-start | bytes 786440 | tf_op jit(solution)/shard_map/ppermute | solution.py:21
  119.1 8.0 %collective-permute-start.1 = (bf16[2,512,128]{2,1,0:T(8,128)(2,1)}, bf16[2,512,128]{2,1,0:T(8,128)(2,1)}, u32[]{:S(2)}, u32[]{:S(2)}) collective-permute-start(bf16[2,512,128]{2,1,0:T(8,128)(2,1)} %collective-permute-done), channel_id=1, source_target_pairs={{0,8},{8,16},{16,24},{24,32},{32,40},{40,48},{48,56},{56,64},{64,7... | collective-permute-start | bytes 786440 | tf_op jit(solution)/shard_map/ppermute | solution.py:21
  127.1 8.0 %collective-permute-start.2 = (bf16[2,512,128]{2,1,0:T(8,128)(2,1)}, bf16[2,512,128]{2,1,0:T(8,128)(2,1)}, u32[]{:S(2)}, u32[]{:S(2)}) collective-permute-start(bf16[2,512,128]{2,1,0:T(8,128)(2,1)} %collective-permute-done.1), channel_id=1, source_target_pairs={{0,8},{8,16},{16,24},{24,32},{32,40},{40,48},{48,56},{56,64},{64,7... | collective-permute-start | bytes 786440 | tf_op jit(solution)/shard_map/ppermute | solution.py:21
  241.4 17.4 %copy-start.4 = (bf16[1024,16]{0,1:T(8,128)(2,1)S(1)}, bf16[1024,16]{0,1:T(8,128)(2,1)}, u32[]{:S(2)}) copy-start(bf16[1024,16]{0,1:T(8,128)(2,1)} %param.23) | copy-start | bytes 98308
  241.4 22.1 %copy-start.7 = (bf16[16,128]{1,0:T(8,128)(2,1)S(1)}, bf16[16,128]{1,0:T(8,128)(2,1)}, u32[]{:S(2)}) copy-start(bf16[16,128]{1,0:T(8,128)(2,1)} %param.22) | copy-start | bytes 12292
  241.4 50.5 %copy-start.5 = (bf16[1024,16]{0,1:T(8,128)(2,1)S(1)}, bf16[1024,16]{0,1:T(8,128)(2,1)}, u32[]{:S(2)}) copy-start(bf16[1024,16]{0,1:T(8,128)(2,1)} %param.21) | copy-start | bytes 98308
  241.4 5.8 %collective-permute-start.3 = (f32[512,128]{1,0:T(8,128)S(1)}, f32[512,128]{1,0:T(8,128)S(1)}, u32[]{:S(2)}, u32[]{:S(2)}) collective-permute-start(f32[512,128]{1,0:T(8,128)S(1)} %slice_bitcast_fusion.3), channel_id=1, source_target_pairs={{8,0},{16,8},{24,16},{32,24},{40,32},{48,40},{56,48},{64,56},{72,6... | collective-permute-start | bytes 786440 | tf_op jit(solution)/shard_map/ppermute | solution.py:21
  247.2 7.7 %collective-permute-start.4 = (f32[512,128]{1,0:T(8,128)S(1)}, f32[512,128]{1,0:T(8,128)S(1)}, u32[]{:S(2)}, u32[]{:S(2)}) collective-permute-start(f32[512,128]{1,0:T(8,128)S(1)} %fusion.29), channel_id=1, source_target_pairs={{8,0},{16,8},{24,16},{32,24},{40,32},{48,40},{56,48},{64,56},{72,6... | collective-permute-start | bytes 786440 | tf_op jit(solution)/shard_map/ppermute | solution.py:21
  252.4 44.5 %copy-start.1 = (bf16[512,1024]{1,0:T(8,128)(2,1)}, bf16[512,1024]{1,0:T(8,128)(2,1)S(1)}, u32[]{:S(2)}) copy-start(bf16[512,1024]{1,0:T(8,128)(2,1)S(1)} %copy_bitcast_fusion) | copy-start | bytes 3145732
  252.5 43.1 %copy-start.6 = (bf16[16,1024]{1,0:T(8,128)(2,1)S(1)}, bf16[16,1024]{1,0:T(8,128)(2,1)}, u32[]{:S(2)}) copy-start(bf16[16,1024]{1,0:T(8,128)(2,1)} %param.24) | copy-start | bytes 98308
  255.0 7.7 %collective-permute-start.5 = (f32[512,128]{1,0:T(8,128)S(1)}, f32[512,128]{1,0:T(8,128)S(1)}, u32[]{:S(2)}, u32[]{:S(2)}) collective-permute-start(f32[512,128]{1,0:T(8,128)S(1)} %fusion.28), channel_id=1, source_target_pairs={{8,0},{16,8},{24,16},{32,24},{40,32},{48,40},{56,48},{64,56},{72,6... | collective-permute-start | bytes 786440 | tf_op jit(solution)/shard_map/ppermute | solution.py:21
Sparse Core Ops, SparseCore 0:
  295.7 109.0 all-reduce.4
where the time goes:
time: 420 us; the launch traced here: 417 us
  waiting for transfers between devices  131 us (31%)
  blocking collectives  123 us (29%)
  matrix products  72.1 us (17%)
  other arithmetic  37 us (9%)
  loops' own time  15.6 us (4%)
  starting transfers between devices  15.3 us (4%)
  between operations  14.3 us (3%)
  local copies, waits for them, and re-layouts  8.5 us (2%)
    psum x1, waiting for transfers between devices, shards(): lax.psum(local_a_v.astype(jnp.bfloat16), 'ctx').astype(jnp.float32)  108 us
    psum x1, blocking collectives, shards(): margins = lax.psum(jnp.sum(onehot * token_logratio[:, None], axis=0), 'ctx')  62.3 us
    psum x2, blocking collectives, lowrank_sum(): return lax.psum(local_term, 'tp')  60.7 us
    dot_general x12, matrix products, row_contraction(): lax.dot_general(left, right, (((0,), (0,)), ((), ())), preferred_element_...  31.3 us
    ppermute x6, waiting for transfers between devices, from_behind(): return lax.ppermute(value, axis, pairs)  23.5 us
    dot_general x8, matrix products, score_block(): lax.dot_general(left, right, (((1,), (1,)), ((), ())), preferred_element_...  20.8 us
    dynamic_update_slice x8, other arithmetic, shards(): stored, outputs = lax.map(head_forward, head_ids)  16.9 us
    another operation x1, loops' own time, shards(): stored, outputs = lax.map(head_forward, head_ids)  15.6 us
  transfers between devices with their start and end apart: 7, of which 7 were waited for; matrix products, arithmetic and copies ran while one was open for 2% of the time, Pallas kernels for 0%

commit v1 on v0

v1 whole, which is shorter than its diff:
```python
import functools
import math

import jax
import jax.numpy as jnp
from jax import lax
from jax.experimental import pallas as pl
from jax.experimental.pallas import tpu as pltpu
from jax.sharding import PartitionSpec as P

HD = 128
BETA = 0.5
NEG = -1e30
F32 = jnp.float32
BF16 = jnp.bfloat16
KB = 256


def shift(value, by):
    n = lax.axis_size("ctx")
    pairs = [(i, i + by) for i in range(n) if 0 <= i + by < n]
    return lax.ppermute(value, "ctx", pairs)


def flip(value, mask):
    n = lax.axis_size("ctx")
    return lax.ppermute(value, "ctx", [(i, i ^ mask) for i in range(n)])


def spread_margins(part):
    n_ctx, n_tp = lax.axis_size("ctx"), lax.axis_size("tp")
    per = n_ctx // n_tp
    total = None
    for m in range(per):
        pairs = [
            ((c ^ (per * j + m)) * n_tp + j, c * n_tp + j)
            for c in range(n_ctx)
            for j in range(n_tp)
        ]
        got = lax.ppermute(part, ("ctx", "tp"), pairs)
        total = got if total is None else total + got
    return total


def share_tp(rows):
    n = lax.axis_size("tp")
    return lax.all_to_all(jnp.broadcast_to(rows[None], (n,) + rows.shape), "tp", 0, 0)


def nt(left, right):
    return lax.dot_general(left, right, (((1,), (1,)), ((), ())), preferred_element_type=F32)


def nn(left, right):
    return lax.dot_general(left, right, (((1,), (0,)), ((), ())), preferred_element_type=F32)


def tn(left, right):
    return lax.dot_general(left, right, (((0,), (0,)), ((), ())), preferred_element_type=F32)


def attn_kernel(
    start_ref, q_ref, g_ref, aot_ref, r_ref, k0, k1, k2, k3, v0, v1, v2, v3, lv_ref, uvt_ref, uv_ref,
    o_ref, lowo_ref, z_ref, vg_ref,
    bias, vt, s_scr, p_scr, vg,
):
    head = pl.program_id(0)
    rows = q_ref.shape[0]
    width = 4 * rows
    n_kb = width // KB
    scale = math.log2(math.e) / math.sqrt(HD)
    ks = (k0, k1, k2, k3)
    per = rows // KB

    @pl.when(head == 0)
    def _():
        start = start_ref[0:1, :]
        qpos = start_ref[1:2, :]
        for kb in range(n_kb):
            kpos = lax.broadcasted_iota(jnp.int32, (KB, rows), 0) + kb * KB
            ok = (kpos >= start) & (kpos <= qpos)
            bias[kb * KB : (kb + 1) * KB, :] = jnp.where(ok, 0.0, NEG)
        for s, ref in enumerate((v0, v1, v2, v3)):
            low = lv_ref[:, s * rows : (s + 1) * rows]
            frozen = ref[...].astype(F32).T
            vt[:, s * rows : (s + 1) * rows] = (frozen + 2.0 * nn(uvt_ref[...], low)).astype(BF16)
        vg[...] = jnp.zeros_like(vg)
        lowo_ref[...] = jnp.zeros_like(lowo_ref)

    q = q_ref[...]
    top = None
    for kb in range(n_kb):
        key = ks[kb // per][(kb % per) * KB : (kb % per + 1) * KB, :]
        s = nt(key, q) * scale + bias[kb * KB : (kb + 1) * KB, :]
        s_scr[kb * KB : (kb + 1) * KB, :] = s
        m = jnp.max(s, axis=0, keepdims=True)
        top = m if top is None else jnp.maximum(top, m)
    total = None
    for kb in range(n_kb):
        e = jnp.exp2(s_scr[kb * KB : (kb + 1) * KB, :] - top)
        p_scr[kb * KB : (kb + 1) * KB, :] = e.astype(BF16)
        m = jnp.sum(e, axis=0, keepdims=True)
        total = m if total is None else total + m
    inv = 1.0 / total
    ot = (nn(vt[...], p_scr[...]) * inv).astype(BF16)
    o_ref[...] = ot.astype(F32).T.astype(BF16)
    lowo_ref[...] += nn(aot_ref[...], ot)
    inv_rows = jnp.broadcast_to(inv, (HD, rows)).T
    grad = g_ref[...].astype(F32) + nn(r_ref[...], aot_ref[...])
    grad = (grad * inv_rows).astype(BF16)
    vg[...] += nn(p_scr[...], grad)

    @pl.when(head == pl.num_programs(0) - 1)
    def _():
        total_vg = vg[...].astype(BF16)
        vg_ref[...] = total_vg
        z_ref[...] = nt(uv_ref[...], total_vg).astype(BF16)


def attention(start_q, queries, cotangent, a_o_t, r, keys, frozen, low_v_t, u_v):
    rows = queries.shape[0]
    heads = queries.shape[1] // HD
    rank = u_v.shape[0]
    full = lambda shape: pl.BlockSpec(shape, lambda h: (0, 0))
    column = pl.BlockSpec((rows, HD), lambda h: (0, h))
    return pl.pallas_call(
        attn_kernel,
        grid=(heads,),
        in_specs=[full(start_q.shape), column, column, pl.BlockSpec((rank, HD), lambda h: (0, h)), full(r.shape)]
        + [full((rows, HD))] * 8
        + [full(low_v_t.shape), full((HD, rank)), full((rank, HD))],
        out_specs=[column, full((rank, rows)), full((rank, 4 * rows)), full((4 * rows, HD))],
        out_shape=[
            jax.ShapeDtypeStruct((rows, heads * HD), BF16),
            jax.ShapeDtypeStruct((rank, rows), F32),
            jax.ShapeDtypeStruct((rank, 4 * rows), BF16),
            jax.ShapeDtypeStruct((4 * rows, HD), BF16),
        ],
        scratch_shapes=[
            pltpu.VMEM((4 * rows, rows), F32),
            pltpu.VMEM((HD, 4 * rows), BF16),
            pltpu.VMEM((4 * rows, rows), F32),
            pltpu.VMEM((4 * rows, rows), BF16),
            pltpu.VMEM((4 * rows, HD), F32),
        ],
        compiler_params=pltpu.CompilerParams(
            dimension_semantics=("arbitrary",), vmem_limit_bytes=48 * 2**20
        ),
        name="attn",
    )(start_q, queries, cotangent, a_o_t, r, *keys, *frozen, low_v_t, u_v.T, u_v)


def grads_kernel(
    shared_ref, pair_ref, ends_ref, rt_ref, lv_ref, vg_ref, hidden_ref, o_ref, dout_ref,
    vd_ref, od_ref, ou_ref, vu_ref, lowo_ref, lvg_ref, wr_scr, wlo_scr,
):
    step = pl.program_id(0)
    rank, rows = rt_ref.shape
    width = lv_ref.shape[1]

    @pl.when(step == 0)
    def _():
        sums = shared_ref[0].astype(F32)
        for j in range(1, shared_ref.shape[0]):
            sums = sums + shared_ref[j].astype(F32)
        line = sums[2 * rank : 2 * rank + 1, :]
        margin = line[:, 0:128] + line[:, 128:256] + line[:, 256:384]
        gap = jnp.sum(pair_ref[:, 0:128] * margin, axis=1, keepdims=True)
        sign = pair_ref[:, 128:129]
        weight = -BETA * sign / (1.0 + jnp.exp(BETA * gap))
        docs = weight.shape[0]
        token = lax.broadcasted_iota(jnp.int32, (docs, width), 1)
        inside = (token >= ends_ref[:, 0:1]) & (token < ends_ref[:, 1:2])
        token_weight = jnp.sum(jnp.where(inside, weight, 0.0), axis=0, keepdims=True)
        own = token_weight[:, width - rows :]
        lvg_ref[...] = (2.0 * own * sums[0:rank]).astype(BF16)
        low_o = sums[rank : 2 * rank].astype(BF16)
        lowo_ref[...] = low_o
        wr_scr[...] = (own * rt_ref[...].astype(F32)).astype(BF16)
        wlo_scr[...] = (own * low_o.astype(F32)).astype(BF16)
        wlv = (token_weight * lv_ref[...].astype(F32)).astype(BF16)
        vu_ref[...] = (2.0 * nn(wlv, vg_ref[...])).astype(BF16)

    vd_ref[...] = nn(lvg_ref[...], hidden_ref[...]).astype(BF16)
    od_ref[...] = nn(wr_scr[...], o_ref[...]).astype(BF16)
    ou_ref[...] = (2.0 * nn(wlo_scr[...], dout_ref[...])).astype(BF16)


def grads(shared, pair, ends, r_t, low_v_t, vg, hidden, o, d_out):
    rank, rows = r_t.shape
    cols = hidden.shape[1]
    tile = min(256, cols)
    full = lambda a: pl.BlockSpec(a.shape, lambda i: (0,) * a.ndim)
    column = pl.BlockSpec((rows, tile), lambda i: (0, i))
    part = pl.BlockSpec((rank, tile), lambda i: (0, i))
    small = pl.BlockSpec((rank, rows), lambda i: (0, 0))
    return pl.pallas_call(
        grads_kernel,
        grid=(cols // tile,),
        in_specs=[full(a) for a in (shared, pair, ends, r_t, low_v_t, vg)] + [column] * 3,
        out_specs=[part, part, part, pl.BlockSpec((rank, HD), lambda i: (0, 0)), small, small],
        out_shape=[jax.ShapeDtypeStruct((rank, cols), BF16)] * 3
        + [jax.ShapeDtypeStruct((rank, HD), BF16)]
        + [jax.ShapeDtypeStruct((rank, rows), BF16)] * 2,
        scratch_shapes=[pltpu.VMEM((rank, rows), BF16)] * 2,
        compiler_params=pltpu.CompilerParams(
            dimension_semantics=("arbitrary",), vmem_limit_bytes=32 * 2**20
        ),
        name="grads",
    )(shared, pair, ends, r_t, low_v_t, vg, hidden, o, d_out)


def three_parts(x):
    keep = functools.partial(lax.reduce_precision, exponent_bits=8, mantissa_bits=7)
    high = keep(x)
    mid = keep(x - high)
    return high, mid, x - high - mid


def shards(
    hidden, queries, rotated_keys, frozen_value_rows, adapter_a_v, value_up_matrix, adapter_a_o,
    output_up_matrix, doc_lengths, pair_slots, token_logratio, out_cotangent, attn_cotangent,
):
    rows = hidden.shape[0]
    rank = value_up_matrix.shape[0]
    docs = doc_lengths.shape[0]
    first = lax.axis_index("ctx") * rows

    kv = jnp.concatenate([rotated_keys, frozen_value_rows], axis=0)
    kv_behind = [shift(kv, by) for by in (3, 2, 1)]
    keys = [x[:rows] for x in kv_behind] + [rotated_keys]
    frozen = [x[rows:] for x in kv_behind] + [frozen_value_rows]

    low_v_part = lax.dot_general(
        adapter_a_v, hidden, (((0,), (1,)), ((), ())), preferred_element_type=F32
    )
    r_part = nt(output_up_matrix, out_cotangent)
    stacked = jnp.concatenate([low_v_part, r_part], axis=0).astype(BF16)
    shared = jnp.sum(share_tp(stacked).astype(F32), axis=0)
    low_v_t = shared[:rank].astype(BF16)
    r_t = (2.0 * shared[rank:]).astype(BF16)
    low_v_window = jnp.concatenate([shift(low_v_t, by) for by in (3, 2, 1)] + [low_v_t], axis=1)

    doc_ids = jnp.arange(docs, dtype=jnp.int32)
    upto = (doc_ids[:, None] <= doc_ids[None, :]).astype(jnp.int32)
    doc_ends = jnp.sum(upto * doc_lengths[:, None], axis=0)
    doc_starts = doc_ends - doc_lengths
    pos = first + jnp.arange(rows, dtype=jnp.int32)
    own = (doc_starts[:, None] <= pos[None, :]) & (pos[None, :] < doc_ends[:, None])
    margin_part = jnp.sum(jnp.where(own, token_logratio[None, :], 0.0), axis=1)
    margin_part = spread_margins(margin_part)
    base = first - 3 * rows
    start = jnp.sum(jnp.where(own, doc_starts[:, None], 0), axis=0) - base
    start_q = jnp.zeros((8, rows), jnp.int32).at[0].set(start).at[1].set(pos - base)

    o, low_o_part, z, vg = attention(
        start_q, queries, attn_cotangent, adapter_a_o.T, r_t.T, keys, frozen, low_v_window, value_up_matrix
    )

    z_own = z[:, 3 * rows :].astype(F32)
    for slot in range(3):
        z_own = z_own + shift(z[:, slot * rows : (slot + 1) * rows], slot - 3).astype(F32)
    line = jnp.zeros((1, rows), F32)
    for i, piece in enumerate(three_parts(margin_part)):
        line = lax.dynamic_update_slice(line, piece[None, :], (0, 128 * i))
    line = jnp.pad(line, ((0, 7), (0, 0)))
    sent = jnp.concatenate([z_own, low_o_part, line], axis=0).astype(BF16)
    shared_back = share_tp(sent)

    pair_ids = pair_slots // 2
    sign = jnp.where(pair_slots % 2 == 0, 1.0, -1.0).astype(F32)
    pair = jnp.where(pair_ids[:, None] == pair_ids[None, :], sign[None, :], 0.0)
    pair = jnp.concatenate(
        [jnp.pad(pair, ((0, 0), (0, 128 - docs))), jnp.broadcast_to(sign[:, None], (docs, 128))], axis=1
    )
    ends = jnp.stack([doc_starts - base, doc_ends - base], axis=1)
    ends = jnp.pad(ends, ((0, 0), (0, 126)))
    vd, od, ou, vu, low_o_t, lvg_t = grads(
        shared_back, pair, ends, r_t, low_v_window, vg, hidden, o, out_cotangent
    )
    total = jnp.concatenate([vd, od, ou, vu], axis=1).astype(F32)
    for mask in (1, 2, 4, 8, 16):
        total = total + flip(total.astype(BF16), mask).astype(F32)
    cols = hidden.shape[1]
    term = (2.0 * tn(low_o_t, output_up_matrix)).astype(BF16)
    input_grad = lax.dot_general(
        lvg_t, adapter_a_v, (((0,), (1,)), ((), ())), preferred_element_type=F32
    ).astype(BF16)
    return (
        o,
        term,
        input_grad,
        total[:, :cols].T,
        total[:, 3 * cols :],
        total[:, cols : 2 * cols].T,
        total[:, 2 * cols : 3 * cols],
    )


def solution(mesh):
    both, tp_rows, tp_cols = P("ctx", "tp"), P("tp", None), P(None, "tp")
    in_specs = (
        both, both, both, both, tp_rows, tp_cols, tp_rows, tp_cols, P(), P(), P("ctx"), both, both,
    )
    out_specs = (both, both, both, tp_rows, tp_cols, tp_rows, tp_cols)
    return jax.shard_map(shards, mesh=mesh, in_specs=in_specs, out_specs=out_specs, check_vma=False)
```

time: 420 us -> 164 us (0.39)
  blocking collectives: 123 us -> 0 us
  waiting for transfers between devices: 131 us -> 30.2 us
  matrix products: 72.1 us -> 4.84 us
  starting transfers between devices: 15.3 us -> 68.3 us
  other arithmetic: 37 us -> 8.98 us
  Pallas kernels: 0 us -> 25.9 us
  loops' own time: 15.6 us -> 0 us
  between operations: 14.3 us -> 1.15 us
  local copies, waits for them, and re-layouts: 8.5 us -> 21.3 us
    psum x3 -> x0, blocking collectives: 123 us -> none  [the longest x1 62.3 us: shards(): margins = lax.psum(jnp.sum(onehot * token_logratio[:, None], axis=0), 'ctx')]
    psum x1 -> x0, waiting for transfers between devices: 108 us -> none  [shards(): lax.psum(local_a_v.astype(jnp.bfloat16), 'ctx').astype(jnp.float32)]
    dot_general x36 -> x4, matrix products: 72.1 us -> 4.84 us  [the longest x1 1.62 us: shards(): lax.dot_general(adapter_a_v, hidden, (((0,), (1,)), ((), ())), preferred_...]
    ppermute x6 -> x18, starting transfers between devices: 15.3 us -> 44.3 us  [the longest x9 30.4 us: shift(): return lax.ppermute(value, 'ctx', pairs)]
    pallas_call x0 -> x2, Pallas kernels: none -> 25.9 us  [the longest x1 24.1 us: attention(): pl.pallas_call(attn_kernel, grid=(heads,), in_specs=[full(start_q.shape),...]
    all_to_all x0 -> x2, starting transfers between devices: none -> 24 us  [share_tp(): lax.all_to_all(jnp.broadcast_to(rows[None], (n,) + rows.shape), 'tp', 0, 0)]
    dynamic_update_slice x8 -> x0, other arithmetic: 16.9 us -> none  [shards(): stored, outputs = lax.map(head_forward, head_ids)]
    another operation x2 -> x0, loops' own time: 15.6 us -> none  [the longest x1 15.6 us: shards(): stored, outputs = lax.map(head_forward, head_ids)]
  transfers between devices with their start and end apart: 7 -> 20, of which waited for: 7 -> 8; matrix products, arithmetic and copies ran while one was open for 2% -> 10% of each run, Pallas kernels for 0% -> 0%
where the time goes in v1:
time: 164 us; the launch traced here: 161 us
  starting transfers between devices  68.3 us (42%)
  waiting for transfers between devices  30.2 us (18%)
  Pallas kernels  25.9 us (16%)
  local copies, waits for them, and re-layouts  21.3 us (13%)
  other arithmetic  8.98 us (5%)
  matrix products  4.84 us (3%)
    ppermute x9, starting transfers between devices, shift(): return lax.ppermute(value, 'ctx', pairs)  30.4 us
    pallas_call x1, Pallas kernels, attention(): pl.pallas_call(attn_kernel, grid=(heads,), in_specs=[full(start_q.shape),...  24.1 us
    all_to_all x2, starting transfers between devices, share_tp(): lax.all_to_all(jnp.broadcast_to(rows[None], (n,) + rows.shape), 'tp', 0, 0)  24 us
    all_to_all x2, waiting for transfers between devices, share_tp(): lax.all_to_all(jnp.broadcast_to(rows[None], (n,) + rows.shape), 'tp', 0, 0)  13.2 us
    ppermute x5, waiting for transfers between devices, flip(): return lax.ppermute(value, 'ctx', [(i, i ^ mask) for i in range(n)])  11.3 us
    unnamed x67, local copies, waits for them, and re-layouts  11.3 us
    ppermute x5, starting transfers between devices, flip(): return lax.ppermute(value, 'ctx', [(i, i ^ mask) for i in range(n)])  10.8 us
    ppermute x9, waiting for transfers between devices, shift(): return lax.ppermute(value, 'ctx', pairs)  5.71 us
  transfers between devices with their start and end apart: 20, of which 8 were waited for; matrix products, arithmetic and copies ran while one was open for 10% of the time, Pallas kernels for 0%

profile of v1, /device:TPU:2, one launch (start us, length us, event | category | flops | bytes accessed | tf_op | source)
XLA Modules:
  0.0 160.7 jit_solution(631501292281730055)
XLA Ops:
  0.7 0.8 select_reduce_fusion.2
  1.5 1.2 subtract_bitcast_fusion.1
  2.7 0.9 select_reduce_fusion
  3.7 2.4 %collective-permute-start.11 = (f32[64]{0:T(128)S(1)}, f32[64]{0:T(128)S(1)}, u32[]{:S(2)}, u32[]{:S(2)}) collective-permute-start(f32[64]{0:T(128)S(1)} %select_reduce_fusion), channel_id=1, source_target_pairs={{16,0},{49,1},{82,2},{115,3},{148,4},{181,5},{214,6},{247,7},{24,8... | collective-permute-start | bytes 776 | tf_op jit(solution)/shard_map/ppermute | solution.py:40
  6.0 0.6 collective-permute-start.9
  6.7 1.6 %convolution_convert_fusion.2 = bf16[16,512]{1,0:T(8,128)(2,1)S(1)} fusion(bf16[1024,16]{0,1:T(8,128)(2,1)} %param.21, bf16[512,1024]{1,0:T(8,128)(2,1)} %hidden_ref.1), kind=kOutput, calls=%fused_computation.3 | convolution fusion | flops 16785408 | bytes 1097728 | tf_op jit(solution)/shard_map/dot_general | solution.py:234
  8.8 0.7 broadcast_in_dim.55
  9.5 16.8 %all-to-all-start = ((bf16[8,32,512]{2,1,0:T(8,128)(2,1)}), bf16[8,32,512]{2,1,0:T(8,128)(2,1)}, u32[]{:S(2)}, u32[]{:S(2)}) async-start(bf16[8,32,512]{2,1,0:T(8,128)(2,1)} %broadcast_in_dim.55), calls=%async_computation | async-start | bytes 524288 | tf_op jit(solution)/shard_map/all_to_all | solution.py:47
  26.3 0.7 constant_dynamic-update-slice_fusion.1
  26.9 0.7 constant_dynamic-update-slice_fusion
  27.6 1.9 %collective-permute-start.2 = (bf16[1024,128]{1,0:T(8,128)(2,1)}, bf16[1024,128]{1,0:T(8,128)(2,1)}, u32[]{:S(2)}, u32[]{:S(2)}) collective-permute-start(bf16[1024,128]{1,0:T(8,128)(2,1)} %constant_dynamic-update-slice_fusion), channel_id=1, source_target_pairs={{0,8},{8,16},{16,24},{24,32},{32,40},{40,48},{48,56},{56,64},{64,7... | collective-permute-start | bytes 786440 | tf_op jit(solution)/shard_map/ppermute | solution.py:22
  29.5 0.6 compare_select_fusion.1
  30.1 0.5 and_select_fusion.1
  31.0 3.4 %collective-permute-start.1 = (bf16[1024,128]{1,0:T(8,128)(2,1)}, bf16[1024,128]{1,0:T(8,128)(2,1)S(1)}, u32[]{:S(2)}, u32[]{:S(2)}) collective-permute-start(bf16[1024,128]{1,0:T(8,128)(2,1)} %constant_dynamic-update-slice_fusion), channel_id=1, source_target_pairs={{0,16},{8,24},{16,32},{24,40},{32,48},{40,56},{48,64},{56,72},{64,... | collective-permute-start | bytes 786440 | tf_op jit(solution)/shard_map/ppermute | solution.py:22
  34.4 5.2 %collective-permute-start = (bf16[1024,128]{1,0:T(8,128)(2,1)}, bf16[1024,128]{1,0:T(8,128)(2,1)S(1)}, u32[]{:S(2)}, u32[]{:S(2)}) collective-permute-start(bf16[1024,128]{1,0:T(8,128)(2,1)} %constant_dynamic-update-slice_fusion), channel_id=1, source_target_pairs={{0,24},{8,32},{16,40},{24,48},{32,56},{40,64},{48,72},{56,80},{64,... | collective-permute-start | bytes 786440 | tf_op jit(solution)/shard_map/ppermute | solution.py:22
  39.7 0.6 fusion.6
  40.3 1.9 %fusion.8 = (bf16[512,128]{1,0:T(8,128)(2,1)}, bf16[512,128]{1,0:T(8,128)(2,1)}) fusion(bf16[1024,128]{1,0:T(8,128)(2,1)} %collective-permute-done.2), kind=kLoop, calls=%fused_computation.57 | loop fusion | bytes 524288 | tf_op jit(solution)/shard_map/slice | solution.py:232
  42.1 0.7 fusion.9
  42.8 3.7 %collective-permute-done = bf16[1024,128]{1,0:T(8,128)(2,1)S(1)} collective-permute-done((bf16[1024,128]{1,0:T(8,128)(2,1)}, bf16[1024,128]{1,0:T(8,128)(2,1)S(1)}, u32[]{:S(2)}, u32[]{:S(2)}) %collective-permute-start) | collective-permute-done | bytes 262176 | tf_op jit(solution)/shard_map/ppermute | solution.py:22
  46.5 0.7 fusion.10
  47.2 1.0 convert_reduce_fusion
  48.2 0.6 slice.113
  48.8 2.8 %collective-permute-start.5 = (bf16[16,512]{1,0:T(8,128)(2,1)}, bf16[16,512]{1,0:T(8,128)(2,1)}, u32[]{:S(2)}, u32[]{:S(2)}) collective-permute-start(bf16[16,512]{1,0:T(8,128)(2,1)} %slice.113), channel_id=1, source_target_pairs={{0,8},{8,16},{16,24},{24,32},{32,40},{40,48},{48,56},{56,64},{64,7... | collective-permute-start | bytes 49160 | tf_op jit(solution)/shard_map/ppermute | solution.py:22
  51.6 4.0 %collective-permute-start.4 = (bf16[16,512]{1,0:T(8,128)(2,1)}, bf16[16,512]{1,0:T(8,128)(2,1)}, u32[]{:S(2)}, u32[]{:S(2)}) collective-permute-start(bf16[16,512]{1,0:T(8,128)(2,1)} %slice.113), channel_id=1, source_target_pairs={{0,16},{8,24},{16,32},{24,40},{32,48},{40,56},{48,64},{56,72},{64,... | collective-permute-start | bytes 49160 | tf_op jit(solution)/shard_map/ppermute | solution.py:22
  55.7 7.8 %collective-permute-start.3 = (bf16[16,512]{1,0:T(8,128)(2,1)}, bf16[16,512]{1,0:T(8,128)(2,1)}, u32[]{:S(2)}, u32[]{:S(2)}) collective-permute-start(bf16[16,512]{1,0:T(8,128)(2,1)} %slice.113), channel_id=1, source_target_pairs={{0,24},{8,32},{16,40},{24,48},{32,56},{40,64},{48,72},{56,80},{64,... | collective-permute-start | bytes 49160 | tf_op jit(solution)/shard_map/ppermute | solution.py:22
  63.5 0.6 fusion.21
  64.1 1.5 copy.28.r_ref
  65.6 0.8 pad_maximum_fusion.lv_ref
  66.4 0.9 copy-done.10
  67.3 0.9 copy-done.11
  68.2 0.9 copy-done.12
  69.1 0.9 copy-done.13
  70.0 0.9 copy-done.14
  70.9 0.9 copy-done.15
  71.8 0.9 copy-done.16
  72.7 0.8 copy-done.19
  73.5 0.7 copy-done.21
  74.2 24.1 %attn.1 = (bf16[512,1024]{1,0:T(8,128)(2,1)}, f32[16,512]{1,0:T(8,128)S(1)}, bf16[16,2048]{1,0:T(8,128)(2,1)S(1)}, bf16[2048,128]{1,0:T(8,128)(2,1)S(1)}) custom-call(s32[8,512]{1,0:T(8,128)S(1)} %scatter.9.start_ref, bf16[512,1024]{1,0:T(8,128)(2,1)S(1)} %copy-done.3, bf16[512,1024]{1,0:T(8,128)(2,1)S(1)} %copy-done.4, bf16[16,1024]{1,0:T(8,128)(2,1)S(1)} %bitcast.28, ...), custom_call_target="tpu_custom_call" | custom-call | tf_op jit(solution)/shard_map/attn/pallas_call | solution.py:126
  98.2 0.8 copy-done.6
  99.1 0.6 copy-done.17
  99.7 1.4 collective-permute-start.6
  101.1 1.9 %collective-permute-start.8 = (bf16[16,512]{1,0:T(8,128)(2,1)S(1)}, bf16[16,512]{1,0:T(8,128)(2,1)S(1)}, u32[]{:S(2)}, u32[]{:S(2)}) collective-permute-start(bf16[16,512]{1,0:T(8,128)(2,1)S(1)} %get-tuple-element.65), channel_id=1, source_target_pairs={{8,0},{16,8},{24,16},{32,24},{40,32},{48,40},{56,48},{64,56},{72,6... | collective-permute-start | bytes 49160 | tf_op jit(solution)/shard_map/ppermute | solution.py:22
  103.0 1.9 %collective-permute-start.7 = (bf16[16,512]{1,0:T(8,128)(2,1)S(1)}, bf16[16,512]{1,0:T(8,128)(2,1)S(1)}, u32[]{:S(2)}, u32[]{:S(2)}) collective-permute-start(bf16[16,512]{1,0:T(8,128)(2,1)S(1)} %get-tuple-element.66), channel_id=1, source_target_pairs={{16,0},{24,8},{32,16},{40,24},{48,32},{56,40},{64,48},{72,56},{80,... | collective-permute-start | bytes 49160 | tf_op jit(solution)/shard_map/ppermute | solution.py:22
  105.2 0.8 dynamic_update_slice.11
  106.0 0.8 convert.24
  106.8 2.0 %collective-permute-done.7 = bf16[16,512]{1,0:T(8,128)(2,1)S(1)} collective-permute-done((bf16[16,512]{1,0:T(8,128)(2,1)S(1)}, bf16[16,512]{1,0:T(8,128)(2,1)S(1)}, u32[]{:S(2)}, u32[]{:S(2)}) %collective-permute-start.7) | collective-permute-done | bytes 16416 | tf_op jit(solution)/shard_map/ppermute | solution.py:22
  108.8 0.7 add_convert_fusion
  109.5 0.7 broadcast_in_dim.90
  110.3 7.2 %all-to-all-start.1 = ((bf16[8,40,512]{2,1,0:T(8,128)(2,1)}), bf16[8,40,512]{2,1,0:T(8,128)(2,1)S(1)}, u32[]{:S(2)}, u32[]{:S(2)}) async-start(bf16[8,40,512]{2,1,0:T(8,128)(2,1)} %broadcast_in_dim.90), calls=%async_computation.1 | async-start | bytes 655360 | tf_op jit(solution)/shard_map/all_to_all | solution.py:47
  117.8 13.2 %all-to-all-done.1.shared_ref = bf16[8,40,512]{2,1,0:T(8,128)(2,1)S(1)} async-done(((bf16[8,40,512]{2,1,0:T(8,128)(2,1)}), bf16[8,40,512]{2,1,0:T(8,128)(2,1)S(1)}, u32[]{:S(2)}, u32[]{:S(2)}) %all-to-all-start.1) | async-done | bytes 327712 | tf_op jit(solution)/shard_map/all_to_all | solution.py:47
  131.1 1.2 copy-done.5
  132.3 1.8 %grads.1 = (bf16[16,1024]{1,0:T(8,128)(2,1)S(1)}, bf16[16,1024]{1,0:T(8,128)(2,1)S(1)}, bf16[16,1024]{1,0:T(8,128)(2,1)S(1)}, bf16[16,128]{1,0:T(8,128)(2,1)S(1)...) custom-call(bf16[8,40,512]{2,1,0:T(8,128)(2,1)S(1)} %all-to-all-done.1.shared_ref, ...), custom_call_target="tpu_custom_call" | custom-call | tf_op jit(solution)/shard_map/grads/pallas_call | solution.py:197
  134.3 1.3 collective-permute-done.13
  135.7 4.9 %collective-permute-done.14 = bf16[16,3200]{1,0:T(8,128)(2,1)S(1)} collective-permute-done((bf16[16,3200]{1,0:T(8,128)(2,1)S(1)}, bf16[16,3200]{1,0:T(8,128)(2,1)S(1)}, u32[]{:S(2)}, u32[]{:S(2)}) %collective-permute-start.14) | collective-permute-done | bytes 102432 | tf_op jit(solution)/shard_map/ppermute | solution.py:27
  140.7 4.6 %collective-permute-start.15 = (bf16[16,3200]{1,0:T(8,128)(2,1)S(1)}, bf16[16,3200]{1,0:T(8,128)(2,1)S(1)}, u32[]{:S(2)}, u32[]{:S(2)}) collective-permute-start(bf16[16,3200]{1,0:T(8,128)(2,1)S(1)} %fusion.7), channel_id=1, source_target_pairs={{0,32},{8,40},{16,48},{24,56},{32,0},{40,8},{48,16},{56,24},{64,96... | collective-permute-start | bytes 307208 | tf_op jit(solution)/shard_map/ppermute | solution.py:27
  145.3 2.6 %collective-permute-done.15 = bf16[16,3200]{1,0:T(8,128)(2,1)S(1)} collective-permute-done((bf16[16,3200]{1,0:T(8,128)(2,1)S(1)}, bf16[16,3200]{1,0:T(8,128)(2,1)S(1)}, u32[]{:S(2)}, u32[]{:S(2)}) %collective-permute-start.15) | collective-permute-done | bytes 102432 | tf_op jit(solution)/shard_map/ppermute | solution.py:27
  148.0 2.3 %collective-permute-start.16 = (bf16[16,3200]{1,0:T(8,128)(2,1)S(1)}, bf16[16,3200]{1,0:T(8,128)(2,1)S(1)}, u32[]{:S(2)}, u32[]{:S(2)}) collective-permute-start(bf16[16,3200]{1,0:T(8,128)(2,1)S(1)} %fusion.1), channel_id=1, source_target_pairs={{0,64},{8,72},{16,80},{24,88},{32,96},{40,104},{48,112},{56,120},{... | collective-permute-start | bytes 307208 | tf_op jit(solution)/shard_map/ppermute | solution.py:27
  150.3 1.4 multiply_convert_fusion
  151.7 1.2 collective-permute-done.16
  153.0 3.7 %collective-permute-start.17 = (bf16[16,3200]{1,0:T(8,128)(2,1)S(1)}, bf16[16,3200]{1,0:T(8,128)(2,1)S(1)}, u32[]{:S(2)}, u32[]{:S(2)}) collective-permute-start(bf16[16,3200]{1,0:T(8,128)(2,1)S(1)} %fusion.3), channel_id=1, source_target_pairs={{0,128},{8,136},{16,144},{24,152},{32,160},{40,168},{48,176},{56,1... | collective-permute-start | bytes 307208 | tf_op jit(solution)/shard_map/ppermute | solution.py:27
  156.7 1.4 convolution_convert_fusion
  158.1 1.2 collective-permute-done.17
  159.4 0.6 slice.103
  160.0 0.7 fusion.11
  (96 shorter events, 1.9 us)
Async XLA Ops:
  0.6 7.7 %copy-start = (bf16[16,1024]{1,0:T(8,128)(2,1)S(1)}, bf16[16,1024]{1,0:T(8,128)(2,1)}, u32[]{:S(2)}) copy-start(bf16[16,1024]{1,0:T(8,128)(2,1)} %param.24) | copy-start | bytes 98308
  0.6 7.7 %copy-start.1 = (bf16[512,1024]{1,0:T(8,128)(2,1)S(1)}, bf16[512,1024]{1,0:T(8,128)(2,1)}, u32[]{:S(2)}) copy-start(bf16[512,1024]{1,0:T(8,128)(2,1)} %dout_ref.1) | copy-start | bytes 3145732
  3.6 27.5 %collective-permute-start.12 = (f32[64]{0:T(128)S(1)}, f32[64]{0:T(128)S(1)}, u32[]{:S(2)}, u32[]{:S(2)}) collective-permute-start(f32[64]{0:T(128)S(1)} %select_reduce_fusion), channel_id=1, source_target_pairs={{24,0},{57,1},{90,2},{123,3},{156,4},{189,5},{222,6},{255,7},{16,8... | collective-permute-start | bytes 776 | tf_op jit(solution)/shard_map/ppermute | solution.py:40
  3.7 30.7 %collective-permute-start.11 = (f32[64]{0:T(128)S(1)}, f32[64]{0:T(128)S(1)}, u32[]{:S(2)}, u32[]{:S(2)}) collective-permute-start(f32[64]{0:T(128)S(1)} %select_reduce_fusion), channel_id=1, source_target_pairs={{16,0},{49,1},{82,2},{115,3},{148,4},{181,5},{214,6},{247,7},{24,8... | collective-permute-start | bytes 776 | tf_op jit(solution)/shard_map/ppermute | solution.py:40
  6.0 33.6 %collective-permute-start.10 = (f32[64]{0:T(128)S(1)}, f32[64]{0:T(128)S(1)}, u32[]{:S(2)}, u32[]{:S(2)}) collective-permute-start(f32[64]{0:T(128)S(1)} %select_reduce_fusion), channel_id=1, source_target_pairs={{8,0},{41,1},{74,2},{107,3},{140,4},{173,5},{206,6},{239,7},{0,8},... | collective-permute-start | bytes 776 | tf_op jit(solution)/shard_map/ppermute | solution.py:40
  6.0 33.6 %collective-permute-start.9 = (f32[64]{0:T(128)S(1)}, f32[64]{0:T(128)S(1)}, u32[]{:S(2)}, u32[]{:S(2)}) collective-permute-start(f32[64]{0:T(128)S(1)} %select_reduce_fusion), channel_id=1, source_target_pairs={{0,0},{33,1},{66,2},{99,3},{132,4},{165,5},{198,6},{231,7},{8,8},{... | collective-permute-start | bytes 776 | tf_op jit(solution)/shard_map/ppermute | solution.py:40
  8.3 17.9 %copy-start.8 = (bf16[512,128]{1,0:T(8,128)(2,1)S(1)}, bf16[512,128]{1,0:T(8,128)(2,1)}, u32[]{:S(2)}) copy-start(bf16[512,128]{1,0:T(8,128)(2,1)} %k3.1) | copy-start | bytes 393220
  8.3 18.6 %copy-start.9 = (bf16[512,128]{1,0:T(8,128)(2,1)S(1)}, bf16[512,128]{1,0:T(8,128)(2,1)}, u32[]{:S(2)}) copy-start(bf16[512,128]{1,0:T(8,128)(2,1)} %v3.1) | copy-start | bytes 393220
  8.4 21.2 %copy-start.30 = (s32[64]{0:T(128)S(1)}, s32[64]{0:T(128)}, u32[]{:S(2)}) copy-start(s32[64]{0:T(128)} %param.26) | copy-start | bytes 772
  8.4 22.4 %copy-start.20 = (bf16[16,128]{1,0:T(8,128)(2,1)S(1)}, bf16[16,128]{1,0:T(8,128)(2,1)}, u32[]{:S(2)}) copy-start(bf16[16,128]{1,0:T(8,128)(2,1)} %uv_ref.1) | copy-start | bytes 12292
  9.5 37.7 %all-to-all-start = ((bf16[8,32,512]{2,1,0:T(8,128)(2,1)}), bf16[8,32,512]{2,1,0:T(8,128)(2,1)}, u32[]{:S(2)}, u32[]{:S(2)}) async-start(bf16[8,32,512]{2,1,0:T(8,128)(2,1)} %broadcast_in_dim.55), calls=%async_computation | async-start | bytes 524288 | tf_op jit(solution)/shard_map/all_to_all | solution.py:47
  27.6 12.7 %collective-permute-start.2 = (bf16[1024,128]{1,0:T(8,128)(2,1)}, bf16[1024,128]{1,0:T(8,128)(2,1)}, u32[]{:S(2)}, u32[]{:S(2)}) collective-permute-start(bf16[1024,128]{1,0:T(8,128)(2,1)} %constant_dynamic-update-slice_fusion), channel_id=1, source_target_pairs={{0,8},{8,16},{16,24},{24,32},{32,40},{40,48},{48,56},{56,64},{64,7... | collective-permute-start | bytes 786440 | tf_op jit(solution)/shard_map/ppermute | solution.py:22
  31.0 11.1 %collective-permute-start.1 = (bf16[1024,128]{1,0:T(8,128)(2,1)}, bf16[1024,128]{1,0:T(8,128)(2,1)S(1)}, u32[]{:S(2)}, u32[]{:S(2)}) collective-permute-start(bf16[1024,128]{1,0:T(8,128)(2,1)} %constant_dynamic-update-slice_fusion), channel_id=1, source_target_pairs={{0,16},{8,24},{16,32},{24,40},{32,48},{40,56},{48,64},{56,72},{64,... | collective-permute-start | bytes 786440 | tf_op jit(solution)/shard_map/ppermute | solution.py:22
  34.4 12.1 %collective-permute-start = (bf16[1024,128]{1,0:T(8,128)(2,1)}, bf16[1024,128]{1,0:T(8,128)(2,1)S(1)}, u32[]{:S(2)}, u32[]{:S(2)}) collective-permute-start(bf16[1024,128]{1,0:T(8,128)(2,1)} %constant_dynamic-update-slice_fusion), channel_id=1, source_target_pairs={{0,24},{8,32},{16,40},{24,48},{32,56},{40,64},{48,72},{56,80},{64,... | collective-permute-start | bytes 786440 | tf_op jit(solution)/shard_map/ppermute | solution.py:22
  40.3 26.1 %copy-start.3 = (bf16[512,1024]{1,0:T(8,128)(2,1)S(1)}, bf16[512,1024]{1,0:T(8,128)(2,1)}, u32[]{:S(2)}) copy-start(bf16[512,1024]{1,0:T(8,128)(2,1)} %q_ref.1) | copy-start | bytes 3145732
  40.3 26.1 %copy-start.4 = (bf16[512,1024]{1,0:T(8,128)(2,1)S(1)}, bf16[512,1024]{1,0:T(8,128)(2,1)}, u32[]{:S(2)}) copy-start(bf16[512,1024]{1,0:T(8,128)(2,1)} %g_ref.1) | copy-start | bytes 3145732
  48.2 17.4 %copy-start.22 = (f32[32,512]{1,0:T(8,128)}, f32[32,512]{1,0:T(8,128)S(1)}, u32[]{:S(2)}) copy-start(f32[32,512]{1,0:T(8,128)S(1)} %convert_reduce_fusion) | copy-start | bytes 196612
  48.8 16.7 %collective-permute-start.5 = (bf16[16,512]{1,0:T(8,128)(2,1)}, bf16[16,512]{1,0:T(8,128)(2,1)}, u32[]{:S(2)}, u32[]{:S(2)}) collective-permute-start(bf16[16,512]{1,0:T(8,128)(2,1)} %slice.113), channel_id=1, source_target_pairs={{0,8},{8,16},{16,24},{24,32},{32,40},{40,48},{48,56},{56,64},{64,7... | collective-permute-start | bytes 49160 | tf_op jit(solution)/shard_map/ppermute | solution.py:22
  51.6 13.9 %collective-permute-start.4 = (bf16[16,512]{1,0:T(8,128)(2,1)}, bf16[16,512]{1,0:T(8,128)(2,1)}, u32[]{:S(2)}, u32[]{:S(2)}) collective-permute-start(bf16[16,512]{1,0:T(8,128)(2,1)} %slice.113), channel_id=1, source_target_pairs={{0,16},{8,24},{16,32},{24,40},{32,48},{40,56},{48,64},{56,72},{64,... | collective-permute-start | bytes 49160 | tf_op jit(solution)/shard_map/ppermute | solution.py:22
  55.7 9.9 %collective-permute-start.3 = (bf16[16,512]{1,0:T(8,128)(2,1)}, bf16[16,512]{1,0:T(8,128)(2,1)}, u32[]{:S(2)}, u32[]{:S(2)}) collective-permute-start(bf16[16,512]{1,0:T(8,128)(2,1)} %slice.113), channel_id=1, source_target_pairs={{0,24},{8,32},{16,40},{24,48},{32,56},{40,64},{48,72},{56,80},{64,... | collective-permute-start | bytes 49160 | tf_op jit(solution)/shard_map/ppermute | solution.py:22
  66.4 0.9 copy-start.10
  67.3 0.9 copy-start.11
  68.2 0.9 copy-start.12
  69.1 0.9 copy-start.13
  70.0 0.9 copy-start.14
  70.9 0.9 copy-start.15
  71.8 0.9 copy-start.16
  72.7 0.8 copy-start.19
  73.5 0.7 copy-start.21
  74.2 30.8 %copy-start.29 = (f32[64]{0:T(128)S(1)}, f32[64]{0:T(128)}, u32[]{:S(2)}) copy-start(f32[64]{0:T(128)} %get-tuple-element.54) | copy-start | bytes 772
  98.2 0.8 copy-start.6
  99.0 0.6 copy-start.17
  99.0 0.6 copy-start.18
  99.0 18.4 %copy-start.27 = (s32[64,1]{0,1:T(1,128)S(1)}, s32[64,1]{0,1:T(1,128)}, u32[]{:S(2)}) copy-start(s32[64,1]{0,1:T(1,128)} %get-tuple-element.51) | copy-start | bytes 772
  99.0 18.4 %copy-start.28 = (s32[64,1]{0,1:T(1,128)S(1)}, s32[64,1]{0,1:T(1,128)}, u32[]{:S(2)}) copy-start(s32[64,1]{0,1:T(1,128)} %get-tuple-element.67) | copy-start | bytes 772
  99.1 18.6 %copy-start.25 = (f32[64]{0:T(128)S(1)}, f32[64]{0:T(128)}, u32[]{:S(2)}) copy-start(f32[64]{0:T(128)} %compare_select_fusion.1) | copy-start | bytes 772
  99.1 18.6 %copy-start.26 = (s32[64]{0:T(128)S(1)}, s32[64]{0:T(128)}, u32[]{:S(2)}) copy-start(s32[64]{0:T(128)} %and_select_fusion.1) | copy-start | bytes 772
  99.1 18.7 %copy-start.23 = (f32[32,512]{1,0:T(8,128)S(1)}, f32[32,512]{1,0:T(8,128)}, u32[]{:S(2)}) copy-start(f32[32,512]{1,0:T(8,128)} %copy-done.22) | copy-start | bytes 196612
  99.1 32.0 %copy-start.2 = (bf16[512,1024]{1,0:T(8,128)(2,1)S(1)}, bf16[512,1024]{1,0:T(8,128)(2,1)}, u32[]{:S(2)}) copy-start(bf16[512,1024]{1,0:T(8,128)(2,1)} %hidden_ref.1) | copy-start | bytes 3145732
  99.7 31.4 %copy-start.7 = (bf16[2048,128]{1,0:T(8,128)(2,1)S(1)}, bf16[2048,128]{1,0:T(8,128)(2,1)}, u32[]{:S(2)}) copy-start(bf16[2048,128]{1,0:T(8,128)(2,1)} %copy-done.6) | copy-start | bytes 1572868
  99.7 7.1 %collective-permute-start.6 = (bf16[16,512]{1,0:T(8,128)(2,1)S(1)}, bf16[16,512]{1,0:T(8,128)(2,1)S(1)}, u32[]{:S(2)}, u32[]{:S(2)}) collective-permute-start(bf16[16,512]{1,0:T(8,128)(2,1)S(1)} %get-tuple-element.64), channel_id=1, source_target_pairs={{24,0},{32,8},{40,16},{48,24},{56,32},{64,40},{72,48},{80,56},{88,... | collective-permute-start | bytes 49160 | tf_op jit(solution)/shard_map/ppermute | solution.py:22
  101.1 5.6 %collective-permute-start.8 = (bf16[16,512]{1,0:T(8,128)(2,1)S(1)}, bf16[16,512]{1,0:T(8,128)(2,1)S(1)}, u32[]{:S(2)}, u32[]{:S(2)}) collective-permute-start(bf16[16,512]{1,0:T(8,128)(2,1)S(1)} %get-tuple-element.65), channel_id=1, source_target_pairs={{8,0},{16,8},{24,16},{32,24},{40,32},{48,40},{56,48},{64,56},{72,6... | collective-permute-start | bytes 49160 | tf_op jit(solution)/shard_map/ppermute | solution.py:22
  103.0 5.8 %collective-permute-start.7 = (bf16[16,512]{1,0:T(8,128)(2,1)S(1)}, bf16[16,512]{1,0:T(8,128)(2,1)S(1)}, u32[]{:S(2)}, u32[]{:S(2)}) collective-permute-start(bf16[16,512]{1,0:T(8,128)(2,1)S(1)} %get-tuple-element.66), channel_id=1, source_target_pairs={{16,0},{24,8},{32,16},{40,24},{48,32},{56,40},{64,48},{72,56},{80,... | collective-permute-start | bytes 49160 | tf_op jit(solution)/shard_map/ppermute | solution.py:22
  110.3 20.8 %all-to-all-start.1 = ((bf16[8,40,512]{2,1,0:T(8,128)(2,1)}), bf16[8,40,512]{2,1,0:T(8,128)(2,1)S(1)}, u32[]{:S(2)}, u32[]{:S(2)}) async-start(bf16[8,40,512]{2,1,0:T(8,128)(2,1)} %broadcast_in_dim.90), calls=%async_computation.1 | async-start | bytes 655360 | tf_op jit(solution)/shard_map/all_to_all | solution.py:47
  131.1 1.2 copy-start.5
  134.2 1.4 collective-permute-start.13
  135.6 5.0 %collective-permute-start.14 = (bf16[16,3200]{1,0:T(8,128)(2,1)S(1)}, bf16[16,3200]{1,0:T(8,128)(2,1)S(1)}, u32[]{:S(2)}, u32[]{:S(2)}) collective-permute-start(bf16[16,3200]{1,0:T(8,128)(2,1)S(1)} %fusion), channel_id=1, source_target_pairs={{0,16},{8,24},{16,0},{24,8},{32,48},{40,56},{48,32},{56,40},{64,80... | collective-permute-start | bytes 307208 | tf_op jit(solution)/shard_map/ppermute | solution.py:27
  140.7 16.0 %copy-start.24 = (bf16[1024,16]{0,1:T(8,128)(2,1)S(1)}, bf16[1024,16]{0,1:T(8,128)(2,1)}, u32[]{:S(2)}) copy-start(bf16[1024,16]{0,1:T(8,128)(2,1)} %param.21) | copy-start | bytes 98308
  140.7 7.2 %collective-permute-start.15 = (bf16[16,3200]{1,0:T(8,128)(2,1)S(1)}, bf16[16,3200]{1,0:T(8,128)(2,1)S(1)}, u32[]{:S(2)}, u32[]{:S(2)}) collective-permute-start(bf16[16,3200]{1,0:T(8,128)(2,1)S(1)} %fusion.7), channel_id=1, source_target_pairs={{0,32},{8,40},{16,48},{24,56},{32,0},{40,8},{48,16},{56,24},{64,96... | collective-permute-start | bytes 307208 | tf_op jit(solution)/shard_map/ppermute | solution.py:27
  148.0 4.9 %collective-permute-start.16 = (bf16[16,3200]{1,0:T(8,128)(2,1)S(1)}, bf16[16,3200]{1,0:T(8,128)(2,1)S(1)}, u32[]{:S(2)}, u32[]{:S(2)}) collective-permute-start(bf16[16,3200]{1,0:T(8,128)(2,1)S(1)} %fusion.1), channel_id=1, source_target_pairs={{0,64},{8,72},{16,80},{24,88},{32,96},{40,104},{48,112},{56,120},{... | collective-permute-start | bytes 307208 | tf_op jit(solution)/shard_map/ppermute | solution.py:27
  153.0 6.4 %collective-permute-start.17 = (bf16[16,3200]{1,0:T(8,128)(2,1)S(1)}, bf16[16,3200]{1,0:T(8,128)(2,1)S(1)}, u32[]{:S(2)}, u32[]{:S(2)}) collective-permute-start(bf16[16,3200]{1,0:T(8,128)(2,1)S(1)} %fusion.3), channel_id=1, source_target_pairs={{0,128},{8,136},{16,144},{24,152},{32,160},{40,168},{48,176},{56,1... | collective-permute-start | bytes 307208 | tf_op jit(solution)/shard_map/ppermute | solution.py:27

commit v2 on v1

--- a/solution.py
+++ b/solution.py
@@ -18,8 +18,7 @@
 
 def shift(value, by):
     n = lax.axis_size("ctx")
-    pairs = [(i, i + by) for i in range(n) if 0 <= i + by < n]
-    return lax.ppermute(value, "ctx", pairs)
+    return lax.ppermute(value, "ctx", [(i, (i + by) % n) for i in range(n)])
 
 
 def flip(value, mask):
@@ -27,19 +26,13 @@
     return lax.ppermute(value, "ctx", [(i, i ^ mask) for i in range(n)])
 
 
-def spread_margins(part):
+def spread(part):
     n_ctx, n_tp = lax.axis_size("ctx"), lax.axis_size("tp")
     per = n_ctx // n_tp
-    total = None
-    for m in range(per):
-        pairs = [
-            ((c ^ (per * j + m)) * n_tp + j, c * n_tp + j)
-            for c in range(n_ctx)
-            for j in range(n_tp)
-        ]
-        got = lax.ppermute(part, ("ctx", "tp"), pairs)
-        total = got if total is None else total + got
-    return total
+    pairs = [
+        ((c + per * j) % n_ctx * n_tp + j, c * n_tp + j) for c in range(n_ctx) for j in range(n_tp)
+    ]
+    return lax.ppermute(part, ("ctx", "tp"), pairs)
 
 
 def share_tp(rows):
@@ -60,37 +53,47 @@
 
 
 def attn_kernel(
-    start_ref, q_ref, g_ref, aot_ref, r_ref, k0, k1, k2, k3, v0, v1, v2, v3, lv_ref, uvt_ref, uv_ref,
+    start_ref, q_ref, g_ref, aot_ref, rt_ref, kv0, kv1, kv2, kv3, lv_far, lv_near, lv_own, uvt_ref, uv_ref,
     o_ref, lowo_ref, z_ref, vg_ref,
-    bias, vt, s_scr, p_scr, vg,
+    kv, sems, bias, vt, r_scr, s_scr, p_scr, vg,
 ):
     head = pl.program_id(0)
     rows = q_ref.shape[0]
+    rank = uv_ref.shape[0]
     width = 4 * rows
     n_kb = width // KB
     scale = math.log2(math.e) / math.sqrt(HD)
-    ks = (k0, k1, k2, k3)
     per = rows // KB
 
     @pl.when(head == 0)
     def _():
+        copies = [
+            pltpu.make_async_copy(ref, kv.at[slot], sems.at[slot])
+            for slot, ref in enumerate((kv0, kv1, kv2, kv3))
+        ]
+        for copy in copies:
+            copy.start()
         start = start_ref[0:1, :]
         qpos = start_ref[1:2, :]
         for kb in range(n_kb):
             kpos = lax.broadcasted_iota(jnp.int32, (KB, rows), 0) + kb * KB
             ok = (kpos >= start) & (kpos <= qpos)
             bias[kb * KB : (kb + 1) * KB, :] = jnp.where(ok, 0.0, NEG)
-        for s, ref in enumerate((v0, v1, v2, v3)):
-            low = lv_ref[:, s * rows : (s + 1) * rows]
-            frozen = ref[...].astype(F32).T
-            vt[:, s * rows : (s + 1) * rows] = (frozen + 2.0 * nn(uvt_ref[...], low)).astype(BF16)
+        r_scr[...] = rt_ref[...].astype(F32).T.astype(BF16)
         vg[...] = jnp.zeros_like(vg)
         lowo_ref[...] = jnp.zeros_like(lowo_ref)
+        lows = (
+            lv_far[0:rank, 0:rows], lv_far[0:rank, rows : 2 * rows], lv_near[0:rank, :], lv_own[0:rank, :],
+        )
+        for slot, copy in enumerate(copies):
+            copy.wait()
+            frozen = kv[slot, rows : 2 * rows, :].astype(F32).T
+            vt[:, slot * rows : (slot + 1) * rows] = (frozen + 2.0 * nn(uvt_ref[...], lows[slot])).astype(BF16)
 
     q = q_ref[...]
     top = None
     for kb in range(n_kb):
-        key = ks[kb // per][(kb % per) * KB : (kb % per + 1) * KB, :]
+        key = kv[kb // per, (kb % per) * KB : (kb % per + 1) * KB, :]
         s = nt(key, q) * scale + bias[kb * KB : (kb + 1) * KB, :]
         s_scr[kb * KB : (kb + 1) * KB, :] = s
         m = jnp.max(s, axis=0, keepdims=True)
@@ -106,7 +109,7 @@
     o_ref[...] = ot.astype(F32).T.astype(BF16)
     lowo_ref[...] += nn(aot_ref[...], ot)
     inv_rows = jnp.broadcast_to(inv, (HD, rows)).T
-    grad = g_ref[...].astype(F32) + nn(r_ref[...], aot_ref[...])
+    grad = g_ref[...].astype(F32) + nn(r_scr[...], aot_ref[...])
     grad = (grad * inv_rows).astype(BF16)
     vg[...] += nn(p_scr[...], grad)
 
@@ -117,7 +120,7 @@
         z_ref[...] = nt(uv_ref[...], total_vg).astype(BF16)
 
 
-def attention(start_q, queries, cotangent, a_o_t, r, keys, frozen, low_v_t, u_v):
+def attention(start_q, queries, cotangent, a_o_t, r_t, kvs, lows, u_v):
     rows = queries.shape[0]
     heads = queries.shape[1] // HD
     rank = u_v.shape[0]
@@ -126,9 +129,10 @@
     return pl.pallas_call(
         attn_kernel,
         grid=(heads,),
-        in_specs=[full(start_q.shape), column, column, pl.BlockSpec((rank, HD), lambda h: (0, h)), full(r.shape)]
-        + [full((rows, HD))] * 8
-        + [full(low_v_t.shape), full((HD, rank)), full((rank, HD))],
+        in_specs=[full(start_q.shape), column, column, pl.BlockSpec((rank, HD), lambda h: (0, h)), full(r_t.shape)]
+        + [pl.BlockSpec(memory_space=pl.ANY)] * 4
+        + [full(a.shape) for a in lows]
+        + [full((HD, rank)), full((rank, HD))],
         out_specs=[column, full((rank, rows)), full((rank, 4 * rows)), full((4 * rows, HD))],
         out_shape=[
             jax.ShapeDtypeStruct((rows, heads * HD), BF16),
@@ -137,8 +141,11 @@
             jax.ShapeDtypeStruct((4 * rows, HD), BF16),
         ],
         scratch_shapes=[
+            pltpu.VMEM((4, 2 * rows, HD), BF16),
+            pltpu.SemaphoreType.DMA((4,)),
             pltpu.VMEM((4 * rows, rows), F32),
             pltpu.VMEM((HD, 4 * rows), BF16),
+            pltpu.VMEM((rows, rank), BF16),
             pltpu.VMEM((4 * rows, rows), F32),
             pltpu.VMEM((4 * rows, rows), BF16),
             pltpu.VMEM((4 * rows, HD), F32),
@@ -147,16 +154,16 @@
             dimension_semantics=("arbitrary",), vmem_limit_bytes=48 * 2**20
         ),
         name="attn",
-    )(start_q, queries, cotangent, a_o_t, r, *keys, *frozen, low_v_t, u_v.T, u_v)
+    )(start_q, queries, cotangent, a_o_t, r_t, *kvs, *lows, u_v.T, u_v)
 
 
 def grads_kernel(
-    shared_ref, pair_ref, ends_ref, rt_ref, lv_ref, vg_ref, hidden_ref, o_ref, dout_ref,
+    shared_ref, pair_ref, ends_ref, rt_ref, lv_far, lv_near, lv_own, vg_ref, hidden_ref, o_ref, dout_ref,
     vd_ref, od_ref, ou_ref, vu_ref, lowo_ref, lvg_ref, wr_scr, wlo_scr,
 ):
     step = pl.program_id(0)
     rank, rows = rt_ref.shape
-    width = lv_ref.shape[1]
+    width = vg_ref.shape[0]
 
     @pl.when(step == 0)
     def _():
@@ -178,15 +185,19 @@
         lowo_ref[...] = low_o
         wr_scr[...] = (own * rt_ref[...].astype(F32)).astype(BF16)
         wlo_scr[...] = (own * low_o.astype(F32)).astype(BF16)
-        wlv = (token_weight * lv_ref[...].astype(F32)).astype(BF16)
-        vu_ref[...] = (2.0 * nn(wlv, vg_ref[...])).astype(BF16)
+        up = jnp.zeros(vu_ref.shape, F32)
+        for ref, at in ((lv_far, 0), (lv_near, 2 * rows), (lv_own, 3 * rows)):
+            end = at + ref.shape[1]
+            wlv = (token_weight[:, at:end] * ref[0:rank, :].astype(F32)).astype(BF16)
+            up = up + nn(wlv, vg_ref[at:end, :])
+        vu_ref[...] = (2.0 * up).astype(BF16)
 
     vd_ref[...] = nn(lvg_ref[...], hidden_ref[...]).astype(BF16)
     od_ref[...] = nn(wr_scr[...], o_ref[...]).astype(BF16)
     ou_ref[...] = (2.0 * nn(wlo_scr[...], dout_ref[...])).astype(BF16)
 
 
-def grads(shared, pair, ends, r_t, low_v_t, vg, hidden, o, d_out):
+def grads(shared, pair, ends, r_t, lows, vg, hidden, o, d_out):
     rank, rows = r_t.shape
     cols = hidden.shape[1]
     tile = min(256, cols)
@@ -197,7 +208,7 @@
     return pl.pallas_call(
         grads_kernel,
         grid=(cols // tile,),
-        in_specs=[full(a) for a in (shared, pair, ends, r_t, low_v_t, vg)] + [column] * 3,
+        in_specs=[full(a) for a in (shared, pair, ends, r_t, *lows, vg)] + [column] * 3,
         out_specs=[part, part, part, pl.BlockSpec((rank, HD), lambda i: (0, 0)), small, small],
         out_shape=[jax.ShapeDtypeStruct((rank, cols), BF16)] * 3
         + [jax.ShapeDtypeStruct((rank, HD), BF16)]
@@ -207,7 +218,7 @@
             dimension_semantics=("arbitrary",), vmem_limit_bytes=32 * 2**20
         ),
         name="grads",
-    )(shared, pair, ends, r_t, low_v_t, vg, hidden, o, d_out)
+    )(shared, pair, ends, r_t, *lows, vg, hidden, o, d_out)
 
 
 def three_parts(x):
@@ -215,6 +226,17 @@
     high = keep(x)
     mid = keep(x - high)
     return high, mid, x - high - mid
+
+
+def margin_rows(margin, width):
+    line = [jnp.pad(part, (0, 128 - part.shape[0])) for part in three_parts(margin)]
+    line = jnp.concatenate(line + [jnp.zeros((width - 384,), F32)])
+    return jnp.pad(line[None, :], ((0, 7), (0, 0)))
+
+
+def margin_of(line):
+    line = line.astype(F32)
+    return line[0:128] + line[128:256] + line[256:384]
 
 
 def shards(
@@ -227,9 +249,7 @@
     first = lax.axis_index("ctx") * rows
 
     kv = jnp.concatenate([rotated_keys, frozen_value_rows], axis=0)
-    kv_behind = [shift(kv, by) for by in (3, 2, 1)]
-    keys = [x[:rows] for x in kv_behind] + [rotated_keys]
-    frozen = [x[rows:] for x in kv_behind] + [frozen_value_rows]
+    kvs = [shift(kv, by) for by in (3, 2, 1)]
 
     low_v_part = lax.dot_general(
         adapter_a_v, hidden, (((0,), (1,)), ((), ())), preferred_element_type=F32
@@ -237,9 +257,7 @@
     r_part = nt(output_up_matrix, out_cotangent)
     stacked = jnp.concatenate([low_v_part, r_part], axis=0).astype(BF16)
     shared = jnp.sum(share_tp(stacked).astype(F32), axis=0)
-    low_v_t = shared[:rank].astype(BF16)
     r_t = (2.0 * shared[rank:]).astype(BF16)
-    low_v_window = jnp.concatenate([shift(low_v_t, by) for by in (3, 2, 1)] + [low_v_t], axis=1)
 
     doc_ids = jnp.arange(docs, dtype=jnp.int32)
     upto = (doc_ids[:, None] <= doc_ids[None, :]).astype(jnp.int32)
@@ -247,24 +265,28 @@
     doc_starts = doc_ends - doc_lengths
     pos = first + jnp.arange(rows, dtype=jnp.int32)
     own = (doc_starts[:, None] <= pos[None, :]) & (pos[None, :] < doc_ends[:, None])
-    margin_part = jnp.sum(jnp.where(own, token_logratio[None, :], 0.0), axis=1)
-    margin_part = spread_margins(margin_part)
+    margin = jnp.sum(jnp.where(own, token_logratio[None, :], 0.0), axis=1)
     base = first - 3 * rows
     start = jnp.sum(jnp.where(own, doc_starts[:, None], 0), axis=0) - base
     start_q = jnp.zeros((8, rows), jnp.int32).at[0].set(start).at[1].set(pos - base)
 
+    low_own = jnp.concatenate([shared[:rank], margin_rows(margin, rows)], axis=0).astype(BF16)
+    low_own, kvs = lax.optimization_barrier((low_own, kvs))
+    low_near = shift(low_own, 1)
+    low_far = shift(jnp.concatenate([low_near, low_own], axis=1), 2)
+    lows = (low_far, low_near, low_own)
+
     o, low_o_part, z, vg = attention(
-        start_q, queries, attn_cotangent, adapter_a_o.T, r_t.T, keys, frozen, low_v_window, value_up_matrix
-    )
-
-    z_own = z[:, 3 * rows :].astype(F32)
-    for slot in range(3):
-        z_own = z_own + shift(z[:, slot * rows : (slot + 1) * rows], slot - 3).astype(F32)
-    line = jnp.zeros((1, rows), F32)
-    for i, piece in enumerate(three_parts(margin_part)):
-        line = lax.dynamic_update_slice(line, piece[None, :], (0, 128 * i))
-    line = jnp.pad(line, ((0, 7), (0, 0)))
-    sent = jnp.concatenate([z_own, low_o_part, line], axis=0).astype(BF16)
+        start_q, queries, attn_cotangent, adapter_a_o.T, r_t, kvs + [kv], lows, value_up_matrix
+    )
+
+    margin = margin_of(low_own[rank]) + margin_of(low_near[rank])
+    margin = margin + margin_of(low_far[rank, :rows]) + margin_of(low_far[rank, rows:])
+    margin = spread(margin)
+    z_far = shift(z[:, : 2 * rows], -2).astype(F32)
+    z_near = shift((z[:, 2 * rows : 3 * rows].astype(F32) + z_far[:, :rows]).astype(BF16), -1)
+    z_own = z[:, 3 * rows :].astype(F32) + z_far[:, rows:] + z_near.astype(F32)
+    sent = jnp.concatenate([z_own, low_o_part, margin_rows(margin, rows)], axis=0).astype(BF16)
     shared_back = share_tp(sent)
 
     pair_ids = pair_slots // 2
@@ -276,10 +298,11 @@
     ends = jnp.stack([doc_starts - base, doc_ends - base], axis=1)
     ends = jnp.pad(ends, ((0, 0), (0, 126)))
     vd, od, ou, vu, low_o_t, lvg_t = grads(
-        shared_back, pair, ends, r_t, low_v_window, vg, hidden, o, out_cotangent
+        shared_back, pair, ends, r_t, lows, vg, hidden, o, out_cotangent
     )
     total = jnp.concatenate([vd, od, ou, vu], axis=1).astype(F32)
     for mask in (1, 2, 4, 8, 16):
+        total = lax.reduce_precision(total, 8, 7)
         total = total + flip(total.astype(BF16), mask).astype(F32)
     cols = hidden.shape[1]
     term = (2.0 * tn(low_o_t, output_up_matrix)).astype(BF16)

time: 164 us -> 128 us (0.78); the launches traced: 161 us -> 127 us
  starting transfers between devices: 68.3 us -> 32.3 us
  waiting for transfers between devices: 30.2 us -> 48.8 us
  local copies, waits for them, and re-layouts: 21.3 us -> 10.7 us
  other arithmetic: 8.98 us -> 3.11 us
    ppermute x13 -> x8, starting transfers between devices: 33.5 us -> 10.8 us  [the longest x7 10.2 us: shift(): return lax.ppermute(value, 'ctx', [(i, (i + by) % n) for i in range(n)])]
    all_to_all x2, waiting for transfers between devices: 13.2 us -> 23.9 us  [share_tp(): lax.all_to_all(jnp.broadcast_to(rows[None], (n,) + rows.shape), 'tp', 0, 0)]
    all_to_all x2, starting transfers between devices: 24 us -> 13.5 us  [share_tp(): lax.all_to_all(jnp.broadcast_to(rows[None], (n,) + rows.shape), 'tp', 0, 0)]
    ppermute x13 -> x8, waiting for transfers between devices: 5.72 us -> 11.9 us  [the longest x7 11.9 us: shift(): return lax.ppermute(value, 'ctx', [(i, (i + by) % n) for i in range(n)])]
    unnamed x67 -> x50, local copies, waits for them, and re-layouts: 11.3 us -> 6.76 us
    slice x5 -> x2, local copies, waits for them, and re-layouts: 3.91 us -> 0.01 us  [the longest x1 0.01 us: shards(): shared[:rank]]
    ppermute x5, starting transfers between devices: 10.8 us -> 7.97 us  [flip(): return lax.ppermute(value, 'ctx', [(i, i ^ mask) for i in range(n)])]
    ppermute x5, waiting for transfers between devices: 11.3 us -> 13 us  [flip(): return lax.ppermute(value, 'ctx', [(i, i ^ mask) for i in range(n)])]
  transfers between devices with their start and end apart: 20 -> 15, of which waited for: 8 -> 11; matrix products, arithmetic and copies ran while one was open for 10% -> 7% of each run, Pallas kernels for 0% -> 19%
where the time goes in v2:
time: 128 us; the launch traced here: 127 us
  waiting for transfers between devices  48.8 us (38%)
  starting transfers between devices  32.3 us (25%)
  Pallas kernels  26.5 us (21%)
  local copies, waits for them, and re-layouts  10.7 us (8%)
  matrix products  4.83 us (4%)
  other arithmetic  3.11 us (2%)
    pallas_call x1, Pallas kernels, attention(): pl.pallas_call(attn_kernel, grid=(heads,), in_specs=[full(start_q.shape),...  24.6 us
    all_to_all x2, waiting for transfers between devices, share_tp(): lax.all_to_all(jnp.broadcast_to(rows[None], (n,) + rows.shape), 'tp', 0, 0)  23.9 us
    all_to_all x2, starting transfers between devices, share_tp(): lax.all_to_all(jnp.broadcast_to(rows[None], (n,) + rows.shape), 'tp', 0, 0)  13.5 us
    ppermute x5, waiting for transfers between devices, flip(): return lax.ppermute(value, 'ctx', [(i, i ^ mask) for i in range(n)])  13 us
    ppermute x7, waiting for transfers between devices, shift(): return lax.ppermute(value, 'ctx', [(i, (i + by) % n) for i in range(n)])  11.9 us
    ppermute x7, starting transfers between devices, shift(): return lax.ppermute(value, 'ctx', [(i, (i + by) % n) for i in range(n)])  10.2 us
    ppermute x5, starting transfers between devices, flip(): return lax.ppermute(value, 'ctx', [(i, i ^ mask) for i in range(n)])  7.97 us
    unnamed x50, local copies, waits for them, and re-layouts  6.76 us
  transfers between devices with their start and end apart: 15, of which 11 were waited for; matrix products, arithmetic and copies ran while one was open for 7% of the time, Pallas kernels for 19%

profile of v2, /device:TPU:2, one launch (start us, length us, event | category | flops | bytes accessed | tf_op | source)
XLA Modules:
  0.0 127.4 jit_solution(264431085093782627)
XLA Ops:
  0.6 0.0 copy-start
  0.7 1.0 constant_dynamic-update-slice_fusion.1
  1.7 0.9 constant_dynamic-update-slice_fusion.kv3
  2.6 0.1 collective-permute-start.2
  2.7 1.6 %collective-permute-start.1 = (bf16[1024,128]{1,0:T(8,128)(2,1)S(1)}, bf16[1024,128]{1,0:T(8,128)(2,1)}, u32[]{:S(2)}, u32[]{:S(2)}) collective-permute-start(bf16[1024,128]{1,0:T(8,128)(2,1)S(1)} %constant_dynamic-update-slice_fusion.kv3), channel_id=1, source_target_pairs={{0,16},{8,24},{16,32},{24,40},{32,48},{40,56},{48,64},{56,72},{64,... | collective-permute-start | bytes 786440 | tf_op jit(solution)/shard_map/ppermute | solution.py:21
  4.3 2.0 %collective-permute-start = (bf16[1024,128]{1,0:T(8,128)(2,1)S(1)}, bf16[1024,128]{1,0:T(8,128)(2,1)}, u32[]{:S(2)}, u32[]{:S(2)}) collective-permute-start(bf16[1024,128]{1,0:T(8,128)(2,1)S(1)} %constant_dynamic-update-slice_fusion.kv3), channel_id=1, source_target_pairs={{0,24},{8,32},{16,40},{24,48},{32,56},{40,64},{48,72},{56,80},{64,... | collective-permute-start | bytes 786440 | tf_op jit(solution)/shard_map/ppermute | solution.py:21
  6.3 1.6 %convolution_convert_fusion.2 = bf16[16,512]{1,0:T(8,128)(2,1)S(1)} fusion(bf16[1024,16]{0,1:T(8,128)(2,1)} %param.21, bf16[512,1024]{1,0:T(8,128)(2,1)} %hidden_ref.1), kind=kOutput, calls=%fused_computation.3 | convolution fusion | flops 16785408 | bytes 1097728 | tf_op jit(solution)/shard_map/dot_general | solution.py:254
  7.9 0.0 copy-done.1
  7.9 0.0 copy-start.21
  7.9 0.0 copy-start.16
  8.0 0.0 copy-start.4
  8.0 0.4 convolution_convert_fusion.1
  8.4 0.7 broadcast_in_dim.82
  9.1 8.5 %all-to-all-start = ((bf16[8,32,512]{2,1,0:T(8,128)(2,1)}), bf16[8,32,512]{2,1,0:T(8,128)(2,1)}, u32[]{:S(2)}, u32[]{:S(2)}) async-start(bf16[8,32,512]{2,1,0:T(8,128)(2,1)} %broadcast_in_dim.82), calls=%async_computation | async-start | bytes 524288 | tf_op jit(solution)/shard_map/all_to_all | solution.py:40
  17.6 0.1 select_reduce_fusion.2
  17.7 0.5 subtract_bitcast_fusion.1
  18.2 0.1 select_reduce_fusion.1
  18.3 0.2 select_reduce_fusion
  18.5 0.0 copy-start.19
  18.6 0.7 copy.25
  19.3 0.1 scatter.9.start_ref
  19.4 0.6 compare_select_fusion.1
  20.0 9.9 %all-to-all-done = bf16[8,32,512]{2,1,0:T(8,128)(2,1)} async-done(((bf16[8,32,512]{2,1,0:T(8,128)(2,1)}), bf16[8,32,512]{2,1,0:T(8,128)(2,1)}, u32[]{:S(2)}, u32[]{:S(2)}) %all-to-all-start) | async-done | bytes 262176 | tf_op jit(solution)/shard_map/all_to_all | solution.py:40
  29.9 1.0 convert_reduce_fusion
  31.0 0.1 collective-permute-start.3
  31.1 3.2 %collective-permute-done.3.lv_near = bf16[24,512]{1,0:T(8,128)(2,1)S(1)} collective-permute-done((bf16[24,512]{1,0:T(8,128)(2,1)S(1)}, bf16[24,512]{1,0:T(8,128)(2,1)S(1)}, u32[]{:S(2)}, u32[]{:S(2)}) %collective-permute-start.3) | collective-permute-done | bytes 24608 | tf_op jit(solution)/shard_map/ppermute | solution.py:21
  34.3 0.9 collective-permute-start.4
  35.2 5.6 %collective-permute-done.4.lv_far = bf16[24,1024]{1,0:T(8,128)(2,1)S(1)} collective-permute-done((bf16[24,1024]{1,0:T(8,128)(2,1)S(1)}, bf16[24,1024]{1,0:T(8,128)(2,1)S(1)}, u32[]{:S(2)}, u32[]{:S(2)}) %collective-permute-start.4) | collective-permute-done | bytes 49184 | tf_op jit(solution)/shard_map/ppermute | solution.py:21
  40.9 0.7 collective-permute-start.7
  41.6 0.7 copy-done.8
  42.3 0.7 copy-done.10
  43.1 0.8 copy-done.11
  43.8 0.7 copy-done.13
  44.5 24.6 %attn.1 = (bf16[512,1024]{1,0:T(8,128)(2,1)}, f32[16,512]{1,0:T(8,128)S(1)}, bf16[16,2048]{1,0:T(8,128)(2,1)S(1)}, bf16[2048,128]{1,0:T(8,128)(2,1)S(1)}) custom-call(s32[8,512]{1,0:T(8,128)S(1)} %copy-done.10, bf16[512,1024]{1,0:T(8,128)(2,1)S(1)} %copy-done.3, bf16[512,1024]{1,0:T(8,128)(2,1)S(1)} %copy-done.4, bf16[16,1024]{1,0:T(8,128)(2,1)S(1)} %bitcast.22, ...), custom_call_target="tpu_custom_call" | custom-call | tf_op jit(solution)/shard_map/attn/pallas_call | solution.py:129
  69.2 0.8 copy-done.6
  70.0 5.4 %collective-permute-start.5 = (bf16[16,1024]{1,0:T(8,128)(2,1)S(1)}, bf16[16,1024]{1,0:T(8,128)(2,1)S(1)}, u32[]{:S(2)}, u32[]{:S(2)}) collective-permute-start(bf16[16,1024]{1,0:T(8,128)(2,1)S(1)} %slice.126), channel_id=1, source_target_pairs={{0,240},{8,248},{16,0},{24,8},{32,16},{40,24},{48,32},{56,40},{64,... | collective-permute-start | bytes 98312 | tf_op jit(solution)/shard_map/ppermute | solution.py:21
  75.4 1.6 %collective-permute-done.5 = bf16[16,1024]{1,0:T(8,128)(2,1)S(1)} collective-permute-done((bf16[16,1024]{1,0:T(8,128)(2,1)S(1)}, bf16[16,1024]{1,0:T(8,128)(2,1)S(1)}, u32[]{:S(2)}, u32[]{:S(2)}) %collective-permute-start.5) | collective-permute-done | bytes 32800 | tf_op jit(solution)/shard_map/ppermute | solution.py:21
  77.1 0.1 collective-permute-start.6
  77.2 1.4 %collective-permute-done.6 = bf16[16,512]{1,0:T(8,128)(2,1)S(1)} collective-permute-done((bf16[16,512]{1,0:T(8,128)(2,1)S(1)}, bf16[16,512]{1,0:T(8,128)(2,1)S(1)}, u32[]{:S(2)}, u32[]{:S(2)}) %collective-permute-start.6) | collective-permute-done | bytes 16416 | tf_op jit(solution)/shard_map/ppermute | solution.py:21
  78.6 0.7 broadcast_in_dim.87
  79.4 5.1 %all-to-all-start.1 = ((bf16[8,40,512]{2,1,0:T(8,128)(2,1)}), bf16[8,40,512]{2,1,0:T(8,128)(2,1)S(1)}, u32[]{:S(2)}, u32[]{:S(2)}) async-start(bf16[8,40,512]{2,1,0:T(8,128)(2,1)} %broadcast_in_dim.87), calls=%async_computation.1 | async-start | bytes 655360 | tf_op jit(solution)/shard_map/all_to_all | solution.py:40
  84.4 0.1 copy.26
  84.6 0.1 compare_select_fusion
  84.7 0.1 broadcast_in_dim.92
  84.7 14.0 %all-to-all-done.1.shared_ref = bf16[8,40,512]{2,1,0:T(8,128)(2,1)S(1)} async-done(((bf16[8,40,512]{2,1,0:T(8,128)(2,1)}), bf16[8,40,512]{2,1,0:T(8,128)(2,1)S(1)}, u32[]{:S(2)}, u32[]{:S(2)}) %all-to-all-start.1) | async-done | bytes 327712 | tf_op jit(solution)/shard_map/all_to_all | solution.py:40
  98.8 1.2 copy-done.5
  100.0 1.9 %grads.1 = (bf16[16,1024]{1,0:T(8,128)(2,1)S(1)}, bf16[16,1024]{1,0:T(8,128)(2,1)S(1)}, bf16[16,1024]{1,0:T(8,128)(2,1)S(1)}, bf16[16,128]{1,0:T(8,128)(2,1)S(1)...) custom-call(bf16[8,40,512]{2,1,0:T(8,128)(2,1)S(1)} %all-to-all-done.1.shared_ref, ...), custom_call_target="tpu_custom_call" | custom-call | tf_op jit(solution)/shard_map/grads/pallas_call | solution.py:208
  101.9 0.4 collective-permute-start.8
  102.3 1.2 collective-permute-done.8
  103.5 1.3 %collective-permute-start.9 = (bf16[16,3200]{1,0:T(8,128)(2,1)S(1)}, bf16[16,3200]{1,0:T(8,128)(2,1)S(1)}, u32[]{:S(2)}, u32[]{:S(2)}) collective-permute-start(bf16[16,3200]{1,0:T(8,128)(2,1)S(1)} %fusion.1), channel_id=1, source_target_pairs={{0,16},{8,24},{16,0},{24,8},{32,48},{40,56},{48,32},{56,40},{64,80... | collective-permute-start | bytes 307208 | tf_op jit(solution)/shard_map/ppermute | solution.py:26
  104.8 3.7 %collective-permute-done.9 = bf16[16,3200]{1,0:T(8,128)(2,1)S(1)} collective-permute-done((bf16[16,3200]{1,0:T(8,128)(2,1)S(1)}, bf16[16,3200]{1,0:T(8,128)(2,1)S(1)}, u32[]{:S(2)}, u32[]{:S(2)}) %collective-permute-start.9) | collective-permute-done | bytes 102432 | tf_op jit(solution)/shard_map/ppermute | solution.py:26
  108.6 2.5 %collective-permute-start.10 = (bf16[16,3200]{1,0:T(8,128)(2,1)S(1)}, bf16[16,3200]{1,0:T(8,128)(2,1)S(1)}, u32[]{:S(2)}, u32[]{:S(2)}) collective-permute-start(bf16[16,3200]{1,0:T(8,128)(2,1)S(1)} %fusion.25), channel_id=1, source_target_pairs={{0,32},{8,40},{16,48},{24,56},{32,0},{40,8},{48,16},{56,24},{64,96... | collective-permute-start | bytes 307208 | tf_op jit(solution)/shard_map/ppermute | solution.py:26
  111.0 3.8 %collective-permute-done.10 = bf16[16,3200]{1,0:T(8,128)(2,1)S(1)} collective-permute-done((bf16[16,3200]{1,0:T(8,128)(2,1)S(1)}, bf16[16,3200]{1,0:T(8,128)(2,1)S(1)}, u32[]{:S(2)}, u32[]{:S(2)}) %collective-permute-start.10) | collective-permute-done | bytes 102432 | tf_op jit(solution)/shard_map/ppermute | solution.py:26
  114.8 0.1 fusion.2
  114.9 0.9 collective-permute-start.11
  115.8 1.4 %multiply_convert_fusion = bf16[512,1024]{1,0:T(8,128)(2,1)} fusion(bf16[16,512]{1,0:T(8,128)(2,1)S(1)} %get-tuple-element.53, bf16[16,1024]{1,0:T(8,128)(2,1)S(1)} %copy-done), kind=kOutput, calls=%fused_computation | convolution fusion | flops 17825792 | bytes 1097728 | tf_op jit(solution)/shard_map/dot_general | solution.py:52
  117.3 2.4 %collective-permute-done.11 = bf16[16,3200]{1,0:T(8,128)(2,1)S(1)} collective-permute-done((bf16[16,3200]{1,0:T(8,128)(2,1)S(1)}, bf16[16,3200]{1,0:T(8,128)(2,1)S(1)}, u32[]{:S(2)}, u32[]{:S(2)}) %collective-permute-start.11) | collective-permute-done | bytes 102432 | tf_op jit(solution)/shard_map/ppermute | solution.py:26
  119.7 0.1 fusion.4
  119.8 2.8 %collective-permute-start.12 = (bf16[16,3200]{1,0:T(8,128)(2,1)S(1)}, bf16[16,3200]{1,0:T(8,128)(2,1)S(1)}, u32[]{:S(2)}, u32[]{:S(2)}) collective-permute-start(bf16[16,3200]{1,0:T(8,128)(2,1)S(1)} %fusion.4), channel_id=1, source_target_pairs={{0,128},{8,136},{16,144},{24,152},{32,160},{40,168},{48,176},{56,1... | collective-permute-start | bytes 307208 | tf_op jit(solution)/shard_map/ppermute | solution.py:26
  122.6 1.4 %convolution_convert_fusion = bf16[512,1024]{1,0:T(8,128)(2,1)} fusion(bf16[16,512]{1,0:T(8,128)(2,1)S(1)} %get-tuple-element.54, bf16[1024,16]{0,1:T(8,128)(2,1)S(1)} %copy-done.14), kind=kOutput, calls=%fused_computation.1 | convolution fusion | flops 17301504 | bytes 1097728 | tf_op jit(solution)/shard_map/dot_general | solution.py:309
  124.0 2.0 %collective-permute-done.12 = bf16[16,3200]{1,0:T(8,128)(2,1)S(1)} collective-permute-done((bf16[16,3200]{1,0:T(8,128)(2,1)S(1)}, bf16[16,3200]{1,0:T(8,128)(2,1)S(1)}, u32[]{:S(2)}, u32[]{:S(2)}) %collective-permute-start.12) | collective-permute-done | bytes 102432 | tf_op jit(solution)/shard_map/ppermute | solution.py:26
  126.0 0.1 convert_add_fusion
  126.1 0.6 slice.170
  126.7 0.7 fusion.26
  (73 shorter events, 0.4 us)
Async XLA Ops:
  0.6 7.3 %copy-start = (bf16[16,1024]{1,0:T(8,128)(2,1)S(1)}, bf16[16,1024]{1,0:T(8,128)(2,1)}, u32[]{:S(2)}) copy-start(bf16[16,1024]{1,0:T(8,128)(2,1)} %param.24) | copy-start | bytes 98308
  0.6 7.3 %copy-start.1 = (bf16[512,1024]{1,0:T(8,128)(2,1)S(1)}, bf16[512,1024]{1,0:T(8,128)(2,1)}, u32[]{:S(2)}) copy-start(bf16[512,1024]{1,0:T(8,128)(2,1)} %dout_ref.1) | copy-start | bytes 3145732
  2.6 28.4 %collective-permute-start.2 = (bf16[1024,128]{1,0:T(8,128)(2,1)S(1)}, bf16[1024,128]{1,0:T(8,128)(2,1)}, u32[]{:S(2)}, u32[]{:S(2)}) collective-permute-start(bf16[1024,128]{1,0:T(8,128)(2,1)S(1)} %constant_dynamic-update-slice_fusion.kv3), channel_id=1, source_target_pairs={{0,8},{8,16},{16,24},{24,32},{32,40},{40,48},{48,56},{56,64},{64,7... | collective-permute-start | bytes 786440 | tf_op jit(solution)/shard_map/ppermute | solution.py:21
  2.7 28.3 %collective-permute-start.1 = (bf16[1024,128]{1,0:T(8,128)(2,1)S(1)}, bf16[1024,128]{1,0:T(8,128)(2,1)}, u32[]{:S(2)}, u32[]{:S(2)}) collective-permute-start(bf16[1024,128]{1,0:T(8,128)(2,1)S(1)} %constant_dynamic-update-slice_fusion.kv3), channel_id=1, source_target_pairs={{0,16},{8,24},{16,32},{24,40},{32,48},{40,56},{48,64},{56,72},{64,... | collective-permute-start | bytes 786440 | tf_op jit(solution)/shard_map/ppermute | solution.py:21
  4.3 26.8 %collective-permute-start = (bf16[1024,128]{1,0:T(8,128)(2,1)S(1)}, bf16[1024,128]{1,0:T(8,128)(2,1)}, u32[]{:S(2)}, u32[]{:S(2)}) collective-permute-start(bf16[1024,128]{1,0:T(8,128)(2,1)S(1)} %constant_dynamic-update-slice_fusion.kv3), channel_id=1, source_target_pairs={{0,24},{8,32},{16,40},{24,48},{32,56},{40,64},{48,72},{56,80},{64,... | collective-permute-start | bytes 786440 | tf_op jit(solution)/shard_map/ppermute | solution.py:21
  7.9 9.7 %copy-start.21 = (s32[64]{0:T(128)S(1)}, s32[64]{0:T(128)}, u32[]{:S(2)}) copy-start(s32[64]{0:T(128)} %param.25) | copy-start | bytes 772
  7.9 10.4 %copy-start.16 = (f32[512]{0:T(512)S(1)}, f32[512]{0:T(512)}, u32[]{:S(2)}) copy-start(f32[512]{0:T(512)} %param.27) | copy-start | bytes 6148
  8.0 10.6 %copy-start.12 = (bf16[16,128]{1,0:T(8,128)(2,1)S(1)}, bf16[16,128]{1,0:T(8,128)(2,1)}, u32[]{:S(2)}) copy-start(bf16[16,128]{1,0:T(8,128)(2,1)} %uv_ref.1) | copy-start | bytes 12292
  8.0 11.4 %copy-start.22 = (s32[64]{0:T(128)S(1)}, s32[64]{0:T(128)}, u32[]{:S(2)}) copy-start(s32[64]{0:T(128)} %param.26) | copy-start | bytes 772
  8.0 33.6 %copy-start.4 = (bf16[512,1024]{1,0:T(8,128)(2,1)S(1)}, bf16[512,1024]{1,0:T(8,128)(2,1)}, u32[]{:S(2)}) copy-start(bf16[512,1024]{1,0:T(8,128)(2,1)} %g_ref.1) | copy-start | bytes 3145732
  8.4 33.2 %copy-start.3 = (bf16[512,1024]{1,0:T(8,128)(2,1)S(1)}, bf16[512,1024]{1,0:T(8,128)(2,1)}, u32[]{:S(2)}) copy-start(bf16[512,1024]{1,0:T(8,128)(2,1)} %q_ref.1) | copy-start | bytes 3145732
  9.1 20.8 %all-to-all-start = ((bf16[8,32,512]{2,1,0:T(8,128)(2,1)}), bf16[8,32,512]{2,1,0:T(8,128)(2,1)}, u32[]{:S(2)}, u32[]{:S(2)}) async-start(bf16[8,32,512]{2,1,0:T(8,128)(2,1)} %broadcast_in_dim.82), calls=%async_computation | async-start | bytes 524288 | tf_op jit(solution)/shard_map/all_to_all | solution.py:40
  18.5 0.8 copy-start.19
  19.4 11.5 %copy-start.9 = (s32[8,512]{1,0:T(8,128)}, s32[8,512]{1,0:T(8,128)S(1)}, u32[]{:S(2)}) copy-start(s32[8,512]{1,0:T(8,128)S(1)} %scatter.9.start_ref) | copy-start | bytes 49156
  31.0 3.3 %collective-permute-start.3 = (bf16[24,512]{1,0:T(8,128)(2,1)S(1)}, bf16[24,512]{1,0:T(8,128)(2,1)S(1)}, u32[]{:S(2)}, u32[]{:S(2)}) collective-permute-start(bf16[24,512]{1,0:T(8,128)(2,1)S(1)} %fusion.11.lv_own), channel_id=1, source_target_pairs={{0,8},{8,16},{16,24},{24,32},{32,40},{40,48},{48,56},{56,64},{64,7... | collective-permute-start | bytes 73736 | tf_op jit(solution)/shard_map/ppermute | solution.py:21
  34.3 6.5 %collective-permute-start.4 = (bf16[24,1024]{1,0:T(8,128)(2,1)S(1)}, bf16[24,1024]{1,0:T(8,128)(2,1)S(1)}, u32[]{:S(2)}, u32[]{:S(2)}) collective-permute-start(bf16[24,1024]{1,0:T(8,128)(2,1)S(1)} %pad_maximum_fusion.1), channel_id=1, source_target_pairs={{0,16},{8,24},{16,32},{24,40},{32,48},{40,56},{48,64},{56,72},{64,... | collective-permute-start | bytes 147464 | tf_op jit(solution)/shard_map/ppermute | solution.py:21
  40.9 34.6 %collective-permute-start.7 = (f32[128]{0:T(128)S(1)}, f32[128]{0:T(128)S(1)}, u32[]{:S(2)}, u32[]{:S(2)}) collective-permute-start(f32[128]{0:T(128)S(1)} %fusion.24), channel_id=1, source_target_pairs={{0,0},{33,1},{66,2},{99,3},{132,4},{165,5},{198,6},{231,7},{8,8},{... | collective-permute-start | bytes 1544 | tf_op jit(solution)/shard_map/ppermute | solution.py:35
  41.6 0.8 copy-start.8
  42.3 0.7 copy-start.10
  43.1 0.8 copy-start.11
  43.8 0.7 copy-start.13
  44.5 32.6 %copy-start.20 = (bf16[128]{0:T(256)(128)(2,1)S(1)}, bf16[128]{0:T(256)(128)(2,1)}, u32[]{:S(2)}) copy-start(bf16[128]{0:T(256)(128)(2,1)} %copy-done.19) | copy-start | bytes 772
  69.2 0.8 copy-start.6
  70.0 14.5 %copy-start.17 = (s32[64,1]{0,1:T(1,128)S(1)}, s32[64,1]{0,1:T(1,128)}, u32[]{:S(2)}) copy-start(s32[64,1]{0,1:T(1,128)} %get-tuple-element.59) | copy-start | bytes 772
  70.0 14.5 %copy-start.18 = (s32[64,1]{0,1:T(1,128)S(1)}, s32[64,1]{0,1:T(1,128)}, u32[]{:S(2)}) copy-start(s32[64,1]{0,1:T(1,128)} %get-tuple-element.66) | copy-start | bytes 772
  70.0 14.6 %copy-start.23 = (s32[64]{0:T(128)S(1)}, s32[64]{0:T(128)}, u32[]{:S(2)}) copy-start(s32[64]{0:T(128)} %param.26) | copy-start | bytes 772
  70.0 14.6 %copy-start.15 = (f32[64]{0:T(128)S(1)}, f32[64]{0:T(128)}, u32[]{:S(2)}) copy-start(f32[64]{0:T(128)} %compare_select_fusion.1) | copy-start | bytes 772
  70.0 28.8 %copy-start.2 = (bf16[512,1024]{1,0:T(8,128)(2,1)S(1)}, bf16[512,1024]{1,0:T(8,128)(2,1)}, u32[]{:S(2)}) copy-start(bf16[512,1024]{1,0:T(8,128)(2,1)} %hidden_ref.1) | copy-start | bytes 3145732
  70.0 28.8 %copy-start.7 = (bf16[2048,128]{1,0:T(8,128)(2,1)S(1)}, bf16[2048,128]{1,0:T(8,128)(2,1)}, u32[]{:S(2)}) copy-start(bf16[2048,128]{1,0:T(8,128)(2,1)} %copy-done.6) | copy-start | bytes 1572868
  70.0 7.0 %collective-permute-start.5 = (bf16[16,1024]{1,0:T(8,128)(2,1)S(1)}, bf16[16,1024]{1,0:T(8,128)(2,1)S(1)}, u32[]{:S(2)}, u32[]{:S(2)}) collective-permute-start(bf16[16,1024]{1,0:T(8,128)(2,1)S(1)} %slice.126), channel_id=1, source_target_pairs={{0,240},{8,248},{16,0},{24,8},{32,16},{40,24},{48,32},{56,40},{64,... | collective-permute-start | bytes 98312 | tf_op jit(solution)/shard_map/ppermute | solution.py:21
  77.1 1.5 %collective-permute-start.6 = (bf16[16,512]{1,0:T(8,128)(2,1)S(1)}, bf16[16,512]{1,0:T(8,128)(2,1)S(1)}, u32[]{:S(2)}, u32[]{:S(2)}) collective-permute-start(bf16[16,512]{1,0:T(8,128)(2,1)S(1)} %fusion.7), channel_id=1, source_target_pairs={{0,248},{8,0},{16,8},{24,16},{32,24},{40,32},{48,40},{56,48},{64,5... | collective-permute-start | bytes 49160 | tf_op jit(solution)/shard_map/ppermute | solution.py:21
  79.4 19.4 %all-to-all-start.1 = ((bf16[8,40,512]{2,1,0:T(8,128)(2,1)}), bf16[8,40,512]{2,1,0:T(8,128)(2,1)S(1)}, u32[]{:S(2)}, u32[]{:S(2)}) async-start(bf16[8,40,512]{2,1,0:T(8,128)(2,1)} %broadcast_in_dim.87), calls=%async_computation.1 | async-start | bytes 655360 | tf_op jit(solution)/shard_map/all_to_all | solution.py:40
  98.8 1.2 copy-start.5
  101.9 1.6 %collective-permute-start.8 = (bf16[16,3200]{1,0:T(8,128)(2,1)S(1)}, bf16[16,3200]{1,0:T(8,128)(2,1)S(1)}, u32[]{:S(2)}, u32[]{:S(2)}) collective-permute-start(bf16[16,3200]{1,0:T(8,128)(2,1)S(1)} %fusion), channel_id=1, source_target_pairs={{0,8},{8,0},{16,24},{24,16},{32,40},{40,32},{48,56},{56,48},{64,72... | collective-permute-start | bytes 307208 | tf_op jit(solution)/shard_map/ppermute | solution.py:26
  103.5 5.0 %collective-permute-start.9 = (bf16[16,3200]{1,0:T(8,128)(2,1)S(1)}, bf16[16,3200]{1,0:T(8,128)(2,1)S(1)}, u32[]{:S(2)}, u32[]{:S(2)}) collective-permute-start(bf16[16,3200]{1,0:T(8,128)(2,1)S(1)} %fusion.1), channel_id=1, source_target_pairs={{0,16},{8,24},{16,0},{24,8},{32,48},{40,56},{48,32},{56,40},{64,80... | collective-permute-start | bytes 307208 | tf_op jit(solution)/shard_map/ppermute | solution.py:26
  108.6 14.0 %copy-start.14 = (bf16[1024,16]{0,1:T(8,128)(2,1)S(1)}, bf16[1024,16]{0,1:T(8,128)(2,1)}, u32[]{:S(2)}) copy-start(bf16[1024,16]{0,1:T(8,128)(2,1)} %param.21) | copy-start | bytes 98308
  108.6 6.3 %collective-permute-start.10 = (bf16[16,3200]{1,0:T(8,128)(2,1)S(1)}, bf16[16,3200]{1,0:T(8,128)(2,1)S(1)}, u32[]{:S(2)}, u32[]{:S(2)}) collective-permute-start(bf16[16,3200]{1,0:T(8,128)(2,1)S(1)} %fusion.25), channel_id=1, source_target_pairs={{0,32},{8,40},{16,48},{24,56},{32,0},{40,8},{48,16},{56,24},{64,96... | collective-permute-start | bytes 307208 | tf_op jit(solution)/shard_map/ppermute | solution.py:26
  114.9 4.7 %collective-permute-start.11 = (bf16[16,3200]{1,0:T(8,128)(2,1)S(1)}, bf16[16,3200]{1,0:T(8,128)(2,1)S(1)}, u32[]{:S(2)}, u32[]{:S(2)}) collective-permute-start(bf16[16,3200]{1,0:T(8,128)(2,1)S(1)} %fusion.2), channel_id=1, source_target_pairs={{0,64},{8,72},{16,80},{24,88},{32,96},{40,104},{48,112},{56,120},{... | collective-permute-start | bytes 307208 | tf_op jit(solution)/shard_map/ppermute | solution.py:26
  119.8 6.3 %collective-permute-start.12 = (bf16[16,3200]{1,0:T(8,128)(2,1)S(1)}, bf16[16,3200]{1,0:T(8,128)(2,1)S(1)}, u32[]{:S(2)}, u32[]{:S(2)}) collective-permute-start(bf16[16,3200]{1,0:T(8,128)(2,1)S(1)} %fusion.4), channel_id=1, source_target_pairs={{0,128},{8,136},{16,144},{24,152},{32,160},{40,168},{48,176},{56,1... | collective-permute-start | bytes 307208 | tf_op jit(solution)/shard_map/ppermute | solution.py:26

commit v3 on v2

v3 whole, which is shorter than its diff:
```python
import math

import jax
import jax.numpy as jnp
from jax import lax
from jax.experimental import pallas as pl
from jax.experimental.pallas import tpu as pltpu
from jax.sharding import PartitionSpec as P

HD = 128
BETA = 0.5
NEG = -1e30
F32 = jnp.float32
BF16 = jnp.bfloat16
KB = 256


def shift(value, by):
    n = lax.axis_size("ctx")
    return lax.ppermute(value, "ctx", [(i, (i + by) % n) for i in range(n)])


def flip(value, mask):
    n = lax.axis_size("ctx")
    return lax.ppermute(value, "ctx", [(i, i ^ mask) for i in range(n)])


def spread(part):
    n_ctx, n_tp = lax.axis_size("ctx"), lax.axis_size("tp")
    per = n_ctx // n_tp
    pairs = [
        ((c + per * j) % n_ctx * n_tp + j, c * n_tp + j) for c in range(n_ctx) for j in range(n_tp)
    ]
    return lax.ppermute(part, ("ctx", "tp"), pairs)


def share_tp(rows):
    n = lax.axis_size("tp")
    return lax.all_to_all(jnp.broadcast_to(rows[None], (n,) + rows.shape), "tp", 0, 0)


def nt(left, right):
    return lax.dot_general(left, right, (((1,), (1,)), ((), ())), preferred_element_type=F32)


def nn(left, right):
    return lax.dot_general(left, right, (((1,), (0,)), ((), ())), preferred_element_type=F32)


def tn(left, right):
    return lax.dot_general(left, right, (((0,), (0,)), ((), ())), preferred_element_type=F32)


def three_parts(x):
    high = x.astype(BF16)
    rest = x - high.astype(F32)
    mid = rest.astype(BF16)
    return high, mid, (rest - mid.astype(F32)).astype(BF16)


def iota(shape, dim):
    return lax.broadcasted_iota(jnp.int32, shape, dim)


def column(row, count):
    shape = (count, row.shape[1])
    return jnp.sum(jnp.where(iota(shape, 0) == iota(shape, 1), row, 0), axis=1, keepdims=True)


def doc_bounds(len_row):
    docs = len_row.shape[1]
    shape = (docs, docs)
    end = jnp.sum(jnp.where(iota(shape, 1) <= iota(shape, 0), len_row, 0), axis=1, keepdims=True)
    return end - column(len_row, docs), end


def in_hbm(*arrays):
    return [pltpu.with_memory_space_constraint(a, pltpu.HBM) for a in arrays]


def prep_kernel(
    first_ref, len_hbm, ratio_hbm, avt_hbm, up_hbm, key_hbm, frozen_hbm, hidden_hbm, dout_hbm,
    kv_ref, rank_ref, margin_ref, start_ref,
    len_ref, ratio_ref, avt_ref, up_ref, hidden_ref, dout_ref, sems,
):
    rows = key_hbm.shape[0]
    rank = up_ref.shape[0]
    pairs = [
        (len_hbm, len_ref), (ratio_hbm, ratio_ref), (avt_hbm, avt_ref), (up_hbm, up_ref),
        (hidden_hbm, hidden_ref), (dout_hbm, dout_ref),
        (key_hbm, kv_ref.at[0:rows]), (frozen_hbm, kv_ref.at[rows : 2 * rows]),
    ]
    copies = [pltpu.make_async_copy(src, dst, sems.at[i]) for i, (src, dst) in enumerate(pairs)]
    for copy in copies:
        copy.start()
    copies[0].wait()
    copies[1].wait()
    docs = len_ref.shape[1]
    first = first_ref[0]
    begin, end = doc_bounds(len_ref[...])
    pos = iota((1, rows), 1) + first
    own = (begin <= pos) & (pos < end)
    margin = jnp.sum(jnp.where(own, ratio_ref[...], 0.0), axis=1, keepdims=True)
    shape = (docs, 128)
    margin = jnp.sum(jnp.where(iota(shape, 0) == iota(shape, 1), margin, 0.0), axis=0, keepdims=True)
    margin = jnp.broadcast_to(margin, (8, 128))
    margin_ref[...] = jnp.zeros_like(margin_ref)
    for i, part in enumerate(three_parts(margin)):
        margin_ref[:, i * 128 : (i + 1) * 128] = part
    base = first - 3 * rows
    start = jnp.sum(jnp.where(own, begin, 0), axis=0, keepdims=True) - base
    start_ref[...] = jnp.where(iota(start_ref.shape, 0) == 0, start, pos - base)
    copies[2].wait()
    copies[4].wait()
    rank_ref[0:rank, :] = nt(hidden_ref[...], avt_ref[...]).T.astype(BF16)
    copies[3].wait()
    copies[5].wait()
    rank_ref[rank : 2 * rank, :] = nt(dout_ref[...], up_ref[...]).T.astype(BF16)
    copies[6].wait()
    copies[7].wait()


def prepare(first, doc_lengths, token_logratio, a_v_t, up, keys, frozen, hidden, d_out):
    rows = keys.shape[0]
    rank = up.shape[0]
    vmem = pl.BlockSpec(memory_space=pltpu.VMEM)
    return pl.pallas_call(
        prep_kernel,
        in_specs=[pl.BlockSpec(memory_space=pltpu.SMEM)] + [pl.BlockSpec(memory_space=pltpu.HBM)] * 8,
        out_specs=[vmem] * 4,
        out_shape=[
            jax.ShapeDtypeStruct((2 * rows, HD), BF16),
            jax.ShapeDtypeStruct((2 * rank, rows), BF16),
            jax.ShapeDtypeStruct((8, rows), BF16),
            jax.ShapeDtypeStruct((8, rows), jnp.int32),
        ],
        scratch_shapes=[
            pltpu.VMEM(a.shape, a.dtype)
            for a in (doc_lengths, token_logratio, a_v_t, up, hidden, d_out)
        ]
        + [pltpu.SemaphoreType.DMA((8,))],
        compiler_params=pltpu.CompilerParams(vmem_limit_bytes=32 * 2**20),
        name="prep",
    )(first, *in_hbm(doc_lengths, token_logratio, a_v_t, up, keys, frozen, hidden, d_out))


def margin_of(line):
    return line[:, 0:128] + line[:, 128:256] + line[:, 256:384]


def attn_kernel(
    low_ref, q_ref, g_ref, len_hbm, slot_hbm, aot_hbm, uv_hbm, start_hbm, rt_hbm, kv0, kv1, kv2, kv3, far_hbm, near_hbm, own_hbm,
    o_ref, lowo_ref, z_ref, vu_ref, od_ref, weight_ref,
    len_ref, slot_ref, aot_ref, uv_ref, start_ref, rt_ref, kv, lv_far, lv_near, lv_own, sems,
    bias0, bias1, vt, r_scr, q_all, s_scr, p_scr, ot_scr, grad_all, vg,
):
    rows = q_ref.shape[0]
    heads = q_ref.shape[1] // HD
    rank = uv_ref.shape[0]
    width = 4 * rows
    n_kb = width // KB
    scale = math.log2(math.e) / math.sqrt(HD)
    halves = rows // KB

    pairs = [
        (len_hbm, len_ref), (slot_hbm, slot_ref), (aot_hbm, aot_ref), (uv_hbm, uv_ref),
        (start_hbm, start_ref), (rt_hbm, rt_ref),
        (far_hbm, lv_far), (near_hbm, lv_near), (own_hbm, lv_own),
    ]
    pairs += [(ref, kv.at[slot]) for slot, ref in enumerate((kv0, kv1, kv2, kv3))]
    copies = [pltpu.make_async_copy(src, dst, sems.at[i]) for i, (src, dst) in enumerate(pairs)]
    for copy in copies:
        copy.start()
    vg[...] = jnp.zeros_like(vg)
    lowo_ref[...] = jnp.zeros_like(lowo_ref)
    for copy in copies:
        copy.wait()
    biases = (bias0, bias1)
    for half in range(halves):
        start = start_ref[0:1, half * KB : (half + 1) * KB]
        qpos = start_ref[1:2, half * KB : (half + 1) * KB]
        for kb in range(n_kb):
            kpos = iota((KB, KB), 0) + kb * KB
            ok = (kpos >= start) & (kpos <= qpos)
            biases[half][kb * KB : (kb + 1) * KB, :] = jnp.where(ok, 0.0, NEG)
    r_scr[...] = rt_ref[...].astype(F32).T.astype(BF16)
    uvt = uv_ref[...].astype(F32).T.astype(BF16)
    lows = (
        lv_far[0:rank, 0:rows], lv_far[0:rank, rows : 2 * rows], lv_near[0:rank, :], lv_own[0:rank, :],
    )
    lows = [low.astype(BF16) for low in lows]
    line = lv_far[rank : rank + 1, 0:rows] + lv_far[rank : rank + 1, rows : 2 * rows]
    margin = margin_of(line + lv_near[rank : rank + 1, :] + lv_own[rank : rank + 1, :])
    docs = len_ref.shape[1]
    slots = slot_ref[...]
    slot = column(slots, docs)
    sign = (1 - 2 * (slot & 1)).astype(F32)
    sign_row = (1 - 2 * (slots & 1)).astype(F32)
    pair = jnp.where((slot >> 1) == (slots >> 1), sign_row, 0.0)
    gap = jnp.sum(pair * margin[:, 0:docs], axis=1, keepdims=True)
    weight = -BETA * sign / (1.0 + jnp.exp(BETA * gap))
    begin, end = doc_bounds(len_ref[...])
    token = iota((docs, width), 1) + low_ref[halves]
    weight = jnp.sum(jnp.where((begin <= token) & (token < end), weight, 0.0), axis=0, keepdims=True)
    weight_ref[...] = jnp.broadcast_to(weight[:, 3 * rows :], weight_ref.shape)
    for slot in range(4):
        frozen = kv[slot, rows : 2 * rows, :].astype(F32).T
        v = (frozen + 2.0 * nn(uvt, lows[slot])).astype(BF16)
        for kb in range(halves):
            vt[slot * halves + kb] = v[:, kb * KB : (kb + 1) * KB]

    for half in range(halves):
        mine = slice(half * KB, (half + 1) * KB)
        first = low_ref[half]
        last = n_kb - halves + 1 + half
        lanes = [slice(h * KB, (h + 1) * KB) for h in range(heads)]
        for h in range(heads):
            q_all[h] = q_ref[mine, h * HD : (h + 1) * HD]

        def scores(kb, peaks):
            at = pl.ds(pl.multiple_of(kb * KB, KB), KB)
            key = kv[kb // halves, pl.ds(pl.multiple_of(kb % halves * KB, KB), KB), :]
            mask = biases[half][at, :]
            new = []
            for h in range(heads):
                s = nt(key, q_all[h]) * scale + mask
                s_scr[at, lanes[h]] = s
                new.append(jnp.maximum(peaks[h], jnp.max(s.reshape(KB // 8, 8, KB), axis=0)))
            return tuple(new)

        peaks = lax.fori_loop(first, last, scores, (jnp.full((8, KB), NEG, F32),) * heads)
        tops = [jnp.max(peak, axis=0, keepdims=True) for peak in peaks]
        ot_scr[...] = jnp.zeros_like(ot_scr)

        def probs(kb, totals):
            at = pl.ds(pl.multiple_of(kb * KB, KB), KB)
            new = []
            for h in range(heads):
                e = jnp.exp2(s_scr[at, lanes[h]] - tops[h])
                new.append(totals[h] + jnp.sum(e.reshape(KB // 8, 8, KB), axis=0))
                e = e.astype(BF16)
                p_scr[at, lanes[h]] = e
                ot_scr[:, lanes[h]] += nn(vt[kb], e)
            return tuple(new)

        totals = lax.fori_loop(first, last, probs, (jnp.zeros((8, KB), F32),) * heads)
        for h in range(heads):
            cols = slice(h * HD, (h + 1) * HD)
            inv = 1.0 / jnp.sum(totals[h], axis=0, keepdims=True)
            ot = (ot_scr[:, lanes[h]] * inv).astype(BF16)
            o_ref[mine, cols] = ot.astype(F32).T.astype(BF16)
            lowo_ref[:, mine] += nn(aot_ref[:, cols], ot)
            inv_rows = jnp.broadcast_to(inv, (HD, KB)).T
            grad = g_ref[mine, cols].astype(F32) + nn(r_scr[mine, :], aot_ref[:, cols])
            grad_all[lanes[h], :] = (grad * inv_rows).astype(BF16)

        def back(kb, carry):
            at = pl.ds(pl.multiple_of(kb * KB, KB), KB)
            vg[at, :] += nn(p_scr[at, :], grad_all[...])
            return carry

        lax.fori_loop(first, last, back, 0)

    total_vg = vg[...].astype(BF16)
    z_ref[...] = nt(uv_ref[...], total_vg).astype(BF16)
    up = jnp.zeros(vu_ref.shape, F32)
    for slot in range(4):
        part = slice(slot * rows, (slot + 1) * rows)
        up += nn((weight[:, part] * lows[slot].astype(F32)).astype(BF16), total_vg[part, :])
    vu_ref[...] = (2.0 * up).astype(BF16)
    weighted_r = (weight[:, 3 * rows :] * rt_ref[...].astype(F32)).astype(BF16)
    od_ref[...] = nn(weighted_r, o_ref[...]).astype(BF16)


def attention(base, start_q, queries, cotangent, doc_lengths, pair_slots, a_o_t, r_t, kvs, lows, u_v):
    rows = queries.shape[0]
    cols = queries.shape[1]
    rank = u_v.shape[0]
    heads = cols // HD
    halves = rows // KB
    low = jnp.stack([start_q[0, half * KB] for half in range(halves)]) // KB
    low = jnp.clip(low, 0, 3 * halves + jnp.arange(halves, dtype=jnp.int32))
    low = jnp.concatenate([low, base])
    vmem = pl.BlockSpec(memory_space=pltpu.VMEM)
    anywhere = pl.BlockSpec(memory_space=pl.ANY)
    hbm = pl.BlockSpec(memory_space=pltpu.HBM)
    args = (doc_lengths, pair_slots, a_o_t, u_v)
    made = (start_q, r_t)
    scratch = [pltpu.VMEM(a.shape, a.dtype) for a in args + made]
    scratch += [pltpu.VMEM((4, 2 * rows, HD), BF16)]
    scratch += [pltpu.VMEM(a.shape, a.dtype) for a in lows]
    return pl.pallas_call(
        attn_kernel,
        in_specs=[pl.BlockSpec(memory_space=pltpu.SMEM)] + [vmem] * 2 + [hbm] * 4 + [anywhere] * 9,
        out_specs=[vmem] * 6,
        out_shape=[
            jax.ShapeDtypeStruct((rows, cols), BF16),
            jax.ShapeDtypeStruct((rank, rows), F32),
            jax.ShapeDtypeStruct((rank, 4 * rows), BF16),
            jax.ShapeDtypeStruct((rank, HD), BF16),
            jax.ShapeDtypeStruct((rank, cols), BF16),
            jax.ShapeDtypeStruct((8, rows), F32),
        ],
        scratch_shapes=scratch
        + [
            pltpu.SemaphoreType.DMA((13,)),
            pltpu.VMEM((4 * rows, KB), F32),
            pltpu.VMEM((4 * rows, KB), F32),
            pltpu.VMEM((4 * halves, HD, KB), BF16),
            pltpu.VMEM((rows, rank), BF16),
            pltpu.VMEM((heads, KB, HD), BF16),
            pltpu.VMEM((4 * rows, heads * KB), F32),
            pltpu.VMEM((4 * rows, heads * KB), BF16),
            pltpu.VMEM((HD, heads * KB), F32),
            pltpu.VMEM((heads * KB, HD), BF16),
            pltpu.VMEM((4 * rows, HD), F32),
        ],
        compiler_params=pltpu.CompilerParams(vmem_limit_bytes=48 * 2**20),
        name="attn",
    )(low, queries, cotangent, *in_hbm(*args), *made, *kvs, *lows)


def grads_kernel(shared_ref, weight_ref, vu_ref, od_ref, hidden_ref, dout_ref, sum_ref, lowo_ref, lvg_ref):
    rank = vu_ref.shape[0]
    cols = hidden_ref.shape[1]
    sums = shared_ref[0].astype(F32)
    for j in range(1, shared_ref.shape[0]):
        sums = sums + shared_ref[j].astype(F32)
    own = weight_ref[0:1, :]
    lvg = (2.0 * own * sums[0:rank]).astype(BF16)
    low_o = sums[rank : 2 * rank].astype(BF16)
    lvg_ref[...] = lvg
    lowo_ref[...] = low_o
    sum_ref[:, 0:cols] = nn(lvg, hidden_ref[...]).astype(BF16)
    sum_ref[:, cols : 2 * cols] = od_ref[...]
    weighted = (own * low_o.astype(F32)).astype(BF16)
    sum_ref[:, 2 * cols : 3 * cols] = (2.0 * nn(weighted, dout_ref[...])).astype(BF16)
    sum_ref[:, 3 * cols :] = vu_ref[...]


def grads(shared, weight, vu, od, hidden, d_out):
    rank = vu.shape[0]
    rows, cols = hidden.shape
    vmem = pl.BlockSpec(memory_space=pltpu.VMEM)
    return pl.pallas_call(
        grads_kernel,
        in_specs=[vmem] * 6,
        out_specs=[vmem] * 3,
        out_shape=[
            jax.ShapeDtypeStruct((rank, 3 * cols + HD), BF16),
            jax.ShapeDtypeStruct((rank, rows), BF16),
            jax.ShapeDtypeStruct((rank, rows), BF16),
        ],
        compiler_params=pltpu.CompilerParams(vmem_limit_bytes=32 * 2**20),
        name="grads",
    )(shared, weight, vu, od, hidden, d_out)


def shards(
    hidden, queries, rotated_keys, frozen_value_rows, adapter_a_v, value_up_matrix, adapter_a_o,
    output_up_matrix, doc_lengths, pair_slots, token_logratio, out_cotangent, attn_cotangent,
):
    rows, cols = hidden.shape
    rank = value_up_matrix.shape[0]
    first = (lax.axis_index("ctx") * rows).astype(jnp.int32)[None]
    doc_lengths = doc_lengths[None, :]
    pair_slots = pair_slots[None, :]

    kv, rank_rows, margin, start_q = prepare(
        first, doc_lengths, token_logratio[None, :], adapter_a_v.T, output_up_matrix, rotated_keys,
        frozen_value_rows, hidden, out_cotangent,
    )
    kvs = [shift(kv, by) for by in (3, 2, 1)]
    sent = jnp.concatenate([rank_rows[:rank], spread(margin), rank_rows[rank:]], axis=0)
    shared = jnp.sum(share_tp(sent).astype(F32), axis=0)
    low_own = shared[: rank + 8]
    r_t = (2.0 * shared[rank + 8 :]).astype(BF16)
    low_own, kvs = lax.optimization_barrier((low_own, kvs))
    low_near = shift(low_own, 1)
    low_far = shift(jnp.concatenate([low_near, low_own], axis=1), 2)

    o, low_o_part, z, vu, od, weight = attention(
        first - 3 * rows, start_q, queries, attn_cotangent, doc_lengths, pair_slots, adapter_a_o.T, r_t,
        kvs + [kv], (low_far, low_near, low_own), value_up_matrix,
    )
    z_far = shift(z[:, : 2 * rows], -2).astype(F32)
    z_near = shift((z[:, 2 * rows : 3 * rows].astype(F32) + z_far[:, :rows]).astype(BF16), -1)
    z_own = z[:, 3 * rows :].astype(F32) + z_far[:, rows:] + z_near.astype(F32)
    shared_back = share_tp(jnp.concatenate([z_own, low_o_part], axis=0).astype(BF16))

    total, low_o_t, lvg_t = grads(shared_back, weight, vu, od, hidden, out_cotangent)
    total = total.astype(F32)
    for mask in (1, 2, 4, 8, 16):
        total = lax.reduce_precision(total, 8, 7)
        total = total + flip(total.astype(BF16), mask).astype(F32)
    term = (2.0 * tn(low_o_t, output_up_matrix)).astype(BF16)
    input_grad = lax.dot_general(
        lvg_t, adapter_a_v, (((0,), (1,)), ((), ())), preferred_element_type=F32
    ).astype(BF16)
    return (
        o,
        term,
        input_grad,
        total[:, :cols].T,
        total[:, 3 * cols :],
        total[:, cols : 2 * cols].T,
        total[:, 2 * cols : 3 * cols],
    )


def solution(mesh):
    both, tp_rows, tp_cols = P("ctx", "tp"), P("tp", None), P(None, "tp")
    in_specs = (
        both, both, both, both, tp_rows, tp_cols, tp_rows, tp_cols, P(), P(), P("ctx"), both, both,
    )
    out_specs = (both, both, both, tp_rows, tp_cols, tp_rows, tp_cols)
    return jax.shard_map(shards, mesh=mesh, in_specs=in_specs, out_specs=out_specs, check_vma=False)
```

time: 128 us -> 125 us (0.977)
  blocking collectives: 0 us -> 17.5 us
  Pallas kernels: 26.5 us -> 15.8 us
  local copies, waits for them, and re-layouts: 10.7 us -> 2.6 us
  starting transfers between devices: 32.3 us -> 38.2 us
  waiting for transfers between devices: 48.8 us -> 43.5 us
  matrix products: 4.83 us -> 2.86 us
    all_to_all x0 -> x1, blocking collectives: none -> 17.5 us  [share_tp(): lax.all_to_all(jnp.broadcast_to(rows[None], (n,) + rows.shape), 'tp', 0, 0)]
    all_to_all x2 -> x1, waiting for transfers between devices: 23.9 us -> 6.62 us  [share_tp(): lax.all_to_all(jnp.broadcast_to(rows[None], (n,) + rows.shape), 'tp', 0, 0)]
    pallas_call x2 -> x3, Pallas kernels: 26.5 us -> 15.8 us  [the longest x1 12.6 us: attention(): pl.pallas_call(attn_kernel, in_specs=[pl.BlockSpec(memory_space=pltpu.SME...]
    ppermute x7, waiting for transfers between devices: 11.9 us -> 19.4 us  [shift(): return lax.ppermute(value, 'ctx', [(i, (i + by) % n) for i in range(n)])]
    unnamed x50 -> x12, local copies, waits for them, and re-layouts: 6.76 us -> 0.03 us
    ppermute x5, starting transfers between devices: 7.97 us -> 12.6 us  [flip(): return lax.ppermute(value, 'ctx', [(i, i ^ mask) for i in range(n)])]
    ppermute x5, waiting for transfers between devices: 13 us -> 17.5 us  [flip(): return lax.ppermute(value, 'ctx', [(i, i ^ mask) for i in range(n)])]
    all_to_all x2 -> x1, starting transfers between devices: 13.5 us -> 16.8 us  [share_tp(): lax.all_to_all(jnp.broadcast_to(rows[None], (n,) + rows.shape), 'tp', 0, 0)]
  transfers between devices with their start and end apart: 15 -> 14, of which waited for: 11 -> 11; matrix products, arithmetic and copies ran while one was open for 7% -> 4% of each run, Pallas kernels for 19% -> 0%
where the time goes in v3:
time: 125 us; the launch traced here: 123 us
  waiting for transfers between devices  43.5 us (35%)
  starting transfers between devices  38.2 us (31%)
  blocking collectives  17.5 us (14%)
  Pallas kernels  15.8 us (13%)
  matrix products  2.86 us (2%)
  local copies, waits for them, and re-layouts  2.6 us (2%)
  other arithmetic  1.91 us (2%)
    ppermute x7, waiting for transfers between devices, shift(): return lax.ppermute(value, 'ctx', [(i, (i + by) % n) for i in range(n)])  19.4 us
    all_to_all x1, blocking collectives, share_tp(): lax.all_to_all(jnp.broadcast_to(rows[None], (n,) + rows.shape), 'tp', 0, 0)  17.5 us
    ppermute x5, waiting for transfers between devices, flip(): return lax.ppermute(value, 'ctx', [(i, i ^ mask) for i in range(n)])  17.5 us
    all_to_all x1, starting transfers between devices, share_tp(): lax.all_to_all(jnp.broadcast_to(rows[None], (n,) + rows.shape), 'tp', 0, 0)  16.8 us
    pallas_call x1, Pallas kernels, attention(): pl.pallas_call(attn_kernel, in_specs=[pl.BlockSpec(memory_space=pltpu.SME...  12.6 us
    ppermute x5, starting transfers between devices, flip(): return lax.ppermute(value, 'ctx', [(i, i ^ mask) for i in range(n)])  12.6 us
    ppermute x7, starting transfers between devices, shift(): return lax.ppermute(value, 'ctx', [(i, (i + by) % n) for i in range(n)])  8.08 us
    all_to_all x1, waiting for transfers between devices, share_tp(): lax.all_to_all(jnp.broadcast_to(rows[None], (n,) + rows.shape), 'tp', 0, 0)  6.62 us
  transfers between devices with their start and end apart: 14, of which 11 were waited for; matrix products, arithmetic and copies ran while one was open for 4% of the time, Pallas kernels for 0%

profile of v3, /device:TPU:2, one launch (start us, length us, event | category | flops | bytes accessed | tf_op | source)
XLA Modules:
  0.0 123.3 jit_solution(3355756884293373368)
XLA Ops:
  0.6 0.0 copy-start.3
  0.6 2.9 %prep.1 = (bf16[1024,128]{1,0:T(8,128)(2,1)S(1)}, bf16[32,512]{1,0:T(8,128)(2,1)S(1)}, bf16[8,512]{1,0:T(8,128)(2,1)S(1)}, s32[8,512]{1,0:T(8,128)S(1)}) custom-call(s32[1]{0:T(128)} %bitcast.first_ref, s32[1,64]{1,0:T(1,128)} %bitcast.19, f32[1,512]{1,0:T(1,128)} %bitcast.18, bf16[16,1024]{1,0:T(8,128)(2,1)} %bitcast.16, bf16[16,1024]{1,0:T(8,128)(2,1)} %up_hbm.1, ...), custom_call_target="tpu_custom_call" | custom-call | tf_op jit(solution)/shard_map/prep/pallas_call | solution.py:127
  3.5 0.0 copy-start.2
  3.5 0.8 collective-permute-start
  4.4 0.0 collective-permute-done
  4.4 0.7 broadcast_in_dim.28
  5.1 16.8 %all-to-all-start = ((bf16[8,40,512]{2,1,0:T(8,128)(2,1)}), bf16[8,40,512]{2,1,0:T(8,128)(2,1)S(1)}, u32[]{:S(2)}, u32[]{:S(2)}) async-start(bf16[8,40,512]{2,1,0:T(8,128)(2,1)} %broadcast_in_dim.28), calls=%async_computation | async-start | bytes 655360 | tf_op jit(solution)/shard_map/all_to_all | solution.py:39
  21.9 0.0 collective-permute-start.3
  21.9 1.3 %collective-permute-start.2 = (bf16[1024,128]{1,0:T(8,128)(2,1)S(1)}, bf16[1024,128]{1,0:T(8,128)(2,1)S(1)}, u32[]{:S(2)}, u32[]{:S(2)}) collective-permute-start(bf16[1024,128]{1,0:T(8,128)(2,1)S(1)} %get-tuple-element.27.kv3), channel_id=1, source_target_pairs={{0,16},{8,24},{16,32},{24,40},{32,48},{40,56},{48,64},{56,72},{64,... | collective-permute-start | bytes 786440 | tf_op jit(solution)/shard_map/ppermute | solution.py:20
  23.2 2.3 %collective-permute-start.1 = (bf16[1024,128]{1,0:T(8,128)(2,1)S(1)}, bf16[1024,128]{1,0:T(8,128)(2,1)S(1)}, u32[]{:S(2)}, u32[]{:S(2)}) collective-permute-start(bf16[1024,128]{1,0:T(8,128)(2,1)S(1)} %get-tuple-element.27.kv3), channel_id=1, source_target_pairs={{0,24},{8,32},{16,40},{24,48},{32,56},{40,64},{48,72},{56,80},{64,... | collective-permute-start | bytes 786440 | tf_op jit(solution)/shard_map/ppermute | solution.py:20
  25.5 0.5 fusion.11
  26.0 1.4 %maximum_minimum_fusion = s32[2]{0:T(128)S(1)} fusion(s32[1]{0:T(128)} %bitcast.5, s32[1]{0:T(128)} %bitcast.4), kind=kLoop, calls=%fused_computation.31 | loop fusion | flops 38 | bytes 16 | tf_op jit(solution)/shard_map/jit(clip)/min | solution.py:282
  27.4 6.6 %all-to-all-done = bf16[8,40,512]{2,1,0:T(8,128)(2,1)S(1)} async-done(((bf16[8,40,512]{2,1,0:T(8,128)(2,1)}), bf16[8,40,512]{2,1,0:T(8,128)(2,1)S(1)}, u32[]{:S(2)}, u32[]{:S(2)}) %all-to-all-start) | async-done | bytes 327712 | tf_op jit(solution)/shard_map/all_to_all | solution.py:39
  34.1 0.0 collective-permute-done.3.kv2
  34.1 0.0 collective-permute-done.2.kv1
  34.1 0.9 collective-permute-done.1.kv0
  35.0 1.5 %collective-permute-start.4 = (f32[24,512]{1,0:T(8,128)S(1)}, f32[24,512]{1,0:T(8,128)S(1)}, u32[]{:S(2)}, u32[]{:S(2)}) collective-permute-start(f32[24,512]{1,0:T(8,128)S(1)} %slice.61.own_hbm), channel_id=1, source_target_pairs={{0,8},{8,16},{16,24},{24,32},{32,40},{40,48},{48,56},{56,64},{64,7... | collective-permute-start | bytes 147464 | tf_op jit(solution)/shard_map/ppermute | solution.py:20
  36.6 0.1 pad_add_fusion.1.low_ref
  36.6 7.5 %collective-permute-done.4.near_hbm = f32[24,512]{1,0:T(8,128)S(1)} collective-permute-done((f32[24,512]{1,0:T(8,128)S(1)}, f32[24,512]{1,0:T(8,128)S(1)}, u32[]{:S(2)}, u32[]{:S(2)}) %collective-permute-start.4) | collective-permute-done | bytes 49184 | tf_op jit(solution)/shard_map/ppermute | solution.py:20
  44.2 0.1 collective-permute-start.5
  44.3 8.0 %collective-permute-done.5.far_hbm = f32[24,1024]{1,0:T(8,128)S(1)} collective-permute-done((f32[24,1024]{1,0:T(8,128)S(1)}, f32[24,1024]{1,0:T(8,128)S(1)}, u32[]{:S(2)}, u32[]{:S(2)}) %collective-permute-start.5) | collective-permute-done | bytes 98336 | tf_op jit(solution)/shard_map/ppermute | solution.py:20
  52.2 0.0 copy-done.3
  52.2 0.0 copy-done.2
  52.2 0.0 copy-start.1
  52.2 12.6 %attn.1 = (bf16[512,1024]{1,0:T(8,128)(2,1)}, f32[16,512]{1,0:T(8,128)S(1)}, bf16[16,2048]{1,0:T(8,128)(2,1)S(1)}, bf16[16,128]{1,0:T(8,128)(2,1)S(1)}, bf16[16,...) custom-call(s32[3]{0:T(128)S(1)} %pad_add_fusion.1.low_ref, bf16[512,1024]{1,0:T(8,128)(2,1)S(1)} %copy-done.2, ...), custom_call_target="tpu_custom_call" | custom-call | tf_op jit(solution)/shard_map/attn/pallas_call | solution.py:292
  64.8 0.0 copy-start
  64.8 2.6 %collective-permute-start.6 = (bf16[16,1024]{1,0:T(8,128)(2,1)S(1)}, bf16[16,1024]{1,0:T(8,128)(2,1)S(1)}, u32[]{:S(2)}, u32[]{:S(2)}) collective-permute-start(bf16[16,1024]{1,0:T(8,128)(2,1)S(1)} %slice.52), channel_id=1, source_target_pairs={{0,240},{8,248},{16,0},{24,8},{32,16},{40,24},{48,32},{56,40},{64,... | collective-permute-start | bytes 98312 | tf_op jit(solution)/shard_map/ppermute | solution.py:20
  67.4 1.6 %collective-permute-done.6 = bf16[16,1024]{1,0:T(8,128)(2,1)S(1)} collective-permute-done((bf16[16,1024]{1,0:T(8,128)(2,1)S(1)}, bf16[16,1024]{1,0:T(8,128)(2,1)S(1)}, u32[]{:S(2)}, u32[]{:S(2)}) %collective-permute-start.6) | collective-permute-done | bytes 32800 | tf_op jit(solution)/shard_map/ppermute | solution.py:20
  69.1 0.3 collective-permute-start.7
  69.3 1.4 %collective-permute-done.7 = bf16[16,512]{1,0:T(8,128)(2,1)S(1)} collective-permute-done((bf16[16,512]{1,0:T(8,128)(2,1)S(1)}, bf16[16,512]{1,0:T(8,128)(2,1)S(1)}, u32[]{:S(2)}, u32[]{:S(2)}) %collective-permute-start.7) | collective-permute-done | bytes 16416 | tf_op jit(solution)/shard_map/ppermute | solution.py:20
  70.8 17.5 %all_to_all.10.shared_ref = bf16[8,32,512]{2,1,0:T(8,128)(2,1)S(1)} all-to-all(bf16[8,32,512]{2,1,0:T(8,128)(2,1)S(1)} %broadcast_in_dim.29), channel_id=1, replica_groups=mesh['ctx'=32,'tp'=8] {'tp'}, dimensions={0} | all-to-all | bytes 524288 | tf_op jit(solution)/shard_map/all_to_all | solution.py:39
  88.3 0.0 copy-done.1
  88.3 0.0 copy-done
  88.3 0.4 grads.1
  88.7 0.0 copy-start.4
  88.7 5.7 %collective-permute-start.8 = (bf16[16,3200]{1,0:T(8,128)(2,1)S(1)}, bf16[16,3200]{1,0:T(8,128)(2,1)S(1)}, u32[]{:S(2)}, u32[]{:S(2)}) collective-permute-start(bf16[16,3200]{1,0:T(8,128)(2,1)S(1)} %fusion), channel_id=1, source_target_pairs={{0,8},{8,0},{16,24},{24,16},{32,40},{40,32},{48,56},{56,48},{64,72... | collective-permute-start | bytes 307208 | tf_op jit(solution)/shard_map/ppermute | solution.py:25
  94.4 0.9 collective-permute-done.8
  95.4 0.1 collective-permute-start.9
  95.5 5.1 %collective-permute-done.9 = bf16[16,3200]{1,0:T(8,128)(2,1)S(1)} collective-permute-done((bf16[16,3200]{1,0:T(8,128)(2,1)S(1)}, bf16[16,3200]{1,0:T(8,128)(2,1)S(1)}, u32[]{:S(2)}, u32[]{:S(2)}) %collective-permute-start.9) | collective-permute-done | bytes 102432 | tf_op jit(solution)/shard_map/ppermute | solution.py:25
  100.7 0.0 copy-start.5
  100.7 6.6 %collective-permute-start.10 = (bf16[16,3200]{1,0:T(8,128)(2,1)S(1)}, bf16[16,3200]{1,0:T(8,128)(2,1)S(1)}, u32[]{:S(2)}, u32[]{:S(2)}) collective-permute-start(bf16[16,3200]{1,0:T(8,128)(2,1)S(1)} %fusion.8), channel_id=1, source_target_pairs={{0,32},{8,40},{16,48},{24,56},{32,0},{40,8},{48,16},{56,24},{64,96... | collective-permute-start | bytes 307208 | tf_op jit(solution)/shard_map/ppermute | solution.py:25
  107.3 2.6 %collective-permute-done.10 = bf16[16,3200]{1,0:T(8,128)(2,1)S(1)} collective-permute-done((bf16[16,3200]{1,0:T(8,128)(2,1)S(1)}, bf16[16,3200]{1,0:T(8,128)(2,1)S(1)}, u32[]{:S(2)}, u32[]{:S(2)}) %collective-permute-start.10) | collective-permute-done | bytes 102432 | tf_op jit(solution)/shard_map/ppermute | solution.py:25
  109.9 0.1 fusion.2
  110.0 0.1 collective-permute-start.11
  110.1 0.0 copy-done.4
  110.1 1.4 %multiply_convert_fusion = bf16[512,1024]{1,0:T(8,128)(2,1)} fusion(bf16[16,512]{1,0:T(8,128)(2,1)S(1)} %get-tuple-element.38, bf16[16,1024]{1,0:T(8,128)(2,1)S(1)} %copy-done.4), kind=kOutput, calls=%fused_computation | convolution fusion | flops 17825792 | bytes 1097728 | tf_op jit(solution)/shard_map/dot_general | solution.py:51
  111.5 4.0 %collective-permute-done.11 = bf16[16,3200]{1,0:T(8,128)(2,1)S(1)} collective-permute-done((bf16[16,3200]{1,0:T(8,128)(2,1)S(1)}, bf16[16,3200]{1,0:T(8,128)(2,1)S(1)}, u32[]{:S(2)}, u32[]{:S(2)}) %collective-permute-start.11) | collective-permute-done | bytes 102432 | tf_op jit(solution)/shard_map/ppermute | solution.py:25
  115.6 0.1 fusion.3
  115.7 0.1 collective-permute-start.12
  115.8 0.0 copy-done.5
  115.8 1.4 %convolution_convert_fusion = bf16[512,1024]{1,0:T(8,128)(2,1)} fusion(bf16[16,512]{1,0:T(8,128)(2,1)S(1)} %get-tuple-element.39, bf16[1024,16]{0,1:T(8,128)(2,1)S(1)} %copy-done.5), kind=kOutput, calls=%fused_computation.1 | convolution fusion | flops 17301504 | bytes 1097728 | tf_op jit(solution)/shard_map/dot_general | solution.py:397
  117.2 4.7 %collective-permute-done.12 = bf16[16,3200]{1,0:T(8,128)(2,1)S(1)} collective-permute-done((bf16[16,3200]{1,0:T(8,128)(2,1)S(1)}, bf16[16,3200]{1,0:T(8,128)(2,1)S(1)}, u32[]{:S(2)}, u32[]{:S(2)}) %collective-permute-start.12) | collective-permute-done | bytes 102432 | tf_op jit(solution)/shard_map/ppermute | solution.py:25
  121.9 0.1 convert_add_fusion
  122.0 0.6 slice.65
  122.6 0.7 fusion.9
  (16 shorter events, 0.2 us)
Async XLA Ops:
  0.6 51.6 %copy-start.3 = (bf16[512,1024]{1,0:T(8,128)(2,1)S(1)}, bf16[512,1024]{1,0:T(8,128)(2,1)}, u32[]{:S(2)}) copy-start(bf16[512,1024]{1,0:T(8,128)(2,1)} %g_ref.1) | copy-start | bytes 3145732
  3.5 48.7 %copy-start.2 = (bf16[512,1024]{1,0:T(8,128)(2,1)S(1)}, bf16[512,1024]{1,0:T(8,128)(2,1)}, u32[]{:S(2)}) copy-start(bf16[512,1024]{1,0:T(8,128)(2,1)} %q_ref.1) | copy-start | bytes 3145732
  3.5 0.8 collective-permute-start
  5.1 28.9 %all-to-all-start = ((bf16[8,40,512]{2,1,0:T(8,128)(2,1)}), bf16[8,40,512]{2,1,0:T(8,128)(2,1)S(1)}, u32[]{:S(2)}, u32[]{:S(2)}) async-start(bf16[8,40,512]{2,1,0:T(8,128)(2,1)} %broadcast_in_dim.28), calls=%async_computation | async-start | bytes 655360 | tf_op jit(solution)/shard_map/all_to_all | solution.py:39
  21.9 12.2 %collective-permute-start.3 = (bf16[1024,128]{1,0:T(8,128)(2,1)S(1)}, bf16[1024,128]{1,0:T(8,128)(2,1)S(1)}, u32[]{:S(2)}, u32[]{:S(2)}) collective-permute-start(bf16[1024,128]{1,0:T(8,128)(2,1)S(1)} %get-tuple-element.27.kv3), channel_id=1, source_target_pairs={{0,8},{8,16},{16,24},{24,32},{32,40},{40,48},{48,56},{56,64},{64,7... | collective-permute-start | bytes 786440 | tf_op jit(solution)/shard_map/ppermute | solution.py:20
  21.9 12.2 %collective-permute-start.2 = (bf16[1024,128]{1,0:T(8,128)(2,1)S(1)}, bf16[1024,128]{1,0:T(8,128)(2,1)S(1)}, u32[]{:S(2)}, u32[]{:S(2)}) collective-permute-start(bf16[1024,128]{1,0:T(8,128)(2,1)S(1)} %get-tuple-element.27.kv3), channel_id=1, source_target_pairs={{0,16},{8,24},{16,32},{24,40},{32,48},{40,56},{48,64},{56,72},{64,... | collective-permute-start | bytes 786440 | tf_op jit(solution)/shard_map/ppermute | solution.py:20
  23.2 11.9 %collective-permute-start.1 = (bf16[1024,128]{1,0:T(8,128)(2,1)S(1)}, bf16[1024,128]{1,0:T(8,128)(2,1)S(1)}, u32[]{:S(2)}, u32[]{:S(2)}) collective-permute-start(bf16[1024,128]{1,0:T(8,128)(2,1)S(1)} %get-tuple-element.27.kv3), channel_id=1, source_target_pairs={{0,24},{8,32},{16,40},{24,48},{32,56},{40,64},{48,72},{56,80},{64,... | collective-permute-start | bytes 786440 | tf_op jit(solution)/shard_map/ppermute | solution.py:20
  35.0 9.1 %collective-permute-start.4 = (f32[24,512]{1,0:T(8,128)S(1)}, f32[24,512]{1,0:T(8,128)S(1)}, u32[]{:S(2)}, u32[]{:S(2)}) collective-permute-start(f32[24,512]{1,0:T(8,128)S(1)} %slice.61.own_hbm), channel_id=1, source_target_pairs={{0,8},{8,16},{16,24},{24,32},{32,40},{40,48},{48,56},{56,64},{64,7... | collective-permute-start | bytes 147464 | tf_op jit(solution)/shard_map/ppermute | solution.py:20
  44.2 8.1 %collective-permute-start.5 = (f32[24,1024]{1,0:T(8,128)S(1)}, f32[24,1024]{1,0:T(8,128)S(1)}, u32[]{:S(2)}, u32[]{:S(2)}) collective-permute-start(f32[24,1024]{1,0:T(8,128)S(1)} %pad_maximum_fusion), channel_id=1, source_target_pairs={{0,16},{8,24},{16,32},{24,40},{32,48},{40,56},{48,64},{56,72},{64,... | collective-permute-start | bytes 294920 | tf_op jit(solution)/shard_map/ppermute | solution.py:20
  52.2 36.1 %copy-start.1 = (bf16[512,1024]{1,0:T(8,128)(2,1)S(1)}, bf16[512,1024]{1,0:T(8,128)(2,1)}, u32[]{:S(2)}) copy-start(bf16[512,1024]{1,0:T(8,128)(2,1)} %dout_ref.1) | copy-start | bytes 3145732
  64.8 23.5 %copy-start = (bf16[512,1024]{1,0:T(8,128)(2,1)S(1)}, bf16[512,1024]{1,0:T(8,128)(2,1)}, u32[]{:S(2)}) copy-start(bf16[512,1024]{1,0:T(8,128)(2,1)} %hidden_ref.1) | copy-start | bytes 3145732
  64.8 4.2 %collective-permute-start.6 = (bf16[16,1024]{1,0:T(8,128)(2,1)S(1)}, bf16[16,1024]{1,0:T(8,128)(2,1)S(1)}, u32[]{:S(2)}, u32[]{:S(2)}) collective-permute-start(bf16[16,1024]{1,0:T(8,128)(2,1)S(1)} %slice.52), channel_id=1, source_target_pairs={{0,240},{8,248},{16,0},{24,8},{32,16},{40,24},{48,32},{56,40},{64,... | collective-permute-start | bytes 98312 | tf_op jit(solution)/shard_map/ppermute | solution.py:20
  69.1 1.7 %collective-permute-start.7 = (bf16[16,512]{1,0:T(8,128)(2,1)S(1)}, bf16[16,512]{1,0:T(8,128)(2,1)S(1)}, u32[]{:S(2)}, u32[]{:S(2)}) collective-permute-start(bf16[16,512]{1,0:T(8,128)(2,1)S(1)} %fusion.4), channel_id=1, source_target_pairs={{0,248},{8,0},{16,8},{24,16},{32,24},{40,32},{48,40},{56,48},{64,5... | collective-permute-start | bytes 49160 | tf_op jit(solution)/shard_map/ppermute | solution.py:20
  88.7 21.4 %copy-start.4 = (bf16[16,1024]{1,0:T(8,128)(2,1)S(1)}, bf16[16,1024]{1,0:T(8,128)(2,1)}, u32[]{:S(2)}) copy-start(bf16[16,1024]{1,0:T(8,128)(2,1)} %up_hbm.1) | copy-start | bytes 98308
  88.7 6.6 %collective-permute-start.8 = (bf16[16,3200]{1,0:T(8,128)(2,1)S(1)}, bf16[16,3200]{1,0:T(8,128)(2,1)S(1)}, u32[]{:S(2)}, u32[]{:S(2)}) collective-permute-start(bf16[16,3200]{1,0:T(8,128)(2,1)S(1)} %fusion), channel_id=1, source_target_pairs={{0,8},{8,0},{16,24},{24,16},{32,40},{40,32},{48,56},{56,48},{64,72... | collective-permute-start | bytes 307208 | tf_op jit(solution)/shard_map/ppermute | solution.py:25
  95.4 5.2 %collective-permute-start.9 = (bf16[16,3200]{1,0:T(8,128)(2,1)S(1)}, bf16[16,3200]{1,0:T(8,128)(2,1)S(1)}, u32[]{:S(2)}, u32[]{:S(2)}) collective-permute-start(bf16[16,3200]{1,0:T(8,128)(2,1)S(1)} %fusion.1), channel_id=1, source_target_pairs={{0,16},{8,24},{16,0},{24,8},{32,48},{40,56},{48,32},{56,40},{64,80... | collective-permute-start | bytes 307208 | tf_op jit(solution)/shard_map/ppermute | solution.py:25
  100.7 15.1 %copy-start.5 = (bf16[1024,16]{0,1:T(8,128)(2,1)S(1)}, bf16[1024,16]{0,1:T(8,128)(2,1)}, u32[]{:S(2)}) copy-start(bf16[1024,16]{0,1:T(8,128)(2,1)} %param.17) | copy-start | bytes 98308
  100.7 9.2 %collective-permute-start.10 = (bf16[16,3200]{1,0:T(8,128)(2,1)S(1)}, bf16[16,3200]{1,0:T(8,128)(2,1)S(1)}, u32[]{:S(2)}, u32[]{:S(2)}) collective-permute-start(bf16[16,3200]{1,0:T(8,128)(2,1)S(1)} %fusion.8), channel_id=1, source_target_pairs={{0,32},{8,40},{16,48},{24,56},{32,0},{40,8},{48,16},{56,24},{64,96... | collective-permute-start | bytes 307208 | tf_op jit(solution)/shard_map/ppermute | solution.py:25
  110.0 5.6 %collective-permute-start.11 = (bf16[16,3200]{1,0:T(8,128)(2,1)S(1)}, bf16[16,3200]{1,0:T(8,128)(2,1)S(1)}, u32[]{:S(2)}, u32[]{:S(2)}) collective-permute-start(bf16[16,3200]{1,0:T(8,128)(2,1)S(1)} %fusion.2), channel_id=1, source_target_pairs={{0,64},{8,72},{16,80},{24,88},{32,96},{40,104},{48,112},{56,120},{... | collective-permute-start | bytes 307208 | tf_op jit(solution)/shard_map/ppermute | solution.py:25
  115.7 6.3 %collective-permute-start.12 = (bf16[16,3200]{1,0:T(8,128)(2,1)S(1)}, bf16[16,3200]{1,0:T(8,128)(2,1)S(1)}, u32[]{:S(2)}, u32[]{:S(2)}) collective-permute-start(bf16[16,3200]{1,0:T(8,128)(2,1)S(1)} %fusion.3), channel_id=1, source_target_pairs={{0,128},{8,136},{16,144},{24,152},{32,160},{40,168},{48,176},{56,1... | collective-permute-start | bytes 307208 | tf_op jit(solution)/shard_map/ppermute | solution.py:25

commit v4 on v3

--- a/solution.py
+++ b/solution.py
@@ -80,7 +80,7 @@
 
 def prep_kernel(
     first_ref, len_hbm, ratio_hbm, avt_hbm, up_hbm, key_hbm, frozen_hbm, hidden_hbm, dout_hbm,
-    kv_ref, rank_ref, margin_ref, start_ref,
+    kv_ref, rank_ref, margin_ref, start_ref, low_ref,
     len_ref, ratio_ref, avt_ref, up_ref, hidden_ref, dout_ref, sems,
 ):
     rows = key_hbm.shape[0]
@@ -110,6 +110,11 @@
     base = first - 3 * rows
     start = jnp.sum(jnp.where(own, begin, 0), axis=0, keepdims=True) - base
     start_ref[...] = jnp.where(iota(start_ref.shape, 0) == 0, start, pos - base)
+    halves = rows // KB
+    for half in range(halves):
+        head = jnp.max(start[:, half * KB : half * KB + 1].astype(F32)).astype(jnp.int32)
+        low_ref[half] = jnp.clip(head // KB, 0, 3 * halves + half)
+    low_ref[halves] = base
     copies[2].wait()
     copies[4].wait()
     rank_ref[0:rank, :] = nt(hidden_ref[...], avt_ref[...]).T.astype(BF16)
@@ -127,12 +132,13 @@
     return pl.pallas_call(
         prep_kernel,
         in_specs=[pl.BlockSpec(memory_space=pltpu.SMEM)] + [pl.BlockSpec(memory_space=pltpu.HBM)] * 8,
-        out_specs=[vmem] * 4,
+        out_specs=[vmem] * 4 + [pl.BlockSpec(memory_space=pltpu.SMEM)],
         out_shape=[
             jax.ShapeDtypeStruct((2 * rows, HD), BF16),
             jax.ShapeDtypeStruct((2 * rank, rows), BF16),
             jax.ShapeDtypeStruct((8, rows), BF16),
             jax.ShapeDtypeStruct((8, rows), jnp.int32),
+            jax.ShapeDtypeStruct((rows // KB + 1,), jnp.int32),
         ],
         scratch_shapes=[
             pltpu.VMEM(a.shape, a.dtype)
@@ -149,7 +155,7 @@
 
 
 def attn_kernel(
-    low_ref, q_ref, g_ref, len_hbm, slot_hbm, aot_hbm, uv_hbm, start_hbm, rt_hbm, kv0, kv1, kv2, kv3, far_hbm, near_hbm, own_hbm,
+    low_ref, q_ref, g_ref, len_hbm, slot_hbm, aot_hbm, uv_hbm, start_hbm, rt_hbm, kv_far, kv_near, kv_own, far_hbm, near_hbm, own_hbm,
     o_ref, lowo_ref, z_ref, vu_ref, od_ref, weight_ref,
     len_ref, slot_ref, aot_ref, uv_ref, start_ref, rt_ref, kv, lv_far, lv_near, lv_own, sems,
     bias0, bias1, vt, r_scr, q_all, s_scr, p_scr, ot_scr, grad_all, vg,
@@ -167,7 +173,7 @@
         (start_hbm, start_ref), (rt_hbm, rt_ref),
         (far_hbm, lv_far), (near_hbm, lv_near), (own_hbm, lv_own),
     ]
-    pairs += [(ref, kv.at[slot]) for slot, ref in enumerate((kv0, kv1, kv2, kv3))]
+    pairs += [(kv_far, kv.at[0:2]), (kv_near, kv.at[2]), (kv_own, kv.at[3])]
     copies = [pltpu.make_async_copy(src, dst, sems.at[i]) for i, (src, dst) in enumerate(pairs)]
     for copy in copies:
         copy.start()
@@ -272,15 +278,12 @@
     od_ref[...] = nn(weighted_r, o_ref[...]).astype(BF16)
 
 
-def attention(base, start_q, queries, cotangent, doc_lengths, pair_slots, a_o_t, r_t, kvs, lows, u_v):
+def attention(low, start_q, queries, cotangent, doc_lengths, pair_slots, a_o_t, r_t, kvs, lows, u_v):
     rows = queries.shape[0]
     cols = queries.shape[1]
     rank = u_v.shape[0]
     heads = cols // HD
     halves = rows // KB
-    low = jnp.stack([start_q[0, half * KB] for half in range(halves)]) // KB
-    low = jnp.clip(low, 0, 3 * halves + jnp.arange(halves, dtype=jnp.int32))
-    low = jnp.concatenate([low, base])
     vmem = pl.BlockSpec(memory_space=pltpu.VMEM)
     anywhere = pl.BlockSpec(memory_space=pl.ANY)
     hbm = pl.BlockSpec(memory_space=pltpu.HBM)
@@ -291,7 +294,7 @@
     scratch += [pltpu.VMEM(a.shape, a.dtype) for a in lows]
     return pl.pallas_call(
         attn_kernel,
-        in_specs=[pl.BlockSpec(memory_space=pltpu.SMEM)] + [vmem] * 2 + [hbm] * 4 + [anywhere] * 9,
+        in_specs=[pl.BlockSpec(memory_space=pltpu.SMEM)] + [vmem] * 2 + [hbm] * 4 + [anywhere] * 8,
         out_specs=[vmem] * 6,
         out_shape=[
             jax.ShapeDtypeStruct((rows, cols), BF16),
@@ -303,7 +306,7 @@
         ],
         scratch_shapes=scratch
         + [
-            pltpu.SemaphoreType.DMA((13,)),
+            pltpu.SemaphoreType.DMA((12,)),
             pltpu.VMEM((4 * rows, KB), F32),
             pltpu.VMEM((4 * rows, KB), F32),
             pltpu.VMEM((4 * halves, HD, KB), BF16),
@@ -366,22 +369,23 @@
     doc_lengths = doc_lengths[None, :]
     pair_slots = pair_slots[None, :]
 
-    kv, rank_rows, margin, start_q = prepare(
+    kv, rank_rows, margin, start_q, low = prepare(
         first, doc_lengths, token_logratio[None, :], adapter_a_v.T, output_up_matrix, rotated_keys,
         frozen_value_rows, hidden, out_cotangent,
     )
-    kvs = [shift(kv, by) for by in (3, 2, 1)]
-    sent = jnp.concatenate([rank_rows[:rank], spread(margin), rank_rows[rank:]], axis=0)
+    kv_near = shift(kv, 1)
+    margin, kv_near = lax.optimization_barrier((spread(margin), kv_near))
+    kv_far = shift(jnp.stack([kv_near, kv]), 2)
+    sent = jnp.concatenate([rank_rows[:rank], margin, rank_rows[rank:]], axis=0)
     shared = jnp.sum(share_tp(sent).astype(F32), axis=0)
     low_own = shared[: rank + 8]
     r_t = (2.0 * shared[rank + 8 :]).astype(BF16)
-    low_own, kvs = lax.optimization_barrier((low_own, kvs))
     low_near = shift(low_own, 1)
     low_far = shift(jnp.concatenate([low_near, low_own], axis=1), 2)
 
     o, low_o_part, z, vu, od, weight = attention(
-        first - 3 * rows, start_q, queries, attn_cotangent, doc_lengths, pair_slots, adapter_a_o.T, r_t,
-        kvs + [kv], (low_far, low_near, low_own), value_up_matrix,
+        low, start_q, queries, attn_cotangent, doc_lengths, pair_slots, adapter_a_o.T, r_t,
+        (kv_far, kv_near, kv), (low_far, low_near, low_own), value_up_matrix,
     )
     z_far = shift(z[:, : 2 * rows], -2).astype(F32)
     z_near = shift((z[:, 2 * rows : 3 * rows].astype(F32) + z_far[:, :rows]).astype(BF16), -1)

time: 125 us -> 116 us (0.928); the launches traced: 123 us -> 117 us
  starting transfers between devices: 38.2 us -> 16.3 us
  Pallas kernels: 15.8 us -> 24.8 us
  waiting for transfers between devices: 43.5 us -> 52.3 us
    ppermute x5, starting transfers between devices: 12.6 us -> 1.29 us  [flip(): return lax.ppermute(value, 'ctx', [(i, i ^ mask) for i in range(n)])]
    pallas_call x1, Pallas kernels: 12.6 us -> 21 us  [attention(): pl.pallas_call(attn_kernel, in_specs=[pl.BlockSpec(memory_space=pltpu.SME...]
    ppermute x7 -> x6, starting transfers between devices: 8.08 us -> 2.53 us  [shift(): return lax.ppermute(value, 'ctx', [(i, (i + by) % n) for i in range(n)])]
    all_to_all x1, waiting for transfers between devices: 6.62 us -> 11.8 us  [share_tp(): lax.all_to_all(jnp.broadcast_to(rows[None], (n,) + rows.shape), 'tp', 0, 0)]
    all_to_all x1, starting transfers between devices: 16.8 us -> 11.8 us  [share_tp(): lax.all_to_all(jnp.broadcast_to(rows[None], (n,) + rows.shape), 'tp', 0, 0)]
    ppermute x5, waiting for transfers between devices: 17.5 us -> 20.3 us  [flip(): return lax.ppermute(value, 'ctx', [(i, i ^ mask) for i in range(n)])]
    min x1 -> x0, other arithmetic: 1.37 us -> none  [attention(): low = jnp.clip(low, 0, 3 * halves + jnp.arange(halves, dtype=jnp.int32))]
    ppermute x7 -> x6, waiting for transfers between devices: 19.4 us -> 20.2 us  [shift(): return lax.ppermute(value, 'ctx', [(i, (i + by) % n) for i in range(n)])]
  transfers between devices with their start and end apart: 14 -> 13, of which waited for: 11 -> 11; matrix products, arithmetic and copies ran while one was open for 4% -> 3% of each run, Pallas kernels for 0% -> 0%
where the time goes in v4:
time: 116 us; the launch traced here: 117 us
  waiting for transfers between devices  52.3 us (45%)
  Pallas kernels  24.8 us (21%)
  blocking collectives  16.6 us (14%)
  starting transfers between devices  16.3 us (14%)
  matrix products  2.85 us (2%)
  local copies, waits for them, and re-layouts  2.09 us (2%)
  other arithmetic  1.3 us (1%)
    pallas_call x1, Pallas kernels, attention(): pl.pallas_call(attn_kernel, in_specs=[pl.BlockSpec(memory_space=pltpu.SME...  21 us
    ppermute x5, waiting for transfers between devices, flip(): return lax.ppermute(value, 'ctx', [(i, i ^ mask) for i in range(n)])  20.3 us
    ppermute x6, waiting for transfers between devices, shift(): return lax.ppermute(value, 'ctx', [(i, (i + by) % n) for i in range(n)])  20.2 us
    all_to_all x1, blocking collectives, share_tp(): lax.all_to_all(jnp.broadcast_to(rows[None], (n,) + rows.shape), 'tp', 0, 0)  16.6 us
    all_to_all x1, waiting for transfers between devices, share_tp(): lax.all_to_all(jnp.broadcast_to(rows[None], (n,) + rows.shape), 'tp', 0, 0)  11.8 us
    all_to_all x1, starting transfers between devices, share_tp(): lax.all_to_all(jnp.broadcast_to(rows[None], (n,) + rows.shape), 'tp', 0, 0)  11.8 us
    pallas_call x1, Pallas kernels, prepare(): pl.pallas_call(prep_kernel, in_specs=[pl.BlockSpec(memory_space=pltpu.SME...  3.38 us
    ppermute x6, starting transfers between devices, shift(): return lax.ppermute(value, 'ctx', [(i, (i + by) % n) for i in range(n)])  2.53 us
  transfers between devices with their start and end apart: 13, of which 11 were waited for; matrix products, arithmetic and copies ran while one was open for 3% of the time, Pallas kernels for 0%

profile of v4, /device:TPU:2, one launch (start us, length us, event | category | flops | bytes accessed | tf_op | source)
XLA Modules:
  0.0 117.1 jit_solution(6906209372523155578)
XLA Ops:
  0.6 3.4 %prep.1 = (bf16[1024,128]{1,0:T(8,128)(2,1)S(1)}, bf16[32,512]{1,0:T(8,128)(2,1)S(1)}, bf16[8,512]{1,0:T(8,128)(2,1)S(1)}, s32[8,512]{1,0:T(8,128)S(1)}, s32[3]{0:T(128)S(1)}) custom-call(s32[1]{0:T(128)} %bitcast.first_ref, s32[1,64]{1,0:T(1,128)} %bitcast.21, f32[1,512]{1,0:T(1,128)} %bitcast.20, bf16[16,1024]{1,0:T(8,128)(2,1)} %bitcast.18, ...), custom_call_target="tpu_custom_call" | custom-call | tf_op jit(solution)/shard_map/prep/pallas_call | solution.py:132
  4.0 0.1 collective-permute-start.1
  4.1 0.7 collective-permute-start
  4.8 0.0 collective-permute-done
  4.8 5.1 %collective-permute-done.1.kv_near = bf16[1024,128]{1,0:T(8,128)(2,1)S(1)} collective-permute-done((bf16[1024,128]{1,0:T(8,128)(2,1)S(1)}, bf16[1024,128]{1,0:T(8,128)(2,1)S(1)}, u32[]{:S(2)}, u32[]{:S(2)}) %collective-permute-start.1) | collective-permute-done | bytes 262176 | tf_op jit(solution)/shard_map/ppermute | solution.py:20
  9.9 0.7 broadcast_in_dim.28
  10.6 0.0 copy-start.3
  10.7 11.8 %all-to-all-start = ((bf16[8,40,512]{2,1,0:T(8,128)(2,1)}), bf16[8,40,512]{2,1,0:T(8,128)(2,1)S(1)}, u32[]{:S(2)}, u32[]{:S(2)}) async-start(bf16[8,40,512]{2,1,0:T(8,128)(2,1)} %broadcast_in_dim.28), calls=%async_computation | async-start | bytes 655360 | tf_op jit(solution)/shard_map/all_to_all | solution.py:39
  22.5 0.0 copy-start.2
  22.5 0.8 pad_maximum_fusion
  23.3 1.2 %collective-permute-start.2 = (bf16[2,1024,128]{2,1,0:T(8,128)(2,1)}, bf16[2,1024,128]{2,1,0:T(8,128)(2,1)S(1)}, u32[]{:S(2)}, u32[]{:S(2)}) collective-permute-start(bf16[2,1024,128]{2,1,0:T(8,128)(2,1)} %pad_maximum_fusion), channel_id=1, source_target_pairs={{0,16},{8,24},{16,32},{24,40},{32,48},{40,56},{48,64},{56,72},{64,... | collective-permute-start | bytes 1572872 | tf_op jit(solution)/shard_map/ppermute | solution.py:20
  24.5 11.8 %all-to-all-done = bf16[8,40,512]{2,1,0:T(8,128)(2,1)S(1)} async-done(((bf16[8,40,512]{2,1,0:T(8,128)(2,1)}), bf16[8,40,512]{2,1,0:T(8,128)(2,1)S(1)}, u32[]{:S(2)}, u32[]{:S(2)}) %all-to-all-start) | async-done | bytes 327712 | tf_op jit(solution)/shard_map/all_to_all | solution.py:39
  36.4 0.1 collective-permute-start.3
  36.5 3.5 %collective-permute-done.3.near_hbm = f32[24,512]{1,0:T(8,128)S(1)} collective-permute-done((f32[24,512]{1,0:T(8,128)S(1)}, f32[24,512]{1,0:T(8,128)S(1)}, u32[]{:S(2)}, u32[]{:S(2)}) %collective-permute-start.3) | collective-permute-done | bytes 49184 | tf_op jit(solution)/shard_map/ppermute | solution.py:20
  40.0 1.0 collective-permute-start.4
  41.0 0.0 collective-permute-done.2.kv_far
  41.0 6.3 %collective-permute-done.4.far_hbm = f32[24,1024]{1,0:T(8,128)S(1)} collective-permute-done((f32[24,1024]{1,0:T(8,128)S(1)}, f32[24,1024]{1,0:T(8,128)S(1)}, u32[]{:S(2)}, u32[]{:S(2)}) %collective-permute-start.4) | collective-permute-done | bytes 98336 | tf_op jit(solution)/shard_map/ppermute | solution.py:20
  47.3 0.0 copy-done.3
  47.3 0.0 copy-done.2
  47.3 0.0 copy-start.1
  47.3 21.0 %attn.1 = (bf16[512,1024]{1,0:T(8,128)(2,1)}, f32[16,512]{1,0:T(8,128)S(1)}, bf16[16,2048]{1,0:T(8,128)(2,1)S(1)}, bf16[16,128]{1,0:T(8,128)(2,1)S(1)}, bf16[16,...) custom-call(s32[3]{0:T(128)S(1)} %get-tuple-element.23.low_ref, bf16[512,1024]{1,0:T(8,128)(2,1)S(1)} %copy-done.2, ...), custom_call_target="tpu_custom_call" | custom-call | tf_op jit(solution)/shard_map/attn/pallas_call | solution.py:295
  68.3 0.0 copy-start
  68.4 0.1 collective-permute-start.5
  68.4 3.9 %collective-permute-done.5 = bf16[16,1024]{1,0:T(8,128)(2,1)S(1)} collective-permute-done((bf16[16,1024]{1,0:T(8,128)(2,1)S(1)}, bf16[16,1024]{1,0:T(8,128)(2,1)S(1)}, u32[]{:S(2)}, u32[]{:S(2)}) %collective-permute-start.5) | collective-permute-done | bytes 32800 | tf_op jit(solution)/shard_map/ppermute | solution.py:20
  72.4 0.1 collective-permute-start.6
  72.5 1.4 %collective-permute-done.6 = bf16[16,512]{1,0:T(8,128)(2,1)S(1)} collective-permute-done((bf16[16,512]{1,0:T(8,128)(2,1)S(1)}, bf16[16,512]{1,0:T(8,128)(2,1)S(1)}, u32[]{:S(2)}, u32[]{:S(2)}) %collective-permute-start.6) | collective-permute-done | bytes 16416 | tf_op jit(solution)/shard_map/ppermute | solution.py:20
  73.9 16.6 %all_to_all.10.shared_ref = bf16[8,32,512]{2,1,0:T(8,128)(2,1)S(1)} all-to-all(bf16[8,32,512]{2,1,0:T(8,128)(2,1)S(1)} %broadcast_in_dim.29), channel_id=1, replica_groups=mesh['ctx'=32,'tp'=8] {'tp'}, dimensions={0} | all-to-all | bytes 524288 | tf_op jit(solution)/shard_map/all_to_all | solution.py:39
  90.5 0.0 copy-done.1
  90.5 0.0 copy-done
  90.5 0.4 grads.1
  90.9 0.0 copy-start.4
  91.0 0.1 collective-permute-start.7
  91.1 1.3 %collective-permute-done.7 = bf16[16,3200]{1,0:T(8,128)(2,1)S(1)} collective-permute-done((bf16[16,3200]{1,0:T(8,128)(2,1)S(1)}, bf16[16,3200]{1,0:T(8,128)(2,1)S(1)}, u32[]{:S(2)}, u32[]{:S(2)}) %collective-permute-start.7) | collective-permute-done | bytes 102432 | tf_op jit(solution)/shard_map/ppermute | solution.py:25
  92.4 0.9 collective-permute-start.8
  93.3 4.1 %collective-permute-done.8 = bf16[16,3200]{1,0:T(8,128)(2,1)S(1)} collective-permute-done((bf16[16,3200]{1,0:T(8,128)(2,1)S(1)}, bf16[16,3200]{1,0:T(8,128)(2,1)S(1)}, u32[]{:S(2)}, u32[]{:S(2)}) %collective-permute-start.8) | collective-permute-done | bytes 102432 | tf_op jit(solution)/shard_map/ppermute | solution.py:25
  97.5 0.0 copy-start.5
  97.5 0.1 collective-permute-start.9
  97.6 6.2 %collective-permute-done.9 = bf16[16,3200]{1,0:T(8,128)(2,1)S(1)} collective-permute-done((bf16[16,3200]{1,0:T(8,128)(2,1)S(1)}, bf16[16,3200]{1,0:T(8,128)(2,1)S(1)}, u32[]{:S(2)}, u32[]{:S(2)}) %collective-permute-start.9) | collective-permute-done | bytes 102432 | tf_op jit(solution)/shard_map/ppermute | solution.py:25
  103.7 0.1 fusion.2
  103.8 0.1 collective-permute-start.10
  103.9 0.0 copy-done.4
  103.9 1.4 %multiply_convert_fusion = bf16[512,1024]{1,0:T(8,128)(2,1)} fusion(bf16[16,512]{1,0:T(8,128)(2,1)S(1)} %get-tuple-element.36, bf16[16,1024]{1,0:T(8,128)(2,1)S(1)} %copy-done.4), kind=kOutput, calls=%fused_computation | convolution fusion | flops 17825792 | bytes 1097728 | tf_op jit(solution)/shard_map/dot_general | solution.py:51
  105.3 4.0 %collective-permute-done.10 = bf16[16,3200]{1,0:T(8,128)(2,1)S(1)} collective-permute-done((bf16[16,3200]{1,0:T(8,128)(2,1)S(1)}, bf16[16,3200]{1,0:T(8,128)(2,1)S(1)}, u32[]{:S(2)}, u32[]{:S(2)}) %collective-permute-start.10) | collective-permute-done | bytes 102432 | tf_op jit(solution)/shard_map/ppermute | solution.py:25
  109.3 0.1 fusion.3
  109.4 0.1 collective-permute-start.11
  109.5 0.0 copy-done.5
  109.5 1.4 %convolution_convert_fusion = bf16[512,1024]{1,0:T(8,128)(2,1)} fusion(bf16[16,512]{1,0:T(8,128)(2,1)S(1)} %get-tuple-element.37, bf16[1024,16]{0,1:T(8,128)(2,1)S(1)} %copy-done.5), kind=kOutput, calls=%fused_computation.1 | convolution fusion | flops 17301504 | bytes 1097728 | tf_op jit(solution)/shard_map/dot_general | solution.py:401
  111.0 4.7 %collective-permute-done.11 = bf16[16,3200]{1,0:T(8,128)(2,1)S(1)} collective-permute-done((bf16[16,3200]{1,0:T(8,128)(2,1)S(1)}, bf16[16,3200]{1,0:T(8,128)(2,1)S(1)}, u32[]{:S(2)}, u32[]{:S(2)}) %collective-permute-start.11) | collective-permute-done | bytes 102432 | tf_op jit(solution)/shard_map/ppermute | solution.py:25
  115.7 0.1 convert_add_fusion
  115.8 0.6 slice.57
  116.4 0.7 fusion.9
  (16 shorter events, 0.2 us)
Async XLA Ops:
  4.0 5.9 %collective-permute-start.1 = (bf16[1024,128]{1,0:T(8,128)(2,1)S(1)}, bf16[1024,128]{1,0:T(8,128)(2,1)S(1)}, u32[]{:S(2)}, u32[]{:S(2)}) collective-permute-start(bf16[1024,128]{1,0:T(8,128)(2,1)S(1)} %get-tuple-element.27.kv_own), channel_id=1, source_target_pairs={{0,8},{8,16},{16,24},{24,32},{32,40},{40,48},{48,56},{56,64},{64,7... | collective-permute-start | bytes 786440 | tf_op jit(solution)/shard_map/ppermute | solution.py:20
  4.1 0.7 collective-permute-start
  10.6 36.7 %copy-start.3 = (bf16[512,1024]{1,0:T(8,128)(2,1)S(1)}, bf16[512,1024]{1,0:T(8,128)(2,1)}, u32[]{:S(2)}) copy-start(bf16[512,1024]{1,0:T(8,128)(2,1)} %g_ref.1) | copy-start | bytes 3145732
  10.7 25.7 %all-to-all-start = ((bf16[8,40,512]{2,1,0:T(8,128)(2,1)}), bf16[8,40,512]{2,1,0:T(8,128)(2,1)S(1)}, u32[]{:S(2)}, u32[]{:S(2)}) async-start(bf16[8,40,512]{2,1,0:T(8,128)(2,1)} %broadcast_in_dim.28), calls=%async_computation | async-start | bytes 655360 | tf_op jit(solution)/shard_map/all_to_all | solution.py:39
  22.5 24.8 %copy-start.2 = (bf16[512,1024]{1,0:T(8,128)(2,1)S(1)}, bf16[512,1024]{1,0:T(8,128)(2,1)}, u32[]{:S(2)}) copy-start(bf16[512,1024]{1,0:T(8,128)(2,1)} %q_ref.1) | copy-start | bytes 3145732
  23.3 17.7 %collective-permute-start.2 = (bf16[2,1024,128]{2,1,0:T(8,128)(2,1)}, bf16[2,1024,128]{2,1,0:T(8,128)(2,1)S(1)}, u32[]{:S(2)}, u32[]{:S(2)}) collective-permute-start(bf16[2,1024,128]{2,1,0:T(8,128)(2,1)} %pad_maximum_fusion), channel_id=1, source_target_pairs={{0,16},{8,24},{16,32},{24,40},{32,48},{40,56},{48,64},{56,72},{64,... | collective-permute-start | bytes 1572872 | tf_op jit(solution)/shard_map/ppermute | solution.py:20
  36.4 3.6 %collective-permute-start.3 = (f32[24,512]{1,0:T(8,128)S(1)}, f32[24,512]{1,0:T(8,128)S(1)}, u32[]{:S(2)}, u32[]{:S(2)}) collective-permute-start(f32[24,512]{1,0:T(8,128)S(1)} %slice.53.own_hbm), channel_id=1, source_target_pairs={{0,8},{8,16},{16,24},{24,32},{32,40},{40,48},{48,56},{56,64},{64,7... | collective-permute-start | bytes 147464 | tf_op jit(solution)/shard_map/ppermute | solution.py:20
  40.0 7.3 %collective-permute-start.4 = (f32[24,1024]{1,0:T(8,128)S(1)}, f32[24,1024]{1,0:T(8,128)S(1)}, u32[]{:S(2)}, u32[]{:S(2)}) collective-permute-start(f32[24,1024]{1,0:T(8,128)S(1)} %pad_maximum_fusion.1), channel_id=1, source_target_pairs={{0,16},{8,24},{16,32},{24,40},{32,48},{40,56},{48,64},{56,72},{64,... | collective-permute-start | bytes 294920 | tf_op jit(solution)/shard_map/ppermute | solution.py:20
  47.3 43.2 %copy-start.1 = (bf16[512,1024]{1,0:T(8,128)(2,1)S(1)}, bf16[512,1024]{1,0:T(8,128)(2,1)}, u32[]{:S(2)}) copy-start(bf16[512,1024]{1,0:T(8,128)(2,1)} %dout_ref.1) | copy-start | bytes 3145732
  68.3 22.2 %copy-start = (bf16[512,1024]{1,0:T(8,128)(2,1)S(1)}, bf16[512,1024]{1,0:T(8,128)(2,1)}, u32[]{:S(2)}) copy-start(bf16[512,1024]{1,0:T(8,128)(2,1)} %hidden_ref.1) | copy-start | bytes 3145732
  68.4 4.0 %collective-permute-start.5 = (bf16[16,1024]{1,0:T(8,128)(2,1)S(1)}, bf16[16,1024]{1,0:T(8,128)(2,1)S(1)}, u32[]{:S(2)}, u32[]{:S(2)}) collective-permute-start(bf16[16,1024]{1,0:T(8,128)(2,1)S(1)} %slice.44), channel_id=1, source_target_pairs={{0,240},{8,248},{16,0},{24,8},{32,16},{40,24},{48,32},{56,40},{64,... | collective-permute-start | bytes 98312 | tf_op jit(solution)/shard_map/ppermute | solution.py:20
  72.4 1.5 %collective-permute-start.6 = (bf16[16,512]{1,0:T(8,128)(2,1)S(1)}, bf16[16,512]{1,0:T(8,128)(2,1)S(1)}, u32[]{:S(2)}, u32[]{:S(2)}) collective-permute-start(bf16[16,512]{1,0:T(8,128)(2,1)S(1)} %fusion.4), channel_id=1, source_target_pairs={{0,248},{8,0},{16,8},{24,16},{32,24},{40,32},{48,40},{56,48},{64,5... | collective-permute-start | bytes 49160 | tf_op jit(solution)/shard_map/ppermute | solution.py:20
  90.9 13.0 %copy-start.4 = (bf16[16,1024]{1,0:T(8,128)(2,1)S(1)}, bf16[16,1024]{1,0:T(8,128)(2,1)}, u32[]{:S(2)}) copy-start(bf16[16,1024]{1,0:T(8,128)(2,1)} %up_hbm.1) | copy-start | bytes 98308
  91.0 1.4 %collective-permute-start.7 = (bf16[16,3200]{1,0:T(8,128)(2,1)S(1)}, bf16[16,3200]{1,0:T(8,128)(2,1)S(1)}, u32[]{:S(2)}, u32[]{:S(2)}) collective-permute-start(bf16[16,3200]{1,0:T(8,128)(2,1)S(1)} %fusion), channel_id=1, source_target_pairs={{0,8},{8,0},{16,24},{24,16},{32,40},{40,32},{48,56},{56,48},{64,72... | collective-permute-start | bytes 307208 | tf_op jit(solution)/shard_map/ppermute | solution.py:25
  92.4 5.0 %collective-permute-start.8 = (bf16[16,3200]{1,0:T(8,128)(2,1)S(1)}, bf16[16,3200]{1,0:T(8,128)(2,1)S(1)}, u32[]{:S(2)}, u32[]{:S(2)}) collective-permute-start(bf16[16,3200]{1,0:T(8,128)(2,1)S(1)} %fusion.1), channel_id=1, source_target_pairs={{0,16},{8,24},{16,0},{24,8},{32,48},{40,56},{48,32},{56,40},{64,80... | collective-permute-start | bytes 307208 | tf_op jit(solution)/shard_map/ppermute | solution.py:25
  97.5 12.1 %copy-start.5 = (bf16[1024,16]{0,1:T(8,128)(2,1)S(1)}, bf16[1024,16]{0,1:T(8,128)(2,1)}, u32[]{:S(2)}) copy-start(bf16[1024,16]{0,1:T(8,128)(2,1)} %param.17) | copy-start | bytes 98308
  97.5 6.3 %collective-permute-start.9 = (bf16[16,3200]{1,0:T(8,128)(2,1)S(1)}, bf16[16,3200]{1,0:T(8,128)(2,1)S(1)}, u32[]{:S(2)}, u32[]{:S(2)}) collective-permute-start(bf16[16,3200]{1,0:T(8,128)(2,1)S(1)} %fusion.8), channel_id=1, source_target_pairs={{0,32},{8,40},{16,48},{24,56},{32,0},{40,8},{48,16},{56,24},{64,96... | collective-permute-start | bytes 307208 | tf_op jit(solution)/shard_map/ppermute | solution.py:25
  103.8 5.5 %collective-permute-start.10 = (bf16[16,3200]{1,0:T(8,128)(2,1)S(1)}, bf16[16,3200]{1,0:T(8,128)(2,1)S(1)}, u32[]{:S(2)}, u32[]{:S(2)}) collective-permute-start(bf16[16,3200]{1,0:T(8,128)(2,1)S(1)} %fusion.2), channel_id=1, source_target_pairs={{0,64},{8,72},{16,80},{24,88},{32,96},{40,104},{48,112},{56,120},{... | collective-permute-start | bytes 307208 | tf_op jit(solution)/shard_map/ppermute | solution.py:25
  109.4 6.3 %collective-permute-start.11 = (bf16[16,3200]{1,0:T(8,128)(2,1)S(1)}, bf16[16,3200]{1,0:T(8,128)(2,1)S(1)}, u32[]{:S(2)}, u32[]{:S(2)}) collective-permute-start(bf16[16,3200]{1,0:T(8,128)(2,1)S(1)} %fusion.3), channel_id=1, source_target_pairs={{0,128},{8,136},{16,144},{24,152},{32,160},{40,168},{48,176},{56,1... | collective-permute-start | bytes 307208 | tf_op jit(solution)/shard_map/ppermute | solution.py:25

commit v5 on v4

--- a/solution.py
+++ b/solution.py
@@ -78,35 +78,77 @@
     return [pltpu.with_memory_space_constraint(a, pltpu.HBM) for a in arrays]
 
 
-def prep_kernel(
-    first_ref, len_hbm, ratio_hbm, avt_hbm, up_hbm, key_hbm, frozen_hbm, hidden_hbm, dout_hbm,
-    kv_ref, rank_ref, margin_ref, start_ref, low_ref,
-    len_ref, ratio_ref, avt_ref, up_ref, hidden_ref, dout_ref, sems,
-):
-    rows = key_hbm.shape[0]
-    rank = up_ref.shape[0]
-    pairs = [
-        (len_hbm, len_ref), (ratio_hbm, ratio_ref), (avt_hbm, avt_ref), (up_hbm, up_ref),
-        (hidden_hbm, hidden_ref), (dout_hbm, dout_ref),
-        (key_hbm, kv_ref.at[0:rows]), (frozen_hbm, kv_ref.at[rows : 2 * rows]),
-    ]
+def start_copies(pairs, sems):
     copies = [pltpu.make_async_copy(src, dst, sems.at[i]) for i, (src, dst) in enumerate(pairs)]
     for copy in copies:
         copy.start()
+    return copies
+
+
+def send_kernel(
+    first_ref, len_hbm, ratio_hbm, key_hbm, frozen_hbm, kv_ref, margin_ref, len_ref, ratio_ref, sems,
+):
+    rows = key_hbm.shape[0]
+    copies = start_copies(
+        [
+            (len_hbm, len_ref), (ratio_hbm, ratio_ref),
+            (key_hbm, kv_ref.at[0:rows]), (frozen_hbm, kv_ref.at[rows : 2 * rows]),
+        ],
+        sems,
+    )
+    margin_ref[...] = jnp.zeros_like(margin_ref)
     copies[0].wait()
     copies[1].wait()
     docs = len_ref.shape[1]
-    first = first_ref[0]
     begin, end = doc_bounds(len_ref[...])
-    pos = iota((1, rows), 1) + first
+    pos = iota((1, rows), 1) + first_ref[0]
     own = (begin <= pos) & (pos < end)
     margin = jnp.sum(jnp.where(own, ratio_ref[...], 0.0), axis=1, keepdims=True)
     shape = (docs, 128)
     margin = jnp.sum(jnp.where(iota(shape, 0) == iota(shape, 1), margin, 0.0), axis=0, keepdims=True)
     margin = jnp.broadcast_to(margin, (8, 128))
-    margin_ref[...] = jnp.zeros_like(margin_ref)
     for i, part in enumerate(three_parts(margin)):
         margin_ref[:, i * 128 : (i + 1) * 128] = part
+    copies[2].wait()
+    copies[3].wait()
+
+
+def to_send(first, doc_lengths, token_logratio, keys, frozen):
+    rows = keys.shape[0]
+    vmem = pl.BlockSpec(memory_space=pltpu.VMEM)
+    return pl.pallas_call(
+        send_kernel,
+        in_specs=[pl.BlockSpec(memory_space=pltpu.SMEM)] + [pl.BlockSpec(memory_space=pltpu.HBM)] * 4,
+        out_specs=[vmem] * 2,
+        out_shape=[
+            jax.ShapeDtypeStruct((2 * rows, HD), BF16),
+            jax.ShapeDtypeStruct((8, rows), BF16),
+        ],
+        scratch_shapes=[pltpu.VMEM(a.shape, a.dtype) for a in (doc_lengths, token_logratio)]
+        + [pltpu.SemaphoreType.DMA((4,))],
+        name="send",
+    )(first, *in_hbm(doc_lengths, token_logratio, keys, frozen))
+
+
+def prep_kernel(
+    first_ref, len_hbm, avt_hbm, up_hbm, hidden_hbm, dout_hbm,
+    rank_ref, start_ref, low_ref,
+    len_ref, avt_ref, up_ref, hidden_ref, dout_ref, sems,
+):
+    rows = hidden_ref.shape[0]
+    rank = up_ref.shape[0]
+    copies = start_copies(
+        [
+            (len_hbm, len_ref), (avt_hbm, avt_ref), (hidden_hbm, hidden_ref), (up_hbm, up_ref),
+            (dout_hbm, dout_ref),
+        ],
+        sems,
+    )
+    copies[0].wait()
+    first = first_ref[0]
+    begin, end = doc_bounds(len_ref[...])
+    pos = iota((1, rows), 1) + first
+    own = (begin <= pos) & (pos < end)
     base = first - 3 * rows
     start = jnp.sum(jnp.where(own, begin, 0), axis=0, keepdims=True) - base
     start_ref[...] = jnp.where(iota(start_ref.shape, 0) == 0, start, pos - base)
@@ -115,39 +157,33 @@
         head = jnp.max(start[:, half * KB : half * KB + 1].astype(F32)).astype(jnp.int32)
         low_ref[half] = jnp.clip(head // KB, 0, 3 * halves + half)
     low_ref[halves] = base
+    copies[1].wait()
     copies[2].wait()
-    copies[4].wait()
     rank_ref[0:rank, :] = nt(hidden_ref[...], avt_ref[...]).T.astype(BF16)
     copies[3].wait()
-    copies[5].wait()
+    copies[4].wait()
     rank_ref[rank : 2 * rank, :] = nt(dout_ref[...], up_ref[...]).T.astype(BF16)
-    copies[6].wait()
-    copies[7].wait()
-
-
-def prepare(first, doc_lengths, token_logratio, a_v_t, up, keys, frozen, hidden, d_out):
-    rows = keys.shape[0]
+
+
+def prepare(first, doc_lengths, a_v_t, up, hidden, d_out):
+    rows = hidden.shape[0]
     rank = up.shape[0]
     vmem = pl.BlockSpec(memory_space=pltpu.VMEM)
+    smem = pl.BlockSpec(memory_space=pltpu.SMEM)
     return pl.pallas_call(
         prep_kernel,
-        in_specs=[pl.BlockSpec(memory_space=pltpu.SMEM)] + [pl.BlockSpec(memory_space=pltpu.HBM)] * 8,
-        out_specs=[vmem] * 4 + [pl.BlockSpec(memory_space=pltpu.SMEM)],
+        in_specs=[smem] + [pl.BlockSpec(memory_space=pltpu.HBM)] * 5,
+        out_specs=[vmem] * 2 + [smem],
         out_shape=[
-            jax.ShapeDtypeStruct((2 * rows, HD), BF16),
             jax.ShapeDtypeStruct((2 * rank, rows), BF16),
-            jax.ShapeDtypeStruct((8, rows), BF16),
             jax.ShapeDtypeStruct((8, rows), jnp.int32),
             jax.ShapeDtypeStruct((rows // KB + 1,), jnp.int32),
         ],
-        scratch_shapes=[
-            pltpu.VMEM(a.shape, a.dtype)
-            for a in (doc_lengths, token_logratio, a_v_t, up, hidden, d_out)
-        ]
-        + [pltpu.SemaphoreType.DMA((8,))],
+        scratch_shapes=[pltpu.VMEM(a.shape, a.dtype) for a in (doc_lengths, a_v_t, up, hidden, d_out)]
+        + [pltpu.SemaphoreType.DMA((5,))],
         compiler_params=pltpu.CompilerParams(vmem_limit_bytes=32 * 2**20),
         name="prep",
-    )(first, *in_hbm(doc_lengths, token_logratio, a_v_t, up, keys, frozen, hidden, d_out))
+    )(first, *in_hbm(doc_lengths, a_v_t, up, hidden, d_out))
 
 
 def margin_of(line):
@@ -174,13 +210,10 @@
         (far_hbm, lv_far), (near_hbm, lv_near), (own_hbm, lv_own),
     ]
     pairs += [(kv_far, kv.at[0:2]), (kv_near, kv.at[2]), (kv_own, kv.at[3])]
-    copies = [pltpu.make_async_copy(src, dst, sems.at[i]) for i, (src, dst) in enumerate(pairs)]
-    for copy in copies:
-        copy.start()
+    copies = start_copies(pairs, sems)
     vg[...] = jnp.zeros_like(vg)
     lowo_ref[...] = jnp.zeros_like(lowo_ref)
-    for copy in copies:
-        copy.wait()
+    copies[4].wait()
     biases = (bias0, bias1)
     for half in range(halves):
         start = start_ref[0:1, half * KB : (half + 1) * KB]
@@ -189,6 +222,9 @@
             kpos = iota((KB, KB), 0) + kb * KB
             ok = (kpos >= start) & (kpos <= qpos)
             biases[half][kb * KB : (kb + 1) * KB, :] = jnp.where(ok, 0.0, NEG)
+    for i, copy in enumerate(copies):
+        if i != 4:
+            copy.wait()
     r_scr[...] = rt_ref[...].astype(F32).T.astype(BF16)
     uvt = uv_ref[...].astype(F32).T.astype(BF16)
     lows = (
@@ -369,9 +405,9 @@
     doc_lengths = doc_lengths[None, :]
     pair_slots = pair_slots[None, :]
 
-    kv, rank_rows, margin, start_q, low = prepare(
-        first, doc_lengths, token_logratio[None, :], adapter_a_v.T, output_up_matrix, rotated_keys,
-        frozen_value_rows, hidden, out_cotangent,
+    kv, margin = to_send(first, doc_lengths, token_logratio[None, :], rotated_keys, frozen_value_rows)
+    rank_rows, start_q, low = prepare(
+        first, doc_lengths, adapter_a_v.T, output_up_matrix, hidden, out_cotangent
     )
     kv_near = shift(kv, 1)
     margin, kv_near = lax.optimization_barrier((spread(margin), kv_near))

time: 116 us -> 117 us (level)
  the two profiles are of different devices: /device:TPU:2 before, /device:TPU:16 now
where the time goes in v5:
time: 117 us; the launch traced here: 116 us
  waiting for transfers between devices  53.1 us (45%)
  Pallas kernels  22.3 us (19%)
  starting transfers between devices  17.2 us (15%)
  blocking collectives  15.8 us (14%)
  matrix products  2.85 us (2%)
  local copies, waits for them, and re-layouts  2.09 us (2%)
  other arithmetic  1.31 us (1%)
    ppermute x6, waiting for transfers between devices, shift(): return lax.ppermute(value, 'ctx', [(i, (i + by) % n) for i in range(n)])  21.6 us
    ppermute x5, waiting for transfers between devices, flip(): return lax.ppermute(value, 'ctx', [(i, i ^ mask) for i in range(n)])  19.9 us
    pallas_call x1, Pallas kernels, attention(): pl.pallas_call(attn_kernel, in_specs=[pl.BlockSpec(memory_space=pltpu.SME...  17.5 us
    all_to_all x1, blocking collectives, share_tp(): lax.all_to_all(jnp.broadcast_to(rows[None], (n,) + rows.shape), 'tp', 0, 0)  15.8 us
    all_to_all x1, waiting for transfers between devices, share_tp(): lax.all_to_all(jnp.broadcast_to(rows[None], (n,) + rows.shape), 'tp', 0, 0)  11.5 us
    all_to_all x1, starting transfers between devices, share_tp(): lax.all_to_all(jnp.broadcast_to(rows[None], (n,) + rows.shape), 'tp', 0, 0)  9.71 us
    ppermute x6, starting transfers between devices, shift(): return lax.ppermute(value, 'ctx', [(i, (i + by) % n) for i in range(n)])  4.35 us
    pallas_call x1, Pallas kernels, prepare(): pl.pallas_call(prep_kernel, in_specs=[smem] + [pl.BlockSpec(memory_space=...  2.72 us
  transfers between devices with their start and end apart: 13, of which 11 were waited for; matrix products, arithmetic and copies ran while one was open for 3% of the time, Pallas kernels for 2%

profile of v5, /device:TPU:16, one launch (start us, length us, event | category | flops | bytes accessed | tf_op | source)
XLA Modules:
  0.0 115.5 jit_solution(1184966358416542923)
XLA Ops:
  0.6 1.7 %send.1 = (bf16[1024,128]{1,0:T(8,128)(2,1)}, bf16[8,512]{1,0:T(8,128)(2,1)}) custom-call(s32[1]{0:T(128)} %bitcast.first_ref, s32[1,64]{1,0:T(1,128)} %bitcast.20, f32[1,512]{1,0:T(1,128)} %bitcast.23, bf16[512,128]{1,0:T(8,128)(2,1)} %key_hbm.1, bf16[512,128]{1,0:T(8,128)(2,1)} %frozen_hbm.1), custom_call_target="tpu_custom_call" | custom-call | tf_op jit(solution)/shard_map/send/pallas_call | solution.py:119
  2.4 0.1 collective-permute-start.1
  2.5 1.4 %collective-permute-start = (bf16[8,512]{1,0:T(8,128)(2,1)}, bf16[8,512]{1,0:T(8,128)(2,1)S(1)}, u32[]{:S(2)}, u32[]{:S(2)}) collective-permute-start(bf16[8,512]{1,0:T(8,128)(2,1)} %get-tuple-element.26), channel_id=1, source_target_pairs={{0,0},{33,1},{66,2},{99,3},{132,4},{165,5},{198,6},{231,7},{8,8},{... | collective-permute-start | bytes 24584 | tf_op jit(solution)/shard_map/ppermute | solution.py:34
  3.8 2.7 %prep.1 = (bf16[32,512]{1,0:T(8,128)(2,1)S(1)}, s32[8,512]{1,0:T(8,128)S(1)}, s32[3]{0:T(128)S(1)}) custom-call(s32[1]{0:T(128)} %bitcast.first_ref, s32[1,64]{1,0:T(1,128)} %bitcast.21, bf16[16,1024]{1,0:T(8,128)(2,1)} %bitcast.18, bf16[16,1024]{1,0:T(8,128)(2,1)} %up_hbm.1, bf16[512,1024]{1,0:T(8,128)(2,1)} %hidden_ref.1, bf16[512,1024]{1,0:T(8,128)(2,1)} %dout_ref.1), custom_call_target="tpu_custom_call" | custom-call | tf_op jit(solution)/shard_map/prep/pallas_call | solution.py:173
  6.6 0.0 copy-start.4
  6.6 0.0 collective-permute-done
  6.6 4.0 %collective-permute-done.1.kv_near = bf16[1024,128]{1,0:T(8,128)(2,1)S(1)} collective-permute-done((bf16[1024,128]{1,0:T(8,128)(2,1)}, bf16[1024,128]{1,0:T(8,128)(2,1)S(1)}, u32[]{:S(2)}, u32[]{:S(2)}) %collective-permute-start.1) | collective-permute-done | bytes 262176 | tf_op jit(solution)/shard_map/ppermute | solution.py:20
  10.6 0.7 broadcast_in_dim.28
  11.3 0.0 copy-start.3
  11.3 9.7 %all-to-all-start = ((bf16[8,40,512]{2,1,0:T(8,128)(2,1)}), bf16[8,40,512]{2,1,0:T(8,128)(2,1)S(1)}, u32[]{:S(2)}, u32[]{:S(2)}) async-start(bf16[8,40,512]{2,1,0:T(8,128)(2,1)} %broadcast_in_dim.28), calls=%async_computation | async-start | bytes 655360 | tf_op jit(solution)/shard_map/all_to_all | solution.py:39
  21.1 0.0 copy-start.2
  21.1 0.0 copy-done.4
  21.1 0.8 pad_maximum_fusion
  21.9 1.5 %collective-permute-start.2 = (bf16[2,1024,128]{2,1,0:T(8,128)(2,1)}, bf16[2,1024,128]{2,1,0:T(8,128)(2,1)S(1)}, u32[]{:S(2)}, u32[]{:S(2)}) collective-permute-start(bf16[2,1024,128]{2,1,0:T(8,128)(2,1)} %pad_maximum_fusion), channel_id=1, source_target_pairs={{0,16},{8,24},{16,32},{24,40},{32,48},{40,56},{48,64},{56,72},{64,... | collective-permute-start | bytes 1572872 | tf_op jit(solution)/shard_map/ppermute | solution.py:20
  23.4 11.5 %all-to-all-done = bf16[8,40,512]{2,1,0:T(8,128)(2,1)S(1)} async-done(((bf16[8,40,512]{2,1,0:T(8,128)(2,1)}), bf16[8,40,512]{2,1,0:T(8,128)(2,1)S(1)}, u32[]{:S(2)}, u32[]{:S(2)}) %all-to-all-start) | async-done | bytes 327712 | tf_op jit(solution)/shard_map/all_to_all | solution.py:39
  35.0 0.1 collective-permute-start.3
  35.1 5.6 %collective-permute-done.3.near_hbm = f32[24,512]{1,0:T(8,128)S(1)} collective-permute-done((f32[24,512]{1,0:T(8,128)S(1)}, f32[24,512]{1,0:T(8,128)S(1)}, u32[]{:S(2)}, u32[]{:S(2)}) %collective-permute-start.3) | collective-permute-done | bytes 49184 | tf_op jit(solution)/shard_map/ppermute | solution.py:20
  40.7 0.1 collective-permute-start.4
  40.8 0.0 collective-permute-done.2.kv_far
  40.8 6.7 %collective-permute-done.4.far_hbm = f32[24,1024]{1,0:T(8,128)S(1)} collective-permute-done((f32[24,1024]{1,0:T(8,128)S(1)}, f32[24,1024]{1,0:T(8,128)S(1)}, u32[]{:S(2)}, u32[]{:S(2)}) %collective-permute-start.4) | collective-permute-done | bytes 98336 | tf_op jit(solution)/shard_map/ppermute | solution.py:20
  47.5 0.0 copy-done.3
  47.5 0.0 copy-done.2
  47.5 0.0 copy-start.1
  47.5 17.5 %attn.1 = (bf16[512,1024]{1,0:T(8,128)(2,1)}, f32[16,512]{1,0:T(8,128)S(1)}, bf16[16,2048]{1,0:T(8,128)(2,1)S(1)}, bf16[16,128]{1,0:T(8,128)(2,1)S(1)}, bf16[16,...) custom-call(s32[3]{0:T(128)S(1)} %get-tuple-element.23.low_ref, bf16[512,1024]{1,0:T(8,128)(2,1)S(1)} %copy-done.2, ...), custom_call_target="tpu_custom_call" | custom-call | tf_op jit(solution)/shard_map/attn/pallas_call | solution.py:331
  65.0 0.0 copy-start
  65.0 0.1 collective-permute-start.5
  65.1 3.9 %collective-permute-done.5 = bf16[16,1024]{1,0:T(8,128)(2,1)S(1)} collective-permute-done((bf16[16,1024]{1,0:T(8,128)(2,1)S(1)}, bf16[16,1024]{1,0:T(8,128)(2,1)S(1)}, u32[]{:S(2)}, u32[]{:S(2)}) %collective-permute-start.5) | collective-permute-done | bytes 32800 | tf_op jit(solution)/shard_map/ppermute | solution.py:20
  69.0 2.5 %collective-permute-start.6 = (bf16[16,512]{1,0:T(8,128)(2,1)S(1)}, bf16[16,512]{1,0:T(8,128)(2,1)S(1)}, u32[]{:S(2)}, u32[]{:S(2)}) collective-permute-start(bf16[16,512]{1,0:T(8,128)(2,1)S(1)} %fusion.4), channel_id=1, source_target_pairs={{0,248},{8,0},{16,8},{24,16},{32,24},{40,32},{48,40},{56,48},{64,5... | collective-permute-start | bytes 49160 | tf_op jit(solution)/shard_map/ppermute | solution.py:20
  71.5 1.4 %collective-permute-done.6 = bf16[16,512]{1,0:T(8,128)(2,1)S(1)} collective-permute-done((bf16[16,512]{1,0:T(8,128)(2,1)S(1)}, bf16[16,512]{1,0:T(8,128)(2,1)S(1)}, u32[]{:S(2)}, u32[]{:S(2)}) %collective-permute-start.6) | collective-permute-done | bytes 16416 | tf_op jit(solution)/shard_map/ppermute | solution.py:20
  73.0 15.8 %all_to_all.10.shared_ref = bf16[8,32,512]{2,1,0:T(8,128)(2,1)S(1)} all-to-all(bf16[8,32,512]{2,1,0:T(8,128)(2,1)S(1)} %broadcast_in_dim.29), channel_id=1, replica_groups=mesh['ctx'=32,'tp'=8] {'tp'}, dimensions={0} | all-to-all | bytes 524288 | tf_op jit(solution)/shard_map/all_to_all | solution.py:39
  88.8 0.0 copy-done.1
  88.8 0.0 copy-done
  88.8 0.4 grads.1
  89.2 0.0 copy-start.5
  89.2 0.3 collective-permute-start.7
  89.5 1.3 %collective-permute-done.7 = bf16[16,3200]{1,0:T(8,128)(2,1)S(1)} collective-permute-done((bf16[16,3200]{1,0:T(8,128)(2,1)S(1)}, bf16[16,3200]{1,0:T(8,128)(2,1)S(1)}, u32[]{:S(2)}, u32[]{:S(2)}) %collective-permute-start.7) | collective-permute-done | bytes 102432 | tf_op jit(solution)/shard_map/ppermute | solution.py:25
  90.8 0.1 collective-permute-start.8
  91.0 4.9 %collective-permute-done.8 = bf16[16,3200]{1,0:T(8,128)(2,1)S(1)} collective-permute-done((bf16[16,3200]{1,0:T(8,128)(2,1)S(1)}, bf16[16,3200]{1,0:T(8,128)(2,1)S(1)}, u32[]{:S(2)}, u32[]{:S(2)}) %collective-permute-start.8) | collective-permute-done | bytes 102432 | tf_op jit(solution)/shard_map/ppermute | solution.py:25
  95.9 0.0 copy-start.6
  95.9 1.3 %collective-permute-start.9 = (bf16[16,3200]{1,0:T(8,128)(2,1)S(1)}, bf16[16,3200]{1,0:T(8,128)(2,1)S(1)}, u32[]{:S(2)}, u32[]{:S(2)}) collective-permute-start(bf16[16,3200]{1,0:T(8,128)(2,1)S(1)} %fusion.8), channel_id=1, source_target_pairs={{0,32},{8,40},{16,48},{24,56},{32,0},{40,8},{48,16},{56,24},{64,96... | collective-permute-start | bytes 307208 | tf_op jit(solution)/shard_map/ppermute | solution.py:25
  97.2 5.0 %collective-permute-done.9 = bf16[16,3200]{1,0:T(8,128)(2,1)S(1)} collective-permute-done((bf16[16,3200]{1,0:T(8,128)(2,1)S(1)}, bf16[16,3200]{1,0:T(8,128)(2,1)S(1)}, u32[]{:S(2)}, u32[]{:S(2)}) %collective-permute-start.9) | collective-permute-done | bytes 102432 | tf_op jit(solution)/shard_map/ppermute | solution.py:25
  102.2 0.1 fusion.2
  102.3 0.1 collective-permute-start.10
  102.4 0.0 copy-done.5
  102.4 1.4 %multiply_convert_fusion = bf16[512,1024]{1,0:T(8,128)(2,1)} fusion(bf16[16,512]{1,0:T(8,128)(2,1)S(1)} %get-tuple-element.36, bf16[16,1024]{1,0:T(8,128)(2,1)S(1)} %copy-done.5), kind=kOutput, calls=%fused_computation | convolution fusion | flops 17825792 | bytes 1097728 | tf_op jit(solution)/shard_map/dot_general | solution.py:51
  103.8 4.0 %collective-permute-done.10 = bf16[16,3200]{1,0:T(8,128)(2,1)S(1)} collective-permute-done((bf16[16,3200]{1,0:T(8,128)(2,1)S(1)}, bf16[16,3200]{1,0:T(8,128)(2,1)S(1)}, u32[]{:S(2)}, u32[]{:S(2)}) %collective-permute-start.10) | collective-permute-done | bytes 102432 | tf_op jit(solution)/shard_map/ppermute | solution.py:25
  107.8 0.1 fusion.3
  107.9 0.1 collective-permute-start.11
  108.0 0.0 copy-done.6
  108.0 1.4 %convolution_convert_fusion = bf16[512,1024]{1,0:T(8,128)(2,1)} fusion(bf16[16,512]{1,0:T(8,128)(2,1)S(1)} %get-tuple-element.37, bf16[1024,16]{0,1:T(8,128)(2,1)S(1)} %copy-done.6), kind=kOutput, calls=%fused_computation.1 | convolution fusion | flops 17301504 | bytes 1097728 | tf_op jit(solution)/shard_map/dot_general | solution.py:437
  109.4 4.7 %collective-permute-done.11 = bf16[16,3200]{1,0:T(8,128)(2,1)S(1)} collective-permute-done((bf16[16,3200]{1,0:T(8,128)(2,1)S(1)}, bf16[16,3200]{1,0:T(8,128)(2,1)S(1)}, u32[]{:S(2)}, u32[]{:S(2)}) %collective-permute-start.11) | collective-permute-done | bytes 102432 | tf_op jit(solution)/shard_map/ppermute | solution.py:25
  114.2 0.1 convert_add_fusion
  114.3 0.6 slice.57
  114.9 0.7 fusion.9
  (16 shorter events, 0.2 us)
Async XLA Ops:
  2.4 8.2 %collective-permute-start.1 = (bf16[1024,128]{1,0:T(8,128)(2,1)}, bf16[1024,128]{1,0:T(8,128)(2,1)S(1)}, u32[]{:S(2)}, u32[]{:S(2)}) collective-permute-start(bf16[1024,128]{1,0:T(8,128)(2,1)} %get-tuple-element.27.kv_own), channel_id=1, source_target_pairs={{0,8},{8,16},{16,24},{24,32},{32,40},{40,48},{48,56},{56,64},{64,7... | collective-permute-start | bytes 786440 | tf_op jit(solution)/shard_map/ppermute | solution.py:20
  2.5 4.1 %collective-permute-start = (bf16[8,512]{1,0:T(8,128)(2,1)}, bf16[8,512]{1,0:T(8,128)(2,1)S(1)}, u32[]{:S(2)}, u32[]{:S(2)}) collective-permute-start(bf16[8,512]{1,0:T(8,128)(2,1)} %get-tuple-element.26), channel_id=1, source_target_pairs={{0,0},{33,1},{66,2},{99,3},{132,4},{165,5},{198,6},{231,7},{8,8},{... | collective-permute-start | bytes 24584 | tf_op jit(solution)/shard_map/ppermute | solution.py:34
  6.6 14.5 %copy-start.4 = (bf16[1024,128]{1,0:T(8,128)(2,1)S(1)}, bf16[1024,128]{1,0:T(8,128)(2,1)}, u32[]{:S(2)}) copy-start(bf16[1024,128]{1,0:T(8,128)(2,1)} %get-tuple-element.27.kv_own) | copy-start | bytes 786436
  11.3 36.2 %copy-start.3 = (bf16[512,1024]{1,0:T(8,128)(2,1)S(1)}, bf16[512,1024]{1,0:T(8,128)(2,1)}, u32[]{:S(2)}) copy-start(bf16[512,1024]{1,0:T(8,128)(2,1)} %g_ref.1) | copy-start | bytes 3145732
  11.3 23.6 %all-to-all-start = ((bf16[8,40,512]{2,1,0:T(8,128)(2,1)}), bf16[8,40,512]{2,1,0:T(8,128)(2,1)S(1)}, u32[]{:S(2)}, u32[]{:S(2)}) async-start(bf16[8,40,512]{2,1,0:T(8,128)(2,1)} %broadcast_in_dim.28), calls=%async_computation | async-start | bytes 655360 | tf_op jit(solution)/shard_map/all_to_all | solution.py:39
  21.1 26.5 %copy-start.2 = (bf16[512,1024]{1,0:T(8,128)(2,1)S(1)}, bf16[512,1024]{1,0:T(8,128)(2,1)}, u32[]{:S(2)}) copy-start(bf16[512,1024]{1,0:T(8,128)(2,1)} %q_ref.1) | copy-start | bytes 3145732
  21.9 18.9 %collective-permute-start.2 = (bf16[2,1024,128]{2,1,0:T(8,128)(2,1)}, bf16[2,1024,128]{2,1,0:T(8,128)(2,1)S(1)}, u32[]{:S(2)}, u32[]{:S(2)}) collective-permute-start(bf16[2,1024,128]{2,1,0:T(8,128)(2,1)} %pad_maximum_fusion), channel_id=1, source_target_pairs={{0,16},{8,24},{16,32},{24,40},{32,48},{40,56},{48,64},{56,72},{64,... | collective-permute-start | bytes 1572872 | tf_op jit(solution)/shard_map/ppermute | solution.py:20
  35.0 5.7 %collective-permute-start.3 = (f32[24,512]{1,0:T(8,128)S(1)}, f32[24,512]{1,0:T(8,128)S(1)}, u32[]{:S(2)}, u32[]{:S(2)}) collective-permute-start(f32[24,512]{1,0:T(8,128)S(1)} %slice.53.own_hbm), channel_id=1, source_target_pairs={{0,8},{8,16},{16,24},{24,32},{32,40},{40,48},{48,56},{56,64},{64,7... | collective-permute-start | bytes 147464 | tf_op jit(solution)/shard_map/ppermute | solution.py:20
  40.7 6.8 %collective-permute-start.4 = (f32[24,1024]{1,0:T(8,128)S(1)}, f32[24,1024]{1,0:T(8,128)S(1)}, u32[]{:S(2)}, u32[]{:S(2)}) collective-permute-start(f32[24,1024]{1,0:T(8,128)S(1)} %pad_maximum_fusion.1), channel_id=1, source_target_pairs={{0,16},{8,24},{16,32},{24,40},{32,48},{40,56},{48,64},{56,72},{64,... | collective-permute-start | bytes 294920 | tf_op jit(solution)/shard_map/ppermute | solution.py:20
  47.5 41.3 %copy-start.1 = (bf16[512,1024]{1,0:T(8,128)(2,1)S(1)}, bf16[512,1024]{1,0:T(8,128)(2,1)}, u32[]{:S(2)}) copy-start(bf16[512,1024]{1,0:T(8,128)(2,1)} %dout_ref.1) | copy-start | bytes 3145732
  65.0 23.8 %copy-start = (bf16[512,1024]{1,0:T(8,128)(2,1)S(1)}, bf16[512,1024]{1,0:T(8,128)(2,1)}, u32[]{:S(2)}) copy-start(bf16[512,1024]{1,0:T(8,128)(2,1)} %hidden_ref.1) | copy-start | bytes 3145732
  65.0 4.0 %collective-permute-start.5 = (bf16[16,1024]{1,0:T(8,128)(2,1)S(1)}, bf16[16,1024]{1,0:T(8,128)(2,1)S(1)}, u32[]{:S(2)}, u32[]{:S(2)}) collective-permute-start(bf16[16,1024]{1,0:T(8,128)(2,1)S(1)} %slice.44), channel_id=1, source_target_pairs={{0,240},{8,248},{16,0},{24,8},{32,16},{40,24},{48,32},{56,40},{64,... | collective-permute-start | bytes 98312 | tf_op jit(solution)/shard_map/ppermute | solution.py:20
  69.0 3.9 %collective-permute-start.6 = (bf16[16,512]{1,0:T(8,128)(2,1)S(1)}, bf16[16,512]{1,0:T(8,128)(2,1)S(1)}, u32[]{:S(2)}, u32[]{:S(2)}) collective-permute-start(bf16[16,512]{1,0:T(8,128)(2,1)S(1)} %fusion.4), channel_id=1, source_target_pairs={{0,248},{8,0},{16,8},{24,16},{32,24},{40,32},{48,40},{56,48},{64,5... | collective-permute-start | bytes 49160 | tf_op jit(solution)/shard_map/ppermute | solution.py:20
  89.2 13.2 %copy-start.5 = (bf16[16,1024]{1,0:T(8,128)(2,1)S(1)}, bf16[16,1024]{1,0:T(8,128)(2,1)}, u32[]{:S(2)}) copy-start(bf16[16,1024]{1,0:T(8,128)(2,1)} %up_hbm.1) | copy-start | bytes 98308
  89.2 1.6 %collective-permute-start.7 = (bf16[16,3200]{1,0:T(8,128)(2,1)S(1)}, bf16[16,3200]{1,0:T(8,128)(2,1)S(1)}, u32[]{:S(2)}, u32[]{:S(2)}) collective-permute-start(bf16[16,3200]{1,0:T(8,128)(2,1)S(1)} %fusion), channel_id=1, source_target_pairs={{0,8},{8,0},{16,24},{24,16},{32,40},{40,32},{48,56},{56,48},{64,72... | collective-permute-start | bytes 307208 | tf_op jit(solution)/shard_map/ppermute | solution.py:25
  90.8 5.0 %collective-permute-start.8 = (bf16[16,3200]{1,0:T(8,128)(2,1)S(1)}, bf16[16,3200]{1,0:T(8,128)(2,1)S(1)}, u32[]{:S(2)}, u32[]{:S(2)}) collective-permute-start(bf16[16,3200]{1,0:T(8,128)(2,1)S(1)} %fusion.1), channel_id=1, source_target_pairs={{0,16},{8,24},{16,0},{24,8},{32,48},{40,56},{48,32},{56,40},{64,80... | collective-permute-start | bytes 307208 | tf_op jit(solution)/shard_map/ppermute | solution.py:25
  95.9 12.1 %copy-start.6 = (bf16[1024,16]{0,1:T(8,128)(2,1)S(1)}, bf16[1024,16]{0,1:T(8,128)(2,1)}, u32[]{:S(2)}) copy-start(bf16[1024,16]{0,1:T(8,128)(2,1)} %param.17) | copy-start | bytes 98308
  95.9 6.3 %collective-permute-start.9 = (bf16[16,3200]{1,0:T(8,128)(2,1)S(1)}, bf16[16,3200]{1,0:T(8,128)(2,1)S(1)}, u32[]{:S(2)}, u32[]{:S(2)}) collective-permute-start(bf16[16,3200]{1,0:T(8,128)(2,1)S(1)} %fusion.8), channel_id=1, source_target_pairs={{0,32},{8,40},{16,48},{24,56},{32,0},{40,8},{48,16},{56,24},{64,96... | collective-permute-start | bytes 307208 | tf_op jit(solution)/shard_map/ppermute | solution.py:25
  102.3 5.5 %collective-permute-start.10 = (bf16[16,3200]{1,0:T(8,128)(2,1)S(1)}, bf16[16,3200]{1,0:T(8,128)(2,1)S(1)}, u32[]{:S(2)}, u32[]{:S(2)}) collective-permute-start(bf16[16,3200]{1,0:T(8,128)(2,1)S(1)} %fusion.2), channel_id=1, source_target_pairs={{0,64},{8,72},{16,80},{24,88},{32,96},{40,104},{48,112},{56,120},{... | collective-permute-start | bytes 307208 | tf_op jit(solution)/shard_map/ppermute | solution.py:25
  107.9 6.3 %collective-permute-start.11 = (bf16[16,3200]{1,0:T(8,128)(2,1)S(1)}, bf16[16,3200]{1,0:T(8,128)(2,1)S(1)}, u32[]{:S(2)}, u32[]{:S(2)}) collective-permute-start(bf16[16,3200]{1,0:T(8,128)(2,1)S(1)} %fusion.3), channel_id=1, source_target_pairs={{0,128},{8,136},{16,144},{24,152},{32,160},{40,168},{48,176},{56,1... | collective-permute-start | bytes 307208 | tf_op jit(solution)/shard_map/ppermute | solution.py:25

commit v6 on v5

--- a/solution.py
+++ b/solution.py
@@ -359,9 +359,11 @@
     )(low, queries, cotangent, *in_hbm(*args), *made, *kvs, *lows)
 
 
-def grads_kernel(shared_ref, weight_ref, vu_ref, od_ref, hidden_ref, dout_ref, sum_ref, lowo_ref, lvg_ref):
+def grads_kernel(
+    side_ref, shared_ref, weight_ref, vu_ref, od_ref, hidden_ref, dout_ref, kept_ref, sent_ref, lowo_ref, lvg_ref
+):
     rank = vu_ref.shape[0]
-    cols = hidden_ref.shape[1]
+    half = kept_ref.shape[1]
     sums = shared_ref[0].astype(F32)
     for j in range(1, shared_ref.shape[0]):
         sums = sums + shared_ref[j].astype(F32)
@@ -370,29 +372,34 @@
     low_o = sums[rank : 2 * rank].astype(BF16)
     lvg_ref[...] = lvg
     lowo_ref[...] = low_o
-    sum_ref[:, 0:cols] = nn(lvg, hidden_ref[...]).astype(BF16)
-    sum_ref[:, cols : 2 * cols] = od_ref[...]
+    vd = nn(lvg, hidden_ref[...])
     weighted = (own * low_o.astype(F32)).astype(BF16)
-    sum_ref[:, 2 * cols : 3 * cols] = (2.0 * nn(weighted, dout_ref[...])).astype(BF16)
-    sum_ref[:, 3 * cols :] = vu_ref[...]
-
-
-def grads(shared, weight, vu, od, hidden, d_out):
+    ou = 2.0 * nn(weighted, dout_ref[...])
+    parts = [vd, od_ref[...].astype(F32), ou, vu_ref[...].astype(F32)]
+    whole = jnp.concatenate(parts + [jnp.zeros((rank, 128), F32)], axis=1)
+    left = side_ref[0] == 0
+    kept_ref[...] = jnp.where(left, whole[:, :half], whole[:, half:]).astype(BF16)
+    sent_ref[...] = jnp.where(left, whole[:, half:], whole[:, :half]).astype(BF16)
+
+
+def grads(side, shared, weight, vu, od, hidden, d_out):
     rank = vu.shape[0]
     rows, cols = hidden.shape
+    half = (3 * cols + HD + 128) // 2
     vmem = pl.BlockSpec(memory_space=pltpu.VMEM)
     return pl.pallas_call(
         grads_kernel,
-        in_specs=[vmem] * 6,
-        out_specs=[vmem] * 3,
+        in_specs=[pl.BlockSpec(memory_space=pltpu.SMEM)] + [vmem] * 6,
+        out_specs=[vmem] * 4,
         out_shape=[
-            jax.ShapeDtypeStruct((rank, 3 * cols + HD), BF16),
+            jax.ShapeDtypeStruct((rank, half), BF16),
+            jax.ShapeDtypeStruct((rank, half), BF16),
             jax.ShapeDtypeStruct((rank, rows), BF16),
             jax.ShapeDtypeStruct((rank, rows), BF16),
         ],
         compiler_params=pltpu.CompilerParams(vmem_limit_bytes=32 * 2**20),
         name="grads",
-    )(shared, weight, vu, od, hidden, d_out)
+    )(side, shared, weight, vu, od, hidden, d_out)
 
 
 def shards(
@@ -428,11 +435,16 @@
     z_own = z[:, 3 * rows :].astype(F32) + z_far[:, rows:] + z_near.astype(F32)
     shared_back = share_tp(jnp.concatenate([z_own, low_o_part], axis=0).astype(BF16))
 
-    total, low_o_t, lvg_t = grads(shared_back, weight, vu, od, hidden, out_cotangent)
-    total = total.astype(F32)
-    for mask in (1, 2, 4, 8, 16):
+    side = (lax.axis_index("ctx") % 2).astype(jnp.int32)
+    kept, given, low_o_t, lvg_t = grads(side[None], shared_back, weight, vu, od, hidden, out_cotangent)
+    total = kept.astype(F32) + flip(given, 1).astype(F32)
+    for mask in (2, 4, 8, 16):
         total = lax.reduce_precision(total, 8, 7)
         total = total + flip(total.astype(BF16), mask).astype(F32)
+    total = lax.reduce_precision(total, 8, 7)
+    other = flip(total.astype(BF16), 1).astype(F32)
+    left = side == 0
+    total = jnp.concatenate([jnp.where(left, total, other), jnp.where(left, other, total)], axis=1)
     term = (2.0 * tn(low_o_t, output_up_matrix)).astype(BF16)
     input_grad = lax.dot_general(
         lvg_t, adapter_a_v, (((0,), (1,)), ((), ())), preferred_element_type=F32
@@ -442,7 +454,7 @@
         term,
         input_grad,
         total[:, :cols].T,
-        total[:, 3 * cols :],
+        total[:, 3 * cols : 3 * cols + HD],
         total[:, cols : 2 * cols].T,
         total[:, 2 * cols : 3 * cols],
     )

time: 117 us -> 119 us (1.017)
  the two profiles are of different devices: /device:TPU:16 before, /device:TPU:15 now
where the time goes in v6:
time: 119 us; the launch traced here: 118 us
  starting transfers between devices  47.1 us (40%)
  waiting for transfers between devices  42.4 us (36%)
  Pallas kernels  16.7 us (14%)
  local copies, waits for them, and re-layouts  4.91 us (4%)
  matrix products  2.85 us (2%)
  other arithmetic  2.82 us (2%)
    ppermute x6, starting transfers between devices, shift(): return lax.ppermute(value, 'ctx', [(i, (i + by) % n) for i in range(n)])  22.8 us
    all_to_all x2, waiting for transfers between devices, share_tp(): lax.all_to_all(jnp.broadcast_to(rows[None], (n,) + rows.shape), 'tp', 0, 0)  22.4 us
    all_to_all x2, starting transfers between devices, share_tp(): lax.all_to_all(jnp.broadcast_to(rows[None], (n,) + rows.shape), 'tp', 0, 0)  14.7 us
    ppermute x6, waiting for transfers between devices, flip(): return lax.ppermute(value, 'ctx', [(i, i ^ mask) for i in range(n)])  13.2 us
    pallas_call x1, Pallas kernels, attention(): pl.pallas_call(attn_kernel, in_specs=[pl.BlockSpec(memory_space=pltpu.SME...  11.8 us
    ppermute x6, starting transfers between devices, flip(): return lax.ppermute(value, 'ctx', [(i, i ^ mask) for i in range(n)])  8.21 us
    ppermute x6, waiting for transfers between devices, shift(): return lax.ppermute(value, 'ctx', [(i, (i + by) % n) for i in range(n)])  6.8 us
    unnamed x22, local copies, waits for them, and re-layouts  2.82 us
  transfers between devices with their start and end apart: 15, of which 11 were waited for; matrix products, arithmetic and copies ran while one was open for 4% of the time, Pallas kernels for 2%

profile of v6, /device:TPU:15, one launch (start us, length us, event | category | flops | bytes accessed | tf_op | source)
XLA Modules:
  0.0 117.6 jit_solution(17666150993169457544)
XLA Ops:
  0.6 1.7 %send.1 = (bf16[1024,128]{1,0:T(8,128)(2,1)}, bf16[8,512]{1,0:T(8,128)(2,1)}) custom-call(s32[1]{0:T(128)} %bitcast.first_ref, s32[1,64]{1,0:T(1,128)} %bitcast.21, f32[1,512]{1,0:T(1,128)} %bitcast.24, bf16[512,128]{1,0:T(8,128)(2,1)} %key_hbm.1, bf16[512,128]{1,0:T(8,128)(2,1)} %frozen_hbm.1), custom_call_target="tpu_custom_call" | custom-call | tf_op jit(solution)/shard_map/send/pallas_call | solution.py:119
  2.4 1.8 %collective-permute-start.1 = (bf16[1024,128]{1,0:T(8,128)(2,1)}, bf16[1024,128]{1,0:T(8,128)(2,1)S(1)}, u32[]{:S(2)}, u32[]{:S(2)}) collective-permute-start(bf16[1024,128]{1,0:T(8,128)(2,1)} %get-tuple-element.28.kv_own), channel_id=1, source_target_pairs={{0,8},{8,16},{16,24},{24,32},{32,40},{40,48},{48,56},{56,64},{64,7... | collective-permute-start | bytes 786440 | tf_op jit(solution)/shard_map/ppermute | solution.py:20
  4.2 1.3 %collective-permute-start = (bf16[8,512]{1,0:T(8,128)(2,1)}, bf16[8,512]{1,0:T(8,128)(2,1)S(1)}, u32[]{:S(2)}, u32[]{:S(2)}) collective-permute-start(bf16[8,512]{1,0:T(8,128)(2,1)} %get-tuple-element.27), channel_id=1, source_target_pairs={{0,0},{33,1},{66,2},{99,3},{132,4},{165,5},{198,6},{231,7},{8,8},{... | collective-permute-start | bytes 24584 | tf_op jit(solution)/shard_map/ppermute | solution.py:34
  5.6 2.7 %prep.1 = (bf16[32,512]{1,0:T(8,128)(2,1)S(1)}, s32[8,512]{1,0:T(8,128)S(1)}, s32[3]{0:T(128)S(1)}) custom-call(s32[1]{0:T(128)} %bitcast.first_ref, s32[1,64]{1,0:T(1,128)} %bitcast.22, bf16[16,1024]{1,0:T(8,128)(2,1)} %bitcast.19, bf16[16,1024]{1,0:T(8,128)(2,1)} %up_hbm.1, bf16[512,1024]{1,0:T(8,128)(2,1)} %hidden_ref.1, bf16[512,1024]{1,0:T(8,128)(2,1)} %dout_ref.1), custom_call_target="tpu_custom_call" | custom-call | tf_op jit(solution)/shard_map/prep/pallas_call | solution.py:173
  8.3 0.0 copy-start.4
  8.3 0.0 collective-permute-done
  8.3 0.0 collective-permute-done.1.kv_near
  8.4 0.0 copy-start.5
  8.4 0.7 broadcast_in_dim.31
  9.1 0.0 copy-start.3
  9.1 11.3 %all-to-all-start = ((bf16[8,40,512]{2,1,0:T(8,128)(2,1)}), bf16[8,40,512]{2,1,0:T(8,128)(2,1)}, u32[]{:S(2)}, u32[]{:S(2)}) async-start(bf16[8,40,512]{2,1,0:T(8,128)(2,1)} %broadcast_in_dim.31), calls=%async_computation | async-start | bytes 655360 | tf_op jit(solution)/shard_map/all_to_all | solution.py:39
  20.4 0.0 copy-start.2
  20.4 0.0 copy-done.4
  20.4 0.8 pad_maximum_fusion
  21.3 0.0 copy-done.5
  21.3 2.2 %collective-permute-start.2 = (bf16[2,1024,128]{2,1,0:T(8,128)(2,1)}, bf16[2,1024,128]{2,1,0:T(8,128)(2,1)S(1)}, u32[]{:S(2)}, u32[]{:S(2)}) collective-permute-start(bf16[2,1024,128]{2,1,0:T(8,128)(2,1)} %pad_maximum_fusion), channel_id=1, source_target_pairs={{0,16},{8,24},{16,32},{24,40},{32,48},{40,56},{48,64},{56,72},{64,... | collective-permute-start | bytes 1572872 | tf_op jit(solution)/shard_map/ppermute | solution.py:20
  23.5 10.9 %all-to-all-done = bf16[8,40,512]{2,1,0:T(8,128)(2,1)} async-done(((bf16[8,40,512]{2,1,0:T(8,128)(2,1)}), bf16[8,40,512]{2,1,0:T(8,128)(2,1)}, u32[]{:S(2)}, u32[]{:S(2)}) %all-to-all-start) | async-done | bytes 327712 | tf_op jit(solution)/shard_map/all_to_all | solution.py:39
  34.4 1.0 convert_reduce_fusion
  35.4 2.6 %collective-permute-start.3 = (f32[24,512]{1,0:T(8,128)S(1)}, f32[24,512]{1,0:T(8,128)S(1)}, u32[]{:S(2)}, u32[]{:S(2)}) collective-permute-start(f32[24,512]{1,0:T(8,128)S(1)} %slice.53.own_hbm), channel_id=1, source_target_pairs={{0,8},{8,16},{16,24},{24,32},{32,40},{40,48},{48,56},{56,64},{64,7... | collective-permute-start | bytes 147464 | tf_op jit(solution)/shard_map/ppermute | solution.py:20
  38.0 1.2 %collective-permute-done.3.near_hbm = f32[24,512]{1,0:T(8,128)S(1)} collective-permute-done((f32[24,512]{1,0:T(8,128)S(1)}, f32[24,512]{1,0:T(8,128)S(1)}, u32[]{:S(2)}, u32[]{:S(2)}) %collective-permute-start.3) | collective-permute-done | bytes 49184 | tf_op jit(solution)/shard_map/ppermute | solution.py:20
  39.2 1.2 %collective-permute-start.4 = (f32[24,1024]{1,0:T(8,128)S(1)}, f32[24,1024]{1,0:T(8,128)S(1)}, u32[]{:S(2)}, u32[]{:S(2)}) collective-permute-start(f32[24,1024]{1,0:T(8,128)S(1)} %pad_maximum_fusion.1), channel_id=1, source_target_pairs={{0,16},{8,24},{16,32},{24,40},{32,48},{40,56},{48,64},{56,72},{64,... | collective-permute-start | bytes 294920 | tf_op jit(solution)/shard_map/ppermute | solution.py:20
  40.4 0.0 collective-permute-done.2.kv_far
  40.4 0.0 copy-start.7
  40.4 0.8 copy-done.7
  41.2 2.0 %collective-permute-done.4.far_hbm = f32[24,1024]{1,0:T(8,128)S(1)} collective-permute-done((f32[24,1024]{1,0:T(8,128)S(1)}, f32[24,1024]{1,0:T(8,128)S(1)}, u32[]{:S(2)}, u32[]{:S(2)}) %collective-permute-start.4) | collective-permute-done | bytes 98336 | tf_op jit(solution)/shard_map/ppermute | solution.py:20
  43.2 0.0 copy-done.3
  43.2 0.0 copy-done.2
  43.2 0.0 copy-start.6
  43.2 0.9 copy-done.6
  44.2 0.0 copy-start.8
  44.2 1.0 copy-done.8
  45.2 11.8 %attn.1 = (bf16[512,1024]{1,0:T(8,128)(2,1)}, f32[16,512]{1,0:T(8,128)S(1)}, bf16[16,2048]{1,0:T(8,128)(2,1)S(1)}, bf16[16,128]{1,0:T(8,128)(2,1)S(1)}, bf16[16,...) custom-call(s32[3]{0:T(128)S(1)} %get-tuple-element.24.low_ref, bf16[512,1024]{1,0:T(8,128)(2,1)S(1)} %copy-done.2, ...), custom_call_target="tpu_custom_call" | custom-call | tf_op jit(solution)/shard_map/attn/pallas_call | solution.py:331
  57.0 0.0 copy-start
  57.1 2.2 %collective-permute-start.5 = (bf16[16,1024]{1,0:T(8,128)(2,1)S(1)}, bf16[16,1024]{1,0:T(8,128)(2,1)S(1)}, u32[]{:S(2)}, u32[]{:S(2)}) collective-permute-start(bf16[16,1024]{1,0:T(8,128)(2,1)S(1)} %slice.44), channel_id=1, source_target_pairs={{0,240},{8,248},{16,0},{24,8},{32,16},{40,24},{48,32},{56,40},{64,... | collective-permute-start | bytes 98312 | tf_op jit(solution)/shard_map/ppermute | solution.py:20
  59.2 2.8 %collective-permute-done.5 = bf16[16,1024]{1,0:T(8,128)(2,1)S(1)} collective-permute-done((bf16[16,1024]{1,0:T(8,128)(2,1)S(1)}, bf16[16,1024]{1,0:T(8,128)(2,1)S(1)}, u32[]{:S(2)}, u32[]{:S(2)}) %collective-permute-start.5) | collective-permute-done | bytes 32800 | tf_op jit(solution)/shard_map/ppermute | solution.py:20
  62.0 12.8 %collective-permute-start.6 = (bf16[16,512]{1,0:T(8,128)(2,1)S(1)}, bf16[16,512]{1,0:T(8,128)(2,1)S(1)}, u32[]{:S(2)}, u32[]{:S(2)}) collective-permute-start(bf16[16,512]{1,0:T(8,128)(2,1)S(1)} %fusion.3), channel_id=1, source_target_pairs={{0,248},{8,0},{16,8},{24,16},{32,24},{40,32},{48,40},{56,48},{64,5... | collective-permute-start | bytes 49160 | tf_op jit(solution)/shard_map/ppermute | solution.py:20
  74.8 0.8 collective-permute-done.6
  75.7 0.7 broadcast_in_dim.33
  76.4 3.4 %all-to-all-start.1 = ((bf16[8,32,512]{2,1,0:T(8,128)(2,1)}), bf16[8,32,512]{2,1,0:T(8,128)(2,1)S(1)}, u32[]{:S(2)}, u32[]{:S(2)}) async-start(bf16[8,32,512]{2,1,0:T(8,128)(2,1)} %broadcast_in_dim.33), calls=%async_computation.1 | async-start | bytes 524288 | tf_op jit(solution)/shard_map/all_to_all | solution.py:39
  79.8 11.5 %all-to-all-done.1.shared_ref = bf16[8,32,512]{2,1,0:T(8,128)(2,1)S(1)} async-done(((bf16[8,32,512]{2,1,0:T(8,128)(2,1)}), bf16[8,32,512]{2,1,0:T(8,128)(2,1)S(1)}, u32[]{:S(2)}, u32[]{:S(2)}) %all-to-all-start.1) | async-done | bytes 262176 | tf_op jit(solution)/shard_map/all_to_all | solution.py:39
  91.4 0.0 copy-done.1
  91.4 0.0 copy-done
  91.4 0.4 grads.1
  91.8 1.4 %collective-permute-start.7 = (bf16[16,1664]{1,0:T(8,128)(2,1)S(1)}, bf16[16,1664]{1,0:T(8,128)(2,1)S(1)}, u32[]{:S(2)}, u32[]{:S(2)}) collective-permute-start(bf16[16,1664]{1,0:T(8,128)(2,1)S(1)} %get-tuple-element.40), channel_id=1, source_target_pairs={{0,8},{8,0},{16,24},{24,16},{32,40},{40,32},{48,56},{56,48},{64,72... | collective-permute-start | bytes 159752 | tf_op jit(solution)/shard_map/ppermute | solution.py:25
  93.2 0.9 collective-permute-done.7
  94.1 0.1 collective-permute-start.8
  94.2 3.0 %collective-permute-done.8 = bf16[16,1664]{1,0:T(8,128)(2,1)S(1)} collective-permute-done((bf16[16,1664]{1,0:T(8,128)(2,1)S(1)}, bf16[16,1664]{1,0:T(8,128)(2,1)S(1)}, u32[]{:S(2)}, u32[]{:S(2)}) %collective-permute-start.8) | collective-permute-done | bytes 53280 | tf_op jit(solution)/shard_map/ppermute | solution.py:25
  97.2 0.0 copy-start.10
  97.2 0.1 collective-permute-start.9
  97.3 4.5 %collective-permute-done.9 = bf16[16,1664]{1,0:T(8,128)(2,1)S(1)} collective-permute-done((bf16[16,1664]{1,0:T(8,128)(2,1)S(1)}, bf16[16,1664]{1,0:T(8,128)(2,1)S(1)}, u32[]{:S(2)}, u32[]{:S(2)}) %collective-permute-start.9) | collective-permute-done | bytes 53280 | tf_op jit(solution)/shard_map/ppermute | solution.py:25
  101.8 0.1 collective-permute-start.10
  101.9 3.0 %collective-permute-done.10 = bf16[16,1664]{1,0:T(8,128)(2,1)S(1)} collective-permute-done((bf16[16,1664]{1,0:T(8,128)(2,1)S(1)}, bf16[16,1664]{1,0:T(8,128)(2,1)S(1)}, u32[]{:S(2)}, u32[]{:S(2)}) %collective-permute-start.10) | collective-permute-done | bytes 53280 | tf_op jit(solution)/shard_map/ppermute | solution.py:25
  104.9 0.1 fusion.7
  105.0 1.2 %collective-permute-start.11 = (bf16[16,1664]{1,0:T(8,128)(2,1)S(1)}, bf16[16,1664]{1,0:T(8,128)(2,1)S(1)}, u32[]{:S(2)}, u32[]{:S(2)}) collective-permute-start(bf16[16,1664]{1,0:T(8,128)(2,1)S(1)} %fusion.7), channel_id=1, source_target_pairs={{0,128},{8,136},{16,144},{24,152},{32,160},{40,168},{48,176},{56,1... | collective-permute-start | bytes 159752 | tf_op jit(solution)/shard_map/ppermute | solution.py:25
  106.2 0.0 copy-done.9
  106.2 1.4 %multiply_convert_fusion = bf16[512,1024]{1,0:T(8,128)(2,1)} fusion(bf16[16,512]{1,0:T(8,128)(2,1)S(1)} %get-tuple-element.37, bf16[16,1024]{1,0:T(8,128)(2,1)S(1)} %copy-done.9), kind=kOutput, calls=%fused_computation | convolution fusion | flops 17825792 | bytes 1097728 | tf_op jit(solution)/shard_map/dot_general | solution.py:51
  107.6 1.9 %collective-permute-done.11 = bf16[16,1664]{1,0:T(8,128)(2,1)S(1)} collective-permute-done((bf16[16,1664]{1,0:T(8,128)(2,1)S(1)}, bf16[16,1664]{1,0:T(8,128)(2,1)S(1)}, u32[]{:S(2)}, u32[]{:S(2)}) %collective-permute-start.11) | collective-permute-done | bytes 53280 | tf_op jit(solution)/shard_map/ppermute | solution.py:25
  109.5 0.1 fusion.9
  109.6 5.3 %collective-permute-start.12 = (bf16[16,1664]{1,0:T(8,128)(2,1)S(1)}, bf16[16,1664]{1,0:T(8,128)(2,1)S(1)}, u32[]{:S(2)}, u32[]{:S(2)}) collective-permute-start(bf16[16,1664]{1,0:T(8,128)(2,1)S(1)} %get-tuple-element.41), channel_id=1, source_target_pairs={{0,8},{8,0},{16,24},{24,16},{32,40},{40,32},{48,56},{56,48},{64,72... | collective-permute-start | bytes 159752 | tf_op jit(solution)/shard_map/ppermute | solution.py:25
  114.9 0.0 copy-done.10
  114.9 1.4 %convolution_convert_fusion = bf16[512,1024]{1,0:T(8,128)(2,1)} fusion(bf16[16,512]{1,0:T(8,128)(2,1)S(1)} %get-tuple-element.38, bf16[1024,16]{0,1:T(8,128)(2,1)S(1)} %copy-done.10), kind=kOutput, calls=%fused_computation.1 | convolution fusion | flops 17301504 | bytes 1097728 | tf_op jit(solution)/shard_map/dot_general | solution.py:449
  116.3 0.0 collective-permute-done.12
  116.4 0.6 slice.57
  117.0 0.7 fusion.10
  (17 shorter events, 0.2 us)
Async XLA Ops:
  2.4 6.0 %collective-permute-start.1 = (bf16[1024,128]{1,0:T(8,128)(2,1)}, bf16[1024,128]{1,0:T(8,128)(2,1)S(1)}, u32[]{:S(2)}, u32[]{:S(2)}) collective-permute-start(bf16[1024,128]{1,0:T(8,128)(2,1)} %get-tuple-element.28.kv_own), channel_id=1, source_target_pairs={{0,8},{8,16},{16,24},{24,32},{32,40},{40,48},{48,56},{56,64},{64,7... | collective-permute-start | bytes 786440 | tf_op jit(solution)/shard_map/ppermute | solution.py:20
  4.2 4.1 %collective-permute-start = (bf16[8,512]{1,0:T(8,128)(2,1)}, bf16[8,512]{1,0:T(8,128)(2,1)S(1)}, u32[]{:S(2)}, u32[]{:S(2)}) collective-permute-start(bf16[8,512]{1,0:T(8,128)(2,1)} %get-tuple-element.27), channel_id=1, source_target_pairs={{0,0},{33,1},{66,2},{99,3},{132,4},{165,5},{198,6},{231,7},{8,8},{... | collective-permute-start | bytes 24584 | tf_op jit(solution)/shard_map/ppermute | solution.py:34
  8.3 12.1 %copy-start.4 = (bf16[1024,128]{1,0:T(8,128)(2,1)S(1)}, bf16[1024,128]{1,0:T(8,128)(2,1)}, u32[]{:S(2)}) copy-start(bf16[1024,128]{1,0:T(8,128)(2,1)} %get-tuple-element.28.kv_own) | copy-start | bytes 786436
  8.4 12.9 %copy-start.5 = (bf16[1024,128]{1,0:T(8,128)(2,1)}, bf16[1024,128]{1,0:T(8,128)(2,1)S(1)}, u32[]{:S(2)}) copy-start(bf16[1024,128]{1,0:T(8,128)(2,1)S(1)} %collective-permute-done.1.kv_near) | copy-start | bytes 786436
  9.1 34.1 %copy-start.3 = (bf16[512,1024]{1,0:T(8,128)(2,1)S(1)}, bf16[512,1024]{1,0:T(8,128)(2,1)}, u32[]{:S(2)}) copy-start(bf16[512,1024]{1,0:T(8,128)(2,1)} %g_ref.1) | copy-start | bytes 3145732
  9.1 25.2 %all-to-all-start = ((bf16[8,40,512]{2,1,0:T(8,128)(2,1)}), bf16[8,40,512]{2,1,0:T(8,128)(2,1)}, u32[]{:S(2)}, u32[]{:S(2)}) async-start(bf16[8,40,512]{2,1,0:T(8,128)(2,1)} %broadcast_in_dim.31), calls=%async_computation | async-start | bytes 655360 | tf_op jit(solution)/shard_map/all_to_all | solution.py:39
  20.4 22.8 %copy-start.2 = (bf16[512,1024]{1,0:T(8,128)(2,1)S(1)}, bf16[512,1024]{1,0:T(8,128)(2,1)}, u32[]{:S(2)}) copy-start(bf16[512,1024]{1,0:T(8,128)(2,1)} %q_ref.1) | copy-start | bytes 3145732
  21.3 19.1 %collective-permute-start.2 = (bf16[2,1024,128]{2,1,0:T(8,128)(2,1)}, bf16[2,1024,128]{2,1,0:T(8,128)(2,1)S(1)}, u32[]{:S(2)}, u32[]{:S(2)}) collective-permute-start(bf16[2,1024,128]{2,1,0:T(8,128)(2,1)} %pad_maximum_fusion), channel_id=1, source_target_pairs={{0,16},{8,24},{16,32},{24,40},{32,48},{40,56},{48,64},{56,72},{64,... | collective-permute-start | bytes 1572872 | tf_op jit(solution)/shard_map/ppermute | solution.py:20
  35.4 3.7 %collective-permute-start.3 = (f32[24,512]{1,0:T(8,128)S(1)}, f32[24,512]{1,0:T(8,128)S(1)}, u32[]{:S(2)}, u32[]{:S(2)}) collective-permute-start(f32[24,512]{1,0:T(8,128)S(1)} %slice.53.own_hbm), channel_id=1, source_target_pairs={{0,8},{8,16},{16,24},{24,32},{32,40},{40,48},{48,56},{56,64},{64,7... | collective-permute-start | bytes 147464 | tf_op jit(solution)/shard_map/ppermute | solution.py:20
  39.2 4.0 %collective-permute-start.4 = (f32[24,1024]{1,0:T(8,128)S(1)}, f32[24,1024]{1,0:T(8,128)S(1)}, u32[]{:S(2)}, u32[]{:S(2)}) collective-permute-start(f32[24,1024]{1,0:T(8,128)S(1)} %pad_maximum_fusion.1), channel_id=1, source_target_pairs={{0,16},{8,24},{16,32},{24,40},{32,48},{40,56},{48,64},{56,72},{64,... | collective-permute-start | bytes 294920 | tf_op jit(solution)/shard_map/ppermute | solution.py:20
  40.4 0.8 copy-start.7
  43.2 1.0 copy-start.6
  44.2 1.0 copy-start.8
  45.2 46.2 %copy-start.1 = (bf16[512,1024]{1,0:T(8,128)(2,1)S(1)}, bf16[512,1024]{1,0:T(8,128)(2,1)}, u32[]{:S(2)}) copy-start(bf16[512,1024]{1,0:T(8,128)(2,1)} %dout_ref.1) | copy-start | bytes 3145732
  57.0 34.4 %copy-start = (bf16[512,1024]{1,0:T(8,128)(2,1)S(1)}, bf16[512,1024]{1,0:T(8,128)(2,1)}, u32[]{:S(2)}) copy-start(bf16[512,1024]{1,0:T(8,128)(2,1)} %hidden_ref.1) | copy-start | bytes 3145732
  57.1 5.0 %collective-permute-start.5 = (bf16[16,1024]{1,0:T(8,128)(2,1)S(1)}, bf16[16,1024]{1,0:T(8,128)(2,1)S(1)}, u32[]{:S(2)}, u32[]{:S(2)}) collective-permute-start(bf16[16,1024]{1,0:T(8,128)(2,1)S(1)} %slice.44), channel_id=1, source_target_pairs={{0,240},{8,248},{16,0},{24,8},{32,16},{40,24},{48,32},{56,40},{64,... | collective-permute-start | bytes 98312 | tf_op jit(solution)/shard_map/ppermute | solution.py:20
  62.0 13.6 %collective-permute-start.6 = (bf16[16,512]{1,0:T(8,128)(2,1)S(1)}, bf16[16,512]{1,0:T(8,128)(2,1)S(1)}, u32[]{:S(2)}, u32[]{:S(2)}) collective-permute-start(bf16[16,512]{1,0:T(8,128)(2,1)S(1)} %fusion.3), channel_id=1, source_target_pairs={{0,248},{8,0},{16,8},{24,16},{32,24},{40,32},{48,40},{56,48},{64,5... | collective-permute-start | bytes 49160 | tf_op jit(solution)/shard_map/ppermute | solution.py:20
  76.4 15.0 %all-to-all-start.1 = ((bf16[8,32,512]{2,1,0:T(8,128)(2,1)}), bf16[8,32,512]{2,1,0:T(8,128)(2,1)S(1)}, u32[]{:S(2)}, u32[]{:S(2)}) async-start(bf16[8,32,512]{2,1,0:T(8,128)(2,1)} %broadcast_in_dim.33), calls=%async_computation.1 | async-start | bytes 524288 | tf_op jit(solution)/shard_map/all_to_all | solution.py:39
  91.4 14.8 %copy-start.9 = (bf16[16,1024]{1,0:T(8,128)(2,1)S(1)}, bf16[16,1024]{1,0:T(8,128)(2,1)}, u32[]{:S(2)}) copy-start(bf16[16,1024]{1,0:T(8,128)(2,1)} %up_hbm.1) | copy-start | bytes 98308
  91.8 2.3 %collective-permute-start.7 = (bf16[16,1664]{1,0:T(8,128)(2,1)S(1)}, bf16[16,1664]{1,0:T(8,128)(2,1)S(1)}, u32[]{:S(2)}, u32[]{:S(2)}) collective-permute-start(bf16[16,1664]{1,0:T(8,128)(2,1)S(1)} %get-tuple-element.40), channel_id=1, source_target_pairs={{0,8},{8,0},{16,24},{24,16},{32,40},{40,32},{48,56},{56,48},{64,72... | collective-permute-start | bytes 159752 | tf_op jit(solution)/shard_map/ppermute | solution.py:25
  94.1 3.1 %collective-permute-start.8 = (bf16[16,1664]{1,0:T(8,128)(2,1)S(1)}, bf16[16,1664]{1,0:T(8,128)(2,1)S(1)}, u32[]{:S(2)}, u32[]{:S(2)}) collective-permute-start(bf16[16,1664]{1,0:T(8,128)(2,1)S(1)} %fusion), channel_id=1, source_target_pairs={{0,16},{8,24},{16,0},{24,8},{32,48},{40,56},{48,32},{56,40},{64,80... | collective-permute-start | bytes 159752 | tf_op jit(solution)/shard_map/ppermute | solution.py:25
  97.2 17.7 %copy-start.10 = (bf16[1024,16]{0,1:T(8,128)(2,1)S(1)}, bf16[1024,16]{0,1:T(8,128)(2,1)}, u32[]{:S(2)}) copy-start(bf16[1024,16]{0,1:T(8,128)(2,1)} %param.17) | copy-start | bytes 98308
  97.2 4.6 %collective-permute-start.9 = (bf16[16,1664]{1,0:T(8,128)(2,1)S(1)}, bf16[16,1664]{1,0:T(8,128)(2,1)S(1)}, u32[]{:S(2)}, u32[]{:S(2)}) collective-permute-start(bf16[16,1664]{1,0:T(8,128)(2,1)S(1)} %fusion.8), channel_id=1, source_target_pairs={{0,32},{8,40},{16,48},{24,56},{32,0},{40,8},{48,16},{56,24},{64,96... | collective-permute-start | bytes 159752 | tf_op jit(solution)/shard_map/ppermute | solution.py:25
  101.8 3.1 %collective-permute-start.10 = (bf16[16,1664]{1,0:T(8,128)(2,1)S(1)}, bf16[16,1664]{1,0:T(8,128)(2,1)S(1)}, u32[]{:S(2)}, u32[]{:S(2)}) collective-permute-start(bf16[16,1664]{1,0:T(8,128)(2,1)S(1)} %fusion.1), channel_id=1, source_target_pairs={{0,64},{8,72},{16,80},{24,88},{32,96},{40,104},{48,112},{56,120},{... | collective-permute-start | bytes 159752 | tf_op jit(solution)/shard_map/ppermute | solution.py:25
  105.0 4.6 %collective-permute-start.11 = (bf16[16,1664]{1,0:T(8,128)(2,1)S(1)}, bf16[16,1664]{1,0:T(8,128)(2,1)S(1)}, u32[]{:S(2)}, u32[]{:S(2)}) collective-permute-start(bf16[16,1664]{1,0:T(8,128)(2,1)S(1)} %fusion.7), channel_id=1, source_target_pairs={{0,128},{8,136},{16,144},{24,152},{32,160},{40,168},{48,176},{56,1... | collective-permute-start | bytes 159752 | tf_op jit(solution)/shard_map/ppermute | solution.py:25
  109.6 6.7 %collective-permute-start.12 = (bf16[16,1664]{1,0:T(8,128)(2,1)S(1)}, bf16[16,1664]{1,0:T(8,128)(2,1)S(1)}, u32[]{:S(2)}, u32[]{:S(2)}) collective-permute-start(bf16[16,1664]{1,0:T(8,128)(2,1)S(1)} %get-tuple-element.41), channel_id=1, source_target_pairs={{0,8},{8,0},{16,24},{24,16},{32,40},{40,32},{48,56},{56,48},{64,72... | collective-permute-start | bytes 159752 | tf_op jit(solution)/shard_map/ppermute | solution.py:25
